TPU v7x, 512 devices: a whole 4x4x16 slice. The times are simulated.
512 devices in a mesh: seq: 64 (over z, y), head: 8 (over x, core).
Axes of the slice: x: 4, y: 4, z: 16, core: 2. Of those that a mesh axis runs over, the one named last changes fastest.
Arguments:
- queries: bfloat16 [131072, 2048], P(('seq', 'head')), may hold values from -12 to 12
- key_vectors: bfloat16 [131072, 2048], P(('seq', 'head')), may hold values from -6 to 6
- value_vectors: bfloat16 [131072, 2048], P(('seq', 'head')), may hold values from -6 to 6
- key_blocks: int32 [1024, 14], P('seq'), may hold values from -1 to 1023, as said below
Outputs:
- context: bfloat16 [131072, 2048], P(('seq', 'head'))
Inputs may be any that keep to these rules, and one draw needn't show every extreme that they name: `key_blocks`: row b lists key blocks of query block b. Slots 0 to 9, in falling order: b itself, then 10 - 1 distinct blocks among b - 15 to b - 1, written as -1 where the block number would be negative. Slot 10 + i holds the i-th global block where that block is at most b - 16, else -1. The 4 global blocks are the same for all rows, distinct and rising, the first is 0, and all lie below 1008.
All inputs are finite; a program needn't handle non-finite values.
Results may differ from a plain program's by a relative error of at most 0.0032.
Values may be sent and summed in bfloat16 or wider, within the bound.
No kernel may reach another device: no remote copies, remote signals or barrier semaphores. Data moves between devices by JAX's collectives and lax.ppermute only.
A program may use at most 64 MiB of HBM per device.

v0:
```python
import math

import jax
import jax.numpy as jnp
from jax import lax
from jax.sharding import PartitionSpec as P

HEAD_DIM = 128
BLOCK = 128
WIN = 16
WSEL = 10


def passed_along(value, axis, steps):
    count = lax.axis_size(axis)
    initial, last = (max(0, -steps), min(count, count - steps))
    return lax.ppermute(value, axis, [(source, source + steps) for source in range(initial, last)])


def attend_block(query_block, key_rows, value_rows, block_ids, block_pos, causal):
    slot_count = block_ids.shape[0]
    head_count = query_block.shape[1] // HEAD_DIM
    query_heads = query_block.reshape(BLOCK, head_count, HEAD_DIM)
    key_heads = key_rows.reshape(slot_count, BLOCK, head_count, HEAD_DIM)
    value_heads = value_rows.reshape(slot_count, BLOCK, head_count, HEAD_DIM)
    scores = jnp.einsum(
        "thd,juhd->htju", query_heads, key_heads, preferred_element_type=jnp.float32
    ) * (1.0 / math.sqrt(HEAD_DIM))
    allowed = (block_ids >= 0)[None, :, None] & (
        (block_ids < block_pos)[None, :, None] | causal[:, None, :]
    )
    scores = jnp.where(allowed[None], scores, -1e30)
    row_max = jnp.max(scores, axis=(2, 3), keepdims=True)
    weight = jnp.where(allowed[None], jnp.exp(scores - row_max), 0.0)
    denom_sum = jnp.sum(weight, axis=(2, 3))
    mixed_sum = jnp.einsum(
        "htju,juhd->thd",
        weight.astype(jnp.bfloat16),
        value_heads,
        preferred_element_type=jnp.float32,
    )
    return (
        (mixed_sum / jnp.transpose(denom_sum)[:, :, None])
        .astype(jnp.bfloat16)
        .reshape(BLOCK, head_count * HEAD_DIM)
    )


def shards(queries, key_vectors, value_vectors, key_blocks):
    local_query, local_key, local_value = (
        lax.all_to_all(queries, "head", split_axis=1, concat_axis=0, tiled=True),
        lax.all_to_all(key_vectors, "head", split_axis=1, concat_axis=0, tiled=True),
        lax.all_to_all(value_vectors, "head", split_axis=1, concat_axis=0, tiled=True),
    )
    token_rows, head_width = local_query.shape
    block_count = token_rows // BLOCK
    first_block = lax.axis_index("seq") * block_count
    own_tiles = jnp.stack((local_key, local_value), 0).reshape(2, block_count, BLOCK, head_width)
    span_back = WIN - 1
    shard_reach = (span_back + block_count - 1) // block_count
    keep_count = span_back - (shard_reach - 1) * block_count
    pieces = passed_along(own_tiles[:, block_count - keep_count :], "seq", 1)
    extended = jnp.concatenate((pieces, own_tiles), 1)
    global_ids = lax.pmax(jnp.max(key_blocks[:, WSEL:], axis=0), "seq")
    global_count = global_ids.shape[0]
    offset_local = global_ids - first_block
    present = (offset_local >= 0) & (offset_local < block_count)
    picked = jnp.take(own_tiles, jnp.clip(offset_local, 0, block_count - 1), axis=1)
    masked_term = jnp.where(present[None, :, None, None], picked.astype(jnp.float32), 0.0)
    shared = lax.psum(masked_term, "seq").astype(jnp.bfloat16)
    causal = lax.broadcasted_iota(jnp.int32, (BLOCK, BLOCK), 0) >= lax.broadcasted_iota(
        jnp.int32, (BLOCK, BLOCK), 1
    )
    query_tiles = local_query.reshape(block_count, BLOCK, head_width)
    positions = first_block + jnp.arange(block_count, dtype=jnp.int32)
    source = jnp.concatenate((shared, extended), 1)
    slot_index = jnp.arange(key_blocks.shape[1], dtype=jnp.int32)

    def one_block(block_item):
        query_block, block_ids, block_pos = block_item
        source_place = jnp.where(
            slot_index < WSEL, global_count + span_back + block_ids - first_block, slot_index - WSEL
        )
        source_place = jnp.where(block_ids >= 0, source_place, 0)
        selected = jnp.take(source, source_place, axis=1)
        return attend_block(query_block, selected[0], selected[1], block_ids, block_pos, causal)

    context = lax.map(one_block, (query_tiles, key_blocks, positions))
    return lax.all_to_all(
        context.reshape(token_rows, head_width), "head", split_axis=0, concat_axis=1, tiled=True
    )


def solution(mesh):
    placed = (
        P(("seq", "head"), None),
        P(("seq", "head"), None),
        P(("seq", "head"), None),
        P("seq", None),
    )
    return jax.shard_map(
        shards, mesh=mesh, in_specs=placed, out_specs=P(("seq", "head"), None), check_vma=False
    )
```

profile of v0, /device:TPU:1, one launch (start us, length us, event | category | flops | bytes accessed | tf_op | source)
XLA Modules:
  0.0 597.3 jit_solution(16125236216598636198)
XLA Ops:
  0.0 2.4 copy.59
  2.4 10.3 %all-to-all-start = ((bf16[256,8,256]{2,0,1:T(8,128)(2,1)}), bf16[256,8,256]{2,0,1:T(8,128)(2,1)S(1)}, u32[]{:S(2)}, u32[]{:S(2)}) async-start(bf16[256,8,256]{2,0,1:T(8,128)(2,1)} %bitcast.78), calls=%async_computation | async-start | bytes 2097152 | tf_op jit(solution)/shard_map/all_to_all | solution.py:52
  12.8 15.0 %all-to-all-done = bf16[256,8,256]{2,0,1:T(8,128)(2,1)S(1)} async-done(((bf16[256,8,256]{2,0,1:T(8,128)(2,1)}), bf16[256,8,256]{2,0,1:T(8,128)(2,1)S(1)}, u32[]{:S(2)}, u32[]{:S(2)}) %all-to-all-start) | async-done | bytes 1048608 | tf_op jit(solution)/shard_map/all_to_all | solution.py:52
  27.8 18.3 %all_to_all.67 = bf16[256,8,256]{2,0,1:T(8,128)(2,1)S(1)} all-to-all(bf16[256,8,256]{2,0,1:T(8,128)(2,1)S(1)} %bitcast.137), channel_id=1, replica_groups=mesh['seq'=64,'head'=8] {'head'}, dimensions={1} | all-to-all | bytes 2097152 | tf_op jit(solution)/shard_map/all_to_all | solution.py:53
  46.2 1.4 fusion.13
  47.6 2.7 collective-permute-start
  50.3 1.3 copy.38
  51.6 4.5 all-to-all-start.2
  56.2 56.6 %pmax.7 = s32[4]{0:T(128)S(1)} all-reduce(s32[4]{0:T(128)S(1)} %slice_reduce_fusion), channel_id=1, replica_groups=mesh['seq'=64,'head'=8] {'seq'}, use_global_device_ids=true, to_apply=%region_1.0 | all-reduce | flops 4 | bytes 32 | tf_op jit(solution)/shard_map/pmax | solution.py:64
  112.9 1.5 pad_maximum_fusion
  114.4 3.0 gather_fusion.1
  117.4 2.2 select_bitcast_fusion.1
  119.6 1.3 copy.39
  120.9 231.2 %all-reduce.1 = bf16[2,4,128,256]{3,2,0,1:T(8,128)(2,1)S(1)} all-reduce(f32[2,4,128,256]{3,2,0,1:T(8,128)} %select_bitcast_fusion.1), channel_id=1, replica_groups=mesh['seq'=64,'head'=8] {'seq'}, use_global_device_ids=true, to_apply=%region_2.3 | all-reduce | flops 262144 | bytes 1572864 | tf_op jit(solution)/shard_map/psum | solution.py:70
  352.1 3.5 maximum_maximum_fusion
  355.6 160.5 %while.14 = (s32[]{:T(128)}, bf16[16,128,256]{2,1,0:T(8,128)(2,1)}, s32[16,14]{1,0:T(8,128)S(1)}, s32[]{:T(128)}, bf16[2,35,128,256]{3,2,1,0:T(8,128)(2,1)}, /*i...) while((s32[]{:T(128)}, bf16[16,128,256]{2,1,0:T(8,128)(2,1)}, ...), condition=%wide.region_6.7_spmd.clone.clone, body=%wide.region_3.6_spmd.clone.clone.sunk | while | flops 240468832 | bytes 27075720 | solution.py:88
  356.8 3.0 gather_fusion
  361.4 0.9 constant_dynamic-slice_fusion.4
  366.8 3.0 gather_fusion
  371.4 0.9 constant_dynamic-slice_fusion.4
  376.8 3.0 gather_fusion
  381.5 0.9 constant_dynamic-slice_fusion.4
  386.9 3.0 gather_fusion
  391.5 0.9 constant_dynamic-slice_fusion.4
  396.9 3.0 gather_fusion
  401.5 0.9 constant_dynamic-slice_fusion.4
  406.9 3.0 gather_fusion
  411.5 0.9 constant_dynamic-slice_fusion.4
  416.9 3.0 gather_fusion
  421.6 0.9 constant_dynamic-slice_fusion.4
  427.0 3.0 gather_fusion
  431.6 0.9 constant_dynamic-slice_fusion.4
  437.0 3.0 gather_fusion
  441.6 0.9 constant_dynamic-slice_fusion.4
  447.0 3.0 gather_fusion
  451.7 0.9 constant_dynamic-slice_fusion.4
  457.1 3.0 gather_fusion
  461.7 0.9 constant_dynamic-slice_fusion.4
  467.1 3.0 gather_fusion
  477.1 3.0 gather_fusion
  481.8 0.9 constant_dynamic-slice_fusion.4
  487.1 3.0 gather_fusion
  491.8 0.9 constant_dynamic-slice_fusion.4
  497.2 3.0 gather_fusion
  507.2 3.0 gather_fusion
  511.8 0.9 constant_dynamic-slice_fusion.4
  516.1 79.3 %all_to_all.68 = bf16[8,256,256]{2,1,0:T(8,128)(2,1)S(1)} all-to-all(bf16[8,256,256]{2,1,0:T(8,128)(2,1)} %bitcast.144), channel_id=1, replica_groups=mesh['seq'=64,'head'=8] {'head'}, dimensions={0} | all-to-all | bytes 2097152 | tf_op jit(solution)/shard_map/all_to_all | solution.py:89
  595.9 1.4 copy.43
  (337 shorter events, 99.9 us)
Async XLA Ops:
  0.0 12.7 %copy-start = (bf16[256,2048]{1,0:T(8,128)(2,1)S(1)}, bf16[256,2048]{1,0:T(8,128)(2,1)}, u32[]{:S(2)}) copy-start(bf16[256,2048]{1,0:T(8,128)(2,1)} %param.8) | copy-start | bytes 3145732
  2.4 25.5 %all-to-all-start = ((bf16[256,8,256]{2,0,1:T(8,128)(2,1)}), bf16[256,8,256]{2,0,1:T(8,128)(2,1)S(1)}, u32[]{:S(2)}, u32[]{:S(2)}) async-start(bf16[256,8,256]{2,0,1:T(8,128)(2,1)} %bitcast.78), calls=%async_computation | async-start | bytes 2097152 | tf_op jit(solution)/shard_map/all_to_all | solution.py:52
  46.1 4.2 copy-start.1
  47.6 8.5 %copy-start.2 = (s32[16,14]{1,0:T(8,128)S(1)}, s32[16,14]{1,0:T(8,128)}, u32[]{:S(2)}) copy-start(s32[16,14]{1,0:T(8,128)} %param.9) | copy-start | bytes 2692
  47.6 304.5 %collective-permute-start = (bf16[2,15,128,256]{3,2,1,0:T(8,128)(2,1)}, bf16[2,15,128,256]{3,2,1,0:T(8,128)(2,1)}, u32[]{:S(2)}, u32[]{:S(2)}) collective-permute-start(bf16[2,15,128,256]{3,2,1,0:T(8,128)(2,1)} %fusion.13), channel_id=1, source_target_pairs={{0,8},{8,16},{16,24},{24,32},{32,40},{40,48},{48,56},{56,64},{64,7... | collective-permute-start | bytes 5898248 | tf_op jit(solution)/shard_map/ppermute | solution.py:17
  51.6 68.0 %all-to-all-start.2 = ((bf16[256,8,256]{0,2,1:T(8,128)(2,1)}), bf16[256,8,256]{0,2,1:T(8,128)(2,1)S(1)}, u32[]{:S(2)}, u32[]{:S(2)}) async-start(bf16[256,8,256]{0,2,1:T(8,128)(2,1)} %bitcast.136), calls=%async_computation.2 | async-start | bytes 2097152 | tf_op jit(solution)/shard_map/all_to_all | solution.py:51
where the time goes:
time: 599 us; the launch traced here: 597 us
  blocking collectives  385 us (64%)
  local copies, waits for them, and re-layouts  126 us (21%)
  other arithmetic  39 us (7%)
  starting transfers between devices  17.6 us (3%)
  waiting for transfers between devices  15 us (3%)
  matrix products  12.4 us (2%)
    psum x1, blocking collectives, shards(): shared = lax.psum(masked_term, 'seq').astype(jnp.bfloat16)  231 us
    all_to_all x1, blocking collectives, shards(): lax.all_to_all(context.reshape(token_rows, head_width), 'head', split_axi...  79.3 us
    pmax x1, blocking collectives, shards(): global_ids = lax.pmax(jnp.max(key_blocks[:, WSEL:], axis=0), 'seq')  56.6 us
    gather x16, local copies, waits for them, and re-layouts, one_block(): selected = jnp.take(source, source_place, axis=1)  47.4 us
    dynamic_slice x48, local copies, waits for them, and re-layouts, shards(): context = lax.map(one_block, (query_tiles, key_blocks, positions))  24.6 us
    all_to_all x1, blocking collectives, shards(): lax.all_to_all(value_vectors, 'head', split_axis=1, concat_axis=0, tiled=...  18.3 us
    all_to_all x1, waiting for transfers between devices, shards(): lax.all_to_all(key_vectors, 'head', split_axis=1, concat_axis=0, tiled=True)  15 us
  transfers between devices with their start and end apart: 3, of which 1 were waited for; matrix products, arithmetic and copies ran while one was open for 2% of the time, Pallas kernels for 0%

commit v1 on v0

v1 whole, which is shorter than its diff:
```python
import functools
import math

import jax
import jax.numpy as jnp
from jax import lax
from jax.experimental import pallas as pl
from jax.experimental.pallas import tpu as pltpu
from jax.sharding import Mesh
from jax.sharding import PartitionSpec as P

HEAD_DIM = 128
BLOCK = 128
WIN = 16
WSEL = 10
GLOBALS = 4
SLOTS = WSEL + GLOBALS
HEADS = 16
PLANE = 64
FACTOR = math.log2(math.e) / math.sqrt(HEAD_DIM)
UNROLL = 4
PLANE_AXES = ("y", "x", "core")


def pick_kernel(ids, first, kinds, out):
    for slot in range(GLOBALS):
        place = ids[slot] - first[0]
        held = (place >= 0) & (place < PLANE)
        block = kinds[jnp.where(held, place, 0)]
        out[slot] = jnp.where(held, block, jnp.zeros_like(block))


def pick_globals(ids, first, kinds):
    scalars = pl.BlockSpec(memory_space=pltpu.SMEM)
    whole = pl.BlockSpec(memory_space=pltpu.VMEM)
    return pl.pallas_call(
        pick_kernel,
        out_shape=jax.ShapeDtypeStruct((GLOBALS, BLOCK, HEAD_DIM), jnp.bfloat16),
        in_specs=[scalars, scalars, whole],
        out_specs=whole,
        name="pick_globals",
    )(ids, first, kinds)


def attend_kernel(
    where, rows, query, own, other, halo_own, halo_other, global_own, global_other,
    out, keys, values, scores, weights, sems,
):
    core = where[0]
    first = where[1]

    def fill(own_to, other_to):
        copies = [
            (own, own_to.at[pl.ds(0, PLANE)]),
            (other, other_to.at[pl.ds(0, PLANE)]),
            (halo_own, own_to.at[pl.ds(PLANE, WIN)]),
            (halo_other, other_to.at[pl.ds(PLANE, WIN)]),
            (global_own, own_to.at[pl.ds(PLANE + WIN, GLOBALS)]),
            (global_other, other_to.at[pl.ds(PLANE + WIN, GLOBALS)]),
        ]
        started = [
            pltpu.make_async_copy(source, target, sems.at[at])
            for at, (source, target) in enumerate(copies)
        ]
        for copy in started:
            copy.start()
        for copy in started:
            copy.wait()

    @pl.when(core == 0)
    def _():
        fill(keys, values)

    @pl.when(core != 0)
    def _():
        fill(values, keys)

    causal = lax.broadcasted_iota(jnp.int32, (BLOCK, BLOCK), 0) >= lax.broadcasted_iota(
        jnp.int32, (BLOCK, BLOCK), 1
    )

    def attend_block(at, lane):
        row = 2 * at + core
        block_query = query[at]
        places, listed = [], []
        for slot in range(SLOTS):
            block_id = rows[row, slot]
            if slot < WSEL:
                offset = block_id - first
                place = jnp.where(offset >= 0, offset, offset + PLANE + WIN)
            else:
                place = PLANE + WIN + slot - WSEL
            listed.append(block_id >= 0)
            places.append(jnp.where(block_id >= 0, place, 0))
        highest = None
        for slot in range(0, SLOTS, 2):
            pair = jnp.concatenate([keys[places[slot]], keys[places[slot + 1]]], axis=0)
            both = lax.dot_general(
                block_query, pair, (((1,), (1,)), ((), ())), preferred_element_type=jnp.float32
            )
            for part in range(2):
                score = both[:, part * BLOCK : (part + 1) * BLOCK]
                allowed = causal if slot + part == 0 else listed[slot + part]
                score = jnp.where(allowed, score, -1e30)
                scores[lane, slot + part] = score
                highest = score if highest is None else jnp.maximum(highest, score)
        row_max = jnp.max(highest, axis=1, keepdims=True) * FACTOR
        row_max = jnp.broadcast_to(row_max, (BLOCK, BLOCK))
        total = None
        for slot in range(SLOTS):
            weight = jnp.exp2(scores[lane, slot] * FACTOR - row_max)
            total = weight if total is None else total + weight
            weights[lane, :, slot * BLOCK : (slot + 1) * BLOCK] = weight.astype(jnp.bfloat16)
        mixed = None
        for slot in range(0, SLOTS, 2):
            pair = jnp.concatenate([values[places[slot]], values[places[slot + 1]]], axis=0)
            term = jnp.dot(
                weights[lane, :, slot * BLOCK : (slot + 2) * BLOCK],
                pair,
                preferred_element_type=jnp.float32,
            )
            mixed = term if mixed is None else mixed + term
        denom = jnp.sum(total, axis=1, keepdims=True)
        out[at] = (mixed / denom).astype(jnp.bfloat16)

    def step(at, carry):
        for lane in range(UNROLL):
            attend_block(at * UNROLL + lane, lane)
        return carry

    lax.fori_loop(0, query.shape[0] // UNROLL, step, 0)


def attend(where, rows, query, own, other, halo_own, halo_other, global_own, global_other):
    scalars = pl.BlockSpec(memory_space=pltpu.SMEM)
    whole = pl.BlockSpec(memory_space=pltpu.VMEM)
    left = pl.BlockSpec(memory_space=pl.ANY)
    span = PLANE + WIN + GLOBALS
    pairs = query.shape[0] * SLOTS * BLOCK * BLOCK
    return pl.pallas_call(
        attend_kernel,
        out_shape=jax.ShapeDtypeStruct(query.shape, jnp.bfloat16),
        in_specs=[scalars, scalars, whole] + [left] * 6,
        out_specs=whole,
        scratch_shapes=[
            pltpu.VMEM((span, BLOCK, HEAD_DIM), jnp.bfloat16),
            pltpu.VMEM((span, BLOCK, HEAD_DIM), jnp.bfloat16),
            pltpu.VMEM((UNROLL, SLOTS, BLOCK, BLOCK), jnp.float32),
            pltpu.VMEM((UNROLL, BLOCK, SLOTS * BLOCK), jnp.bfloat16),
            pltpu.SemaphoreType.DMA((6,)),
        ],
        compiler_params=pltpu.CompilerParams(vmem_limit_bytes=40 << 20),
        cost_estimate=pl.CostEstimate(
            flops=4 * pairs * HEAD_DIM, bytes_accessed=8 << 20, transcendentals=pairs
        ),
        name="attend",
    )(where, rows, query, own, other, halo_own, halo_other, global_own, global_other)


def swapped(value):
    return lax.ppermute(value, "core", [(0, 1), (1, 0)])


def shards(queries, key_vectors, value_vectors, key_blocks):
    depth = lax.axis_size("z")
    breadth = lax.axis_size("y")
    up = [(at, at + 1) for at in range(depth - 1)]
    down = [(at + 1, at) for at in range(depth - 1)]
    core = lax.axis_index("core")
    first = lax.axis_index("z") * PLANE

    tokens = queries.shape[0]
    kinds = jnp.stack(
        [
            jnp.swapaxes(array.reshape(tokens, HEADS, HEAD_DIM), 0, 1)
            for array in (key_vectors, value_vectors)
        ],
        axis=1,
    ).reshape(2 * HEADS, tokens, HEAD_DIM)
    own = lax.all_to_all(kinds, PLANE_AXES, 0, 0, tiled=True).reshape(PLANE, BLOCK, HEAD_DIM)

    turned = [key_blocks] + [
        lax.ppermute(key_blocks, "y", [(at, (at + step) % breadth) for at in range(breadth)])
        for step in range(1, breadth)
    ]
    here = lax.axis_index("y")
    rows = jnp.stack(turned)[(here - jnp.arange(breadth)) % breadth].reshape(PLANE, SLOTS)
    above = lax.ppermute(key_blocks[-1, WSEL:], "z", down)
    ids = jnp.maximum(rows[-1, WSEL:], above)

    query = lax.all_to_all(
        jnp.transpose(
            queries.reshape(2, BLOCK, HEADS, HEAD_DIM), (2, 0, 1, 3)
        ).reshape(2 * HEADS, BLOCK, HEAD_DIM),
        PLANE_AXES, 0, 0, tiled=True,
    )

    other = swapped(own)
    halo_own = lax.ppermute(own[PLANE - WIN :], "z", up)
    halo_other = swapped(halo_own)

    part = pick_globals(ids, first[None], own).reshape(depth, -1, HEAD_DIM)
    pieces = lax.all_to_all(part, "z", 0, 0, tiled=True)
    summed = jnp.sum(pieces.astype(jnp.float32), axis=0, keepdims=True).astype(jnp.bfloat16)
    global_own = lax.all_to_all(
        jnp.broadcast_to(summed, part.shape), "z", 0, 0, tiled=True
    ).reshape(GLOBALS, BLOCK, HEAD_DIM)
    global_other = swapped(global_own)

    context = attend(
        jnp.stack([core, first]), rows, query,
        own, other, halo_own, halo_other, global_own, global_other,
    )
    back = lax.all_to_all(context, PLANE_AXES, 0, 0, tiled=True)
    return jnp.transpose(
        back.reshape(HEADS, 2, BLOCK, HEAD_DIM), (1, 2, 0, 3)
    ).reshape(tokens, HEADS * HEAD_DIM)


def solution(mesh):
    fine = Mesh(mesh.devices.reshape(-1, 4, 4, 2), ("z",) + PLANE_AXES)
    tokens = P(("z",) + PLANE_AXES, None)
    return jax.shard_map(
        shards,
        mesh=fine,
        in_specs=(tokens, tokens, tokens, P(("z", "y"), None)),
        out_specs=tokens,
        check_vma=False,
    )
```

time: 599 us -> 164 us (0.27)
  blocking collectives: 385 us -> 45.3 us
  local copies, waits for them, and re-layouts: 126 us -> 10.2 us
  other arithmetic: 39 us -> 0.94 us
  starting transfers between devices: 17.6 us -> 50.1 us
  Pallas kernels: 0 us -> 24.2 us
  waiting for transfers between devices: 15 us -> 32 us
  matrix products: 12.4 us -> 0 us
    psum x1 -> x0, blocking collectives: 231 us -> none  [shards(): shared = lax.psum(masked_term, 'seq').astype(jnp.bfloat16)]
    pmax x1 -> x0, blocking collectives: 56.6 us -> none  [shards(): global_ids = lax.pmax(jnp.max(key_blocks[:, WSEL:], axis=0), 'seq')]
    all_to_all x2, blocking collectives: 97.6 us -> 45.3 us  [the longest x1 24.7 us: shards(): pieces = lax.all_to_all(part, 'z', 0, 0, tiled=True)]
    gather x17 -> x1, local copies, waits for them, and re-layouts: 50.4 us -> 0.55 us  [shards(): jnp.stack(turned)[(here - jnp.arange(breadth)) % breadth]]
    dynamic_slice x48 -> x0, local copies, waits for them, and re-layouts: 24.6 us -> none  [shards(): context = lax.map(one_block, (query_tiles, key_blocks, positions))]
    pallas_call x0 -> x2, Pallas kernels: none -> 24.2 us  [the longest x1 21.9 us: attend(): pl.pallas_call(attend_kernel, out_shape=jax.ShapeDtypeStruct(query.shape,...]
    ppermute x1 -> x8, starting transfers between devices: 2.72 us -> 25.4 us  [the longest x3 11.4 us: shards(): lax.ppermute(key_blocks, 'y', [(at, (at + step) % breadth) for at in rang...]
    slice x48 -> x1, local copies, waits for them, and re-layouts: 21.7 us -> 1.88 us  [shards(): halo_own = lax.ppermute(own[PLANE - WIN:], 'z', up)]
  transfers between devices with their start and end apart: 3 -> 11, of which waited for: 1 -> 4; matrix products, arithmetic and copies ran while one was open for 2% -> 3% of each run, Pallas kernels for 0% -> 1%
where the time goes in v1:
time: 164 us; the launch traced here: 163 us
  starting transfers between devices  50.1 us (31%)
  blocking collectives  45.3 us (28%)
  waiting for transfers between devices  32 us (20%)
  Pallas kernels  24.2 us (15%)
  local copies, waits for them, and re-layouts  10.2 us (6%)
    all_to_all x1, blocking collectives, shards(): pieces = lax.all_to_all(part, 'z', 0, 0, tiled=True)  24.7 us
    pallas_call x1, Pallas kernels, attend(): pl.pallas_call(attend_kernel, out_shape=jax.ShapeDtypeStruct(query.shape,...  21.9 us
    all_to_all x1, blocking collectives, shards(): back = lax.all_to_all(context, PLANE_AXES, 0, 0, tiled=True)  20.6 us
    all_to_all x1, waiting for transfers between devices, shards(): lax.all_to_all(jnp.transpose(queries.reshape(2, BLOCK, HEADS, HEAD_DIM),...  12.8 us
    ppermute x3, waiting for transfers between devices, shards(): lax.ppermute(key_blocks, 'y', [(at, (at + step) % breadth) for at in rang...  11.4 us
    ppermute x3, starting transfers between devices, shards(): lax.ppermute(key_blocks, 'y', [(at, (at + step) % breadth) for at in rang...  11.4 us
    all_to_all x1, starting transfers between devices, shards(): lax.all_to_all(kinds, PLANE_AXES, 0, 0, tiled=True)  11.3 us
    ppermute x3, starting transfers between devices, swapped(): return lax.ppermute(value, 'core', [(0, 1), (1, 0)])  8.62 us
  transfers between devices with their start and end apart: 11, of which 4 were waited for; matrix products, arithmetic and copies ran while one was open for 3% of the time, Pallas kernels for 1%

profile of v1, /device:TPU:1, one launch (start us, length us, event | category | flops | bytes accessed | tf_op | source)
XLA Modules:
  0.0 163.0 jit_solution(15353399278456537680)
XLA Ops:
  0.0 0.0 copy-start
  0.0 1.5 copy.9
  1.5 0.0 copy-done
  1.6 0.2 copy.10
  1.8 0.2 pad_maximum_fusion
  2.0 1.9 %copy.6 = bf16[16,2,256,128]{3,2,1,0:T(8,128)(2,1)} copy(bf16[16,2,256,128]{3,0,2,1:T(8,128)(2,1)S(1)} %pad_maximum_fusion) | data formatting | bytes 4194304 | tf_op jit(solution)/shard_map/stack | solution.py:173
  3.9 0.0 copy-start.2
  3.9 11.3 %all-to-all-start.1 = ((bf16[32,256,128]{2,1,0:T(8,128)(2,1)}), bf16[32,256,128]{2,1,0:T(8,128)(2,1)}, u32[]{:S(2)}, u32[]{:S(2)}) async-start(bf16[32,256,128]{2,1,0:T(8,128)(2,1)} %bitcast.14), calls=%async_computation.1 | async-start | bytes 4194304 | tf_op jit(solution)/shard_map/all_to_all | solution.py:180
  15.2 0.0 copy-done.2
  15.2 4.9 %collective-permute-start.1 = (s32[16,14]{1,0:T(8,128)S(1)}, s32[16,14]{1,0:T(8,128)S(1)}, u32[]{:S(2)}, u32[]{:S(2)}) collective-permute-start(s32[16,14]{1,0:T(8,128)S(1)} %copy-done.2), channel_id=1, source_target_pairs={{0,16},{8,24},{16,0},{24,8},{1,17},{9,25},{17,1},{25,9},{2,18},{10... | collective-permute-start | bytes 2696 | tf_op jit(solution)/shard_map/ppermute | solution.py:183
  20.1 2.2 %collective-permute-start = (s32[16,14]{1,0:T(8,128)S(1)}, s32[16,14]{1,0:T(8,128)S(1)}, u32[]{:S(2)}, u32[]{:S(2)}) collective-permute-start(s32[16,14]{1,0:T(8,128)S(1)} %copy-done.2), channel_id=1, source_target_pairs={{0,8},{8,16},{16,24},{24,0},{1,9},{9,17},{17,25},{25,1},{2,10},{10... | collective-permute-start | bytes 2696 | tf_op jit(solution)/shard_map/ppermute | solution.py:183
  22.4 4.2 %collective-permute-start.2 = (s32[16,14]{1,0:T(8,128)S(1)}, s32[16,14]{1,0:T(8,128)S(1)}, u32[]{:S(2)}, u32[]{:S(2)}) collective-permute-start(s32[16,14]{1,0:T(8,128)S(1)} %copy-done.2), channel_id=1, source_target_pairs={{0,24},{8,0},{16,8},{24,16},{1,25},{9,1},{17,9},{25,17},{2,26},{10... | collective-permute-start | bytes 2696 | tf_op jit(solution)/shard_map/ppermute | solution.py:183
  26.6 0.1 slice_bitcast_fusion.1
  26.7 1.3 collective-permute-start.6
  28.0 11.4 %collective-permute-done.1 = s32[16,14]{1,0:T(8,128)S(1)} collective-permute-done((s32[16,14]{1,0:T(8,128)S(1)}, s32[16,14]{1,0:T(8,128)S(1)}, u32[]{:S(2)}, u32[]{:S(2)}) %collective-permute-start.1) | collective-permute-done | bytes 928 | tf_op jit(solution)/shard_map/ppermute | solution.py:183
  39.5 0.0 collective-permute-done
  39.5 0.0 collective-permute-done.2
  39.5 0.0 copy-start.1
  39.5 0.6 gather_fusion
  40.1 3.1 %all-to-all-done.1 = bf16[32,256,128]{2,1,0:T(8,128)(2,1)} async-done(((bf16[32,256,128]{2,1,0:T(8,128)(2,1)}), bf16[32,256,128]{2,1,0:T(8,128)(2,1)}, u32[]{:S(2)}, u32[]{:S(2)}) %all-to-all-start.1) | async-done | bytes 2097184 | tf_op jit(solution)/shard_map/all_to_all | solution.py:180
  43.2 4.3 %collective-permute-start.3 = (bf16[64,128,128]{2,1,0:T(8,128)(2,1)}, bf16[64,128,128]{2,1,0:T(8,128)(2,1)S(1)}, u32[]{:S(2)}, u32[]{:S(2)}) collective-permute-start(bf16[64,128,128]{2,1,0:T(8,128)(2,1)} %bitcast.15.kinds.own), channel_id=1, source_target_pairs={{0,1},{1,0},{2,3},{3,2},{4,5},{5,4},{6,7},{7,6},{8,9},{9,8},{10,11... | collective-permute-start | bytes 6291464 | tf_op jit(solution)/shard_map/ppermute | solution.py:161
  47.5 0.0 collective-permute-done.6
  47.5 0.6 fusion.2.ids
  48.1 2.3 %pick_globals.1 = bf16[4,128,128]{2,1,0:T(8,128)(2,1)} custom-call(s32[4]{0:T(128)} %fusion.2.ids, s32[1]{0:T(128)} %bitcast.1.first, bf16[64,128,128]{2,1,0:T(8,128)(2,1)} %bitcast.15.kinds.own), custom_call_target="tpu_custom_call" | custom-call | tf_op jit(solution)/shard_map/pick_globals/pallas_call | solution.py:36
  50.4 24.7 %all_to_all.25 = bf16[16,32,128]{2,1,0:T(8,128)(2,1)S(1)} all-to-all(bf16[16,32,128]{2,1,0:T(8,128)(2,1)} %bitcast.59), channel_id=1, replica_groups=mesh['z'=16,'y'=4,'x'=4,'core'=2] {'z'}, dimensions={0} | all-to-all | bytes 262144 | tf_op jit(solution)/shard_map/all_to_all | solution.py:203
  75.1 0.7 broadcast_in_dim.2
  75.8 6.2 %all-to-all-start.3 = ((bf16[16,32,128]{2,1,0:T(8,128)(2,1)}), bf16[16,32,128]{2,1,0:T(8,128)(2,1)S(1)}, u32[]{:S(2)}, u32[]{:S(2)}) async-start(bf16[16,32,128]{2,1,0:T(8,128)(2,1)} %broadcast_in_dim.2), calls=%async_computation.3 | async-start | bytes 262144 | tf_op jit(solution)/shard_map/all_to_all | solution.py:205
  82.0 1.9 %slice.18 = bf16[8,256,128]{2,1,0:T(8,128)(2,1)} slice(bf16[32,256,128]{2,1,0:T(8,128)(2,1)} %all-to-all-done.1), slice={[24:32], [0:256], [0:128]} | slice | bytes 1048576 | tf_op jit(solution)/shard_map/slice | solution.py:199
  83.8 4.1 %collective-permute-start.4 = (bf16[16,128,128]{2,1,0:T(8,128)(2,1)}, bf16[16,128,128]{2,1,0:T(8,128)(2,1)}, u32[]{:S(2)}, u32[]{:S(2)}) collective-permute-start(bf16[16,128,128]{2,1,0:T(8,128)(2,1)} %bitcast.16), channel_id=1, source_target_pairs={{0,32},{32,64},{64,96},{96,128},{128,160},{160,192},{192,224},{224... | collective-permute-start | bytes 1572872 | tf_op jit(solution)/shard_map/ppermute | solution.py:199
  87.9 0.0 copy-done.1
  87.9 0.2 copy.8
  88.1 1.2 copy.5
  89.4 4.6 %all-to-all-done.3 = bf16[16,32,128]{2,1,0:T(8,128)(2,1)S(1)} async-done(((bf16[16,32,128]{2,1,0:T(8,128)(2,1)}), bf16[16,32,128]{2,1,0:T(8,128)(2,1)S(1)}, u32[]{:S(2)}, u32[]{:S(2)}) %all-to-all-start.3) | async-done | bytes 131104 | tf_op jit(solution)/shard_map/all_to_all | solution.py:205
  94.0 7.3 %all-to-all-start = ((bf16[32,128,128]{2,1,0:T(8,128)(2,1)}), bf16[32,128,128]{2,1,0:T(8,128)(2,1)S(1)}, u32[]{:S(2)}, u32[]{:S(2)}) async-start(bf16[32,128,128]{2,1,0:T(8,128)(2,1)} %bitcast.50), calls=%async_computation | async-start | bytes 2097152 | tf_op jit(solution)/shard_map/all_to_all | solution.py:191
  101.3 0.0 collective-permute-done.4.halo_own
  101.3 2.4 %collective-permute-start.5 = (bf16[16,128,128]{2,1,0:T(8,128)(2,1)}, bf16[16,128,128]{2,1,0:T(8,128)(2,1)}, u32[]{:S(2)}, u32[]{:S(2)}) collective-permute-start(bf16[16,128,128]{2,1,0:T(8,128)(2,1)} %collective-permute-done.4.halo_own), channel_id=1, source_target_pairs={{0,1},{1,0},{2,3},{3,2},{4,5},{5,4},{6,7},{7,6},{8,9},{9,8},{10,11... | collective-permute-start | bytes 1572872 | tf_op jit(solution)/shard_map/ppermute | solution.py:161
  103.6 2.0 %collective-permute-start.7 = (bf16[4,128,128]{2,1,0:T(8,128)(2,1)S(1)}, bf16[4,128,128]{2,1,0:T(8,128)(2,1)S(1)}, u32[]{:S(2)}, u32[]{:S(2)}) collective-permute-start(bf16[4,128,128]{2,1,0:T(8,128)(2,1)S(1)} %bitcast.46), channel_id=1, source_target_pairs={{0,1},{1,0},{2,3},{3,2},{4,5},{5,4},{6,7},{7,6},{8,9},{9,8},{10,11... | collective-permute-start | bytes 393224 | tf_op jit(solution)/shard_map/ppermute | solution.py:161
  105.6 0.1 pad_add_fusion.1.where
  105.7 12.8 %all-to-all-done.query = bf16[32,128,128]{2,1,0:T(8,128)(2,1)S(1)} async-done(((bf16[32,128,128]{2,1,0:T(8,128)(2,1)}), bf16[32,128,128]{2,1,0:T(8,128)(2,1)S(1)}, u32[]{:S(2)}, u32[]{:S(2)}) %all-to-all-start) | async-done | bytes 1048608 | tf_op jit(solution)/shard_map/all_to_all | solution.py:191
  118.5 0.0 collective-permute-done.5.halo_other
  118.5 0.0 collective-permute-done.7.global_other
  118.5 0.0 collective-permute-done.3.other
  118.6 21.9 %attend.1 = bf16[32,128,128]{2,1,0:T(8,128)(2,1)S(1)} custom-call(s32[2]{0:T(128)S(1)} %pad_add_fusion.1.where, s32[64,14]{1,0:T(8,128)S(1)} %bitcast.49, bf16[32,128,128]{2,1,0:T(8,128)(2,1)S(1)} %all-to-all-done.query, bf16[64,128,128]{2,1,0:T(8,128)(2,1)} %bitcast.15.kinds.own, bf16[64,128,128]{2,1,0:T(8,128)(2,1)S(1)} %collective-permute-done.3.other, ...), custom_call_target="tpu_custom_call" | custom-call | flops 3758096384 | bytes 8388608 | tf_op jit(solution)/shard_map/attend/pallas_call | solution.py:140
  140.5 20.6 %all_to_all.26 = bf16[32,128,128]{2,1,0:T(8,128)(2,1)S(1)} all-to-all(bf16[32,128,128]{2,1,0:T(8,128)(2,1)S(1)} %attend.1), channel_id=1, replica_groups=mesh['z'=16,'y'=4,'x'=4,'core'=2] {'y','x','core'}, dimensions={0} | all-to-all | bytes 2097152 | tf_op jit(solution)/shard_map/all_to_all | solution.py:214
  161.1 0.7 copy.7
  161.8 1.2 copy.13
  (4 shorter events, 0.1 us)
Async XLA Ops:
  0.0 1.5 copy-start
  3.9 11.4 %copy-start.2 = (s32[16,14]{1,0:T(8,128)S(1)}, s32[16,14]{1,0:T(8,128)}, u32[]{:S(2)}) copy-start(s32[16,14]{1,0:T(8,128)} %param.7) | copy-start | bytes 2692
  3.9 39.3 %all-to-all-start.1 = ((bf16[32,256,128]{2,1,0:T(8,128)(2,1)}), bf16[32,256,128]{2,1,0:T(8,128)(2,1)}, u32[]{:S(2)}, u32[]{:S(2)}) async-start(bf16[32,256,128]{2,1,0:T(8,128)(2,1)} %bitcast.14), calls=%async_computation.1 | async-start | bytes 4194304 | tf_op jit(solution)/shard_map/all_to_all | solution.py:180
  15.2 24.2 %collective-permute-start.1 = (s32[16,14]{1,0:T(8,128)S(1)}, s32[16,14]{1,0:T(8,128)S(1)}, u32[]{:S(2)}, u32[]{:S(2)}) collective-permute-start(s32[16,14]{1,0:T(8,128)S(1)} %copy-done.2), channel_id=1, source_target_pairs={{0,16},{8,24},{16,0},{24,8},{1,17},{9,25},{17,1},{25,9},{2,18},{10... | collective-permute-start | bytes 2696 | tf_op jit(solution)/shard_map/ppermute | solution.py:183
  20.1 19.3 %collective-permute-start = (s32[16,14]{1,0:T(8,128)S(1)}, s32[16,14]{1,0:T(8,128)S(1)}, u32[]{:S(2)}, u32[]{:S(2)}) collective-permute-start(s32[16,14]{1,0:T(8,128)S(1)} %copy-done.2), channel_id=1, source_target_pairs={{0,8},{8,16},{16,24},{24,0},{1,9},{9,17},{17,25},{25,1},{2,10},{10... | collective-permute-start | bytes 2696 | tf_op jit(solution)/shard_map/ppermute | solution.py:183
  22.4 17.1 %collective-permute-start.2 = (s32[16,14]{1,0:T(8,128)S(1)}, s32[16,14]{1,0:T(8,128)S(1)}, u32[]{:S(2)}, u32[]{:S(2)}) collective-permute-start(s32[16,14]{1,0:T(8,128)S(1)} %copy-done.2), channel_id=1, source_target_pairs={{0,24},{8,0},{16,8},{24,16},{1,25},{9,1},{17,9},{25,17},{2,26},{10... | collective-permute-start | bytes 2696 | tf_op jit(solution)/shard_map/ppermute | solution.py:183
  26.7 20.8 %collective-permute-start.6 = (s32[4]{0:T(128)S(1)}, s32[4]{0:T(128)S(1)}, u32[]{:S(2)}, u32[]{:S(2)}) collective-permute-start(s32[4]{0:T(128)S(1)} %slice_bitcast_fusion.1), channel_id=1, source_target_pairs={{32,0},{64,32},{96,64},{128,96},{160,128},{192,160},{224,192},{256... | collective-permute-start | bytes 56 | tf_op jit(solution)/shard_map/ppermute | solution.py:188
  39.5 48.4 %copy-start.1 = (bf16[256,2048]{1,0:T(8,128)(2,1)S(1)}, bf16[256,2048]{1,0:T(8,128)(2,1)}, u32[]{:S(2)}) copy-start(bf16[256,2048]{1,0:T(8,128)(2,1)} %param.4) | copy-start | bytes 3145732
  43.2 75.4 %collective-permute-start.3 = (bf16[64,128,128]{2,1,0:T(8,128)(2,1)}, bf16[64,128,128]{2,1,0:T(8,128)(2,1)S(1)}, u32[]{:S(2)}, u32[]{:S(2)}) collective-permute-start(bf16[64,128,128]{2,1,0:T(8,128)(2,1)} %bitcast.15.kinds.own), channel_id=1, source_target_pairs={{0,1},{1,0},{2,3},{3,2},{4,5},{5,4},{6,7},{7,6},{8,9},{9,8},{10,11... | collective-permute-start | bytes 6291464 | tf_op jit(solution)/shard_map/ppermute | solution.py:161
  75.8 18.2 %all-to-all-start.3 = ((bf16[16,32,128]{2,1,0:T(8,128)(2,1)}), bf16[16,32,128]{2,1,0:T(8,128)(2,1)S(1)}, u32[]{:S(2)}, u32[]{:S(2)}) async-start(bf16[16,32,128]{2,1,0:T(8,128)(2,1)} %broadcast_in_dim.2), calls=%async_computation.3 | async-start | bytes 262144 | tf_op jit(solution)/shard_map/all_to_all | solution.py:205
  83.8 17.4 %collective-permute-start.4 = (bf16[16,128,128]{2,1,0:T(8,128)(2,1)}, bf16[16,128,128]{2,1,0:T(8,128)(2,1)}, u32[]{:S(2)}, u32[]{:S(2)}) collective-permute-start(bf16[16,128,128]{2,1,0:T(8,128)(2,1)} %bitcast.16), channel_id=1, source_target_pairs={{0,32},{32,64},{64,96},{96,128},{128,160},{160,192},{192,224},{224... | collective-permute-start | bytes 1572872 | tf_op jit(solution)/shard_map/ppermute | solution.py:199
  94.0 24.6 %all-to-all-start = ((bf16[32,128,128]{2,1,0:T(8,128)(2,1)}), bf16[32,128,128]{2,1,0:T(8,128)(2,1)S(1)}, u32[]{:S(2)}, u32[]{:S(2)}) async-start(bf16[32,128,128]{2,1,0:T(8,128)(2,1)} %bitcast.50), calls=%async_computation | async-start | bytes 2097152 | tf_op jit(solution)/shard_map/all_to_all | solution.py:191
  101.3 17.3 %collective-permute-start.5 = (bf16[16,128,128]{2,1,0:T(8,128)(2,1)}, bf16[16,128,128]{2,1,0:T(8,128)(2,1)}, u32[]{:S(2)}, u32[]{:S(2)}) collective-permute-start(bf16[16,128,128]{2,1,0:T(8,128)(2,1)} %collective-permute-done.4.halo_own), channel_id=1, source_target_pairs={{0,1},{1,0},{2,3},{3,2},{4,5},{5,4},{6,7},{7,6},{8,9},{9,8},{10,11... | collective-permute-start | bytes 1572872 | tf_op jit(solution)/shard_map/ppermute | solution.py:161
  103.6 14.9 %collective-permute-start.7 = (bf16[4,128,128]{2,1,0:T(8,128)(2,1)S(1)}, bf16[4,128,128]{2,1,0:T(8,128)(2,1)S(1)}, u32[]{:S(2)}, u32[]{:S(2)}) collective-permute-start(bf16[4,128,128]{2,1,0:T(8,128)(2,1)S(1)} %bitcast.46), channel_id=1, source_target_pairs={{0,1},{1,0},{2,3},{3,2},{4,5},{5,4},{6,7},{7,6},{8,9},{9,8},{10,11... | collective-permute-start | bytes 393224 | tf_op jit(solution)/shard_map/ppermute | solution.py:161

commit v2 on v1

v2 whole, which is shorter than its diff:
```python
import functools
import math

import jax
import jax.numpy as jnp
from jax import lax
from jax.experimental import pallas as pl
from jax.experimental.pallas import tpu as pltpu
from jax.sharding import Mesh
from jax.sharding import PartitionSpec as P

HEAD_DIM = 128
BLOCK = 128
WIN = 16
WSEL = 10
GLOBALS = 4
SLOTS = WSEL + GLOBALS
HEADS = 16
PLANE = 64
CHUNK = 16
FACTOR = math.log2(math.e) / math.sqrt(HEAD_DIM)
UNROLL = 4
PLANE_AXES = ("y", "x", "core")

SCALARS = pl.BlockSpec(memory_space=pltpu.SMEM)
WHOLE = pl.BlockSpec(memory_space=pltpu.VMEM)
LEFT = pl.BlockSpec(memory_space=pl.ANY)
BF16_TILE = jax.ShapeDtypeStruct((BLOCK, HEAD_DIM), jnp.bfloat16)


def pick_kernel(where, rows, above, kinds, *refs):
    outs, (buffer, sems) = refs[:GLOBALS], refs[GLOBALS:]
    first, turn = where[1], where[2]
    last = (where[3] + GLOBALS - PLANE // CHUNK + 1) % GLOBALS
    copies, present = [], []
    for step in range(GLOBALS):
        slot = (turn + step) % GLOBALS
        place = jnp.maximum(rows[last, CHUNK - 1, WSEL + slot], above[slot]) - first
        held = (place >= 0) & (place < PLANE)
        copies.append(
            pltpu.make_async_copy(
                kinds.at[jnp.where(held, place, 0)], buffer.at[step], sems.at[step]
            )
        )
        present.append(held)
    for copy in copies:
        copy.start()
    for step in range(GLOBALS):
        copies[step].wait()
        block = buffer[step]
        outs[step][...] = jnp.where(present[step], block, jnp.zeros_like(block))


def pick_globals(where, rows, above, kinds):
    return pl.pallas_call(
        pick_kernel,
        out_shape=[BF16_TILE] * GLOBALS,
        in_specs=[SCALARS, SCALARS, SCALARS, LEFT],
        out_specs=[WHOLE] * GLOBALS,
        scratch_shapes=[
            pltpu.VMEM((GLOBALS, BLOCK, HEAD_DIM), jnp.bfloat16),
            pltpu.SemaphoreType.DMA((GLOBALS,)),
        ],
        compiler_params=pltpu.CompilerParams(vmem_limit_bytes=20 << 20),
        name="pick_globals",
    )(where, rows, above, kinds)


def row_of(where, at):
    row = 2 * at + where[0]
    return (where[3] + GLOBALS - row // CHUNK) % GLOBALS, row % CHUNK


def window_kernel(start, low, high, with_halo, where, rows, query, own, other, *refs):
    if with_halo:
        halo_own, halo_other, *refs = refs
    out, out_max, out_sum, keys, values, scores, weights, sems = refs
    core, first = where[0], where[1]
    count = out.shape[0]
    chunks = (high - low) // CHUNK

    def copies(own_to, other_to, at):
        if at < chunks:
            source, target = pl.ds(low + at * CHUNK, CHUNK), pl.ds(at * CHUNK, CHUNK)
            yield pltpu.make_async_copy(own.at[source], own_to.at[target], sems.at[0, at])
            yield pltpu.make_async_copy(other.at[source], other_to.at[target], sems.at[1, at])
        else:
            target = pl.ds(at * CHUNK, WIN)
            yield pltpu.make_async_copy(halo_own, own_to.at[target], sems.at[0, at])
            yield pltpu.make_async_copy(halo_other, other_to.at[target], sems.at[1, at])

    parts = list(range(chunks)) + ([chunks] if with_halo else [])

    @pl.when(core == 0)
    def _():
        for part in parts:
            for copy in copies(keys, values, part):
                copy.start()

    @pl.when(core != 0)
    def _():
        for part in parts:
            for copy in copies(values, keys, part):
                copy.start()

    needed = {}
    for part in parts:
        step = 0
        if part < chunks:
            step = max(0, (low + part * CHUNK - 2 * start) // (2 * UNROLL))
        needed.setdefault(step, []).append(part)

    causal = lax.broadcasted_iota(jnp.int32, (BLOCK, BLOCK), 0) >= lax.broadcasted_iota(
        jnp.int32, (BLOCK, BLOCK), 1
    )

    def attend_block(at, lane):
        group, row = row_of(where, start + at)
        block_query = query[start + at]
        places, listed = [], []
        for slot in range(WSEL):
            block_id = rows[group, row, slot]
            place = block_id - first - low
            if with_halo:
                place = jnp.where(place >= 0, place, place + high + WIN)
            listed.append(block_id >= 0)
            places.append(jnp.where(block_id >= 0, place, 0))
        highest = None
        for slot in range(0, WSEL, 2):
            pair = jnp.concatenate([keys[places[slot]], keys[places[slot + 1]]], axis=0)
            both = lax.dot_general(
                block_query, pair, (((1,), (1,)), ((), ())), preferred_element_type=jnp.float32
            )
            for part in range(2):
                score = both[:, part * BLOCK : (part + 1) * BLOCK]
                if slot + part == 0:
                    score = jnp.where(causal, score, -1e30)
                elif with_halo:
                    score = jnp.where(listed[slot + part], score, -1e30)
                scores[lane, slot + part] = score
                highest = score if highest is None else jnp.maximum(highest, score)
        row_max = jnp.max(highest, axis=1, keepdims=True) * FACTOR
        row_max = jnp.broadcast_to(row_max, (BLOCK, BLOCK))
        out_max[at] = row_max
        total = None
        for slot in range(WSEL):
            weight = jnp.exp2(scores[lane, slot] * FACTOR - row_max)
            total = weight if total is None else total + weight
            weights[lane, :, slot * BLOCK : (slot + 1) * BLOCK] = weight.astype(jnp.bfloat16)
        out_sum[at] = total
        mixed = None
        for slot in range(0, WSEL, 2):
            pair = jnp.concatenate([values[places[slot]], values[places[slot + 1]]], axis=0)
            term = jnp.dot(
                weights[lane, :, slot * BLOCK : (slot + 2) * BLOCK],
                pair,
                preferred_element_type=jnp.float32,
            )
            mixed = term if mixed is None else mixed + term
        out[at] = mixed

    def step(at, carry):
        for when, needs in needed.items():

            @pl.when(at == when)
            def _(needs=needs):
                for part in needs:
                    for copy in copies(keys, values, part):
                        copy.wait()

        for lane in range(UNROLL):
            attend_block(at * UNROLL + lane, lane)
        return carry

    lax.fori_loop(0, count // UNROLL, step, 0)


def attend_window(start, count, low, high, where, rows, query, own, other, *halo):
    span = high - low + (WIN if halo else 0)
    sums = jax.ShapeDtypeStruct((count, BLOCK, HEAD_DIM), jnp.float32)
    pairs = count * WSEL * BLOCK * BLOCK
    return pl.pallas_call(
        functools.partial(window_kernel, start, low, high, bool(halo)),
        out_shape=[sums] * 3,
        in_specs=[SCALARS, SCALARS, WHOLE] + [LEFT] * (2 + len(halo)),
        out_specs=[WHOLE] * 3,
        scratch_shapes=[
            pltpu.VMEM((span, BLOCK, HEAD_DIM), jnp.bfloat16),
            pltpu.VMEM((span, BLOCK, HEAD_DIM), jnp.bfloat16),
            pltpu.VMEM((UNROLL, WSEL, BLOCK, BLOCK), jnp.float32),
            pltpu.VMEM((UNROLL, BLOCK, WSEL * BLOCK), jnp.bfloat16),
            pltpu.SemaphoreType.DMA((2, span // CHUNK)),
        ],
        compiler_params=pltpu.CompilerParams(vmem_limit_bytes=20 << 20),
        cost_estimate=pl.CostEstimate(
            flops=4 * pairs * HEAD_DIM, bytes_accessed=8 << 20, transcendentals=pairs
        ),
        name="attend_near" if halo else "attend_far",
    )(where, rows, query, own, other, *halo)


def global_kernel(
    where, rows, query, own, other, near_sum, near_max, near_total, far_sum, far_max, far_total,
    out, keys, values, weights, sems,
):
    core, turn = where[0], where[2]

    def copies(own_to, other_to):
        yield pltpu.make_async_copy(own, own_to, sems.at[0])
        yield pltpu.make_async_copy(other, other_to, sems.at[1])

    @pl.when(core == 0)
    def _():
        for copy in copies(keys, values):
            copy.start()

    @pl.when(core != 0)
    def _():
        for copy in copies(values, keys):
            copy.start()

    for copy in copies(keys, values):
        copy.wait()

    slots = [(turn + GLOBALS - step) % GLOBALS for step in range(GLOBALS)]

    def merge(at, of, lane, sums, maxima, totals):
        group, row = row_of(where, at)
        block_query = query[at]
        listed = [rows[group, row, WSEL + slot] >= 0 for slot in slots]
        held, highest = [], None
        for step in range(0, GLOBALS, 2):
            pair = jnp.concatenate([keys[step], keys[step + 1]], axis=0)
            both = lax.dot_general(
                block_query, pair, (((1,), (1,)), ((), ())), preferred_element_type=jnp.float32
            )
            for part in range(2):
                score = both[:, part * BLOCK : (part + 1) * BLOCK]
                score = jnp.where(listed[step + part], score, -1e30)
                held.append(score)
                highest = score if highest is None else jnp.maximum(highest, score)
        row_max = jnp.max(highest, axis=1, keepdims=True) * FACTOR
        window_max = maxima[of]
        row_max = jnp.maximum(jnp.broadcast_to(row_max, (BLOCK, BLOCK)), window_max)
        shrink = jnp.exp2(window_max - row_max)
        total = totals[of] * shrink
        for step in range(GLOBALS):
            weight = jnp.exp2(held[step] * FACTOR - row_max)
            total = total + weight
            weights[lane, :, step * BLOCK : (step + 1) * BLOCK] = weight.astype(jnp.bfloat16)
        mixed = sums[of] * shrink
        for step in range(0, GLOBALS, 2):
            pair = jnp.concatenate([values[step], values[step + 1]], axis=0)
            mixed = mixed + jnp.dot(
                weights[lane, :, step * BLOCK : (step + 2) * BLOCK],
                pair,
                preferred_element_type=jnp.float32,
            )
        denom = jnp.sum(total, axis=1, keepdims=True)
        out[at] = (mixed / denom).astype(jnp.bfloat16)

    split = near_sum.shape[0]

    def near(at, carry):
        for lane in range(UNROLL):
            merge(at * UNROLL + lane, at * UNROLL + lane, lane, near_sum, near_max, near_total)
        return carry

    def far(at, carry):
        for lane in range(UNROLL):
            of = at * UNROLL + lane
            merge(split + of, of, lane, far_sum, far_max, far_total)
        return carry

    lax.fori_loop(0, split // UNROLL, near, 0)
    lax.fori_loop(0, far_sum.shape[0] // UNROLL, far, 0)


def attend_global(where, rows, query, own, other, near, far):
    pairs = query.shape[0] * GLOBALS * BLOCK * BLOCK
    return pl.pallas_call(
        global_kernel,
        out_shape=jax.ShapeDtypeStruct(query.shape, jnp.bfloat16),
        in_specs=[SCALARS, SCALARS, WHOLE, LEFT, LEFT] + [WHOLE] * 6,
        out_specs=WHOLE,
        scratch_shapes=[
            pltpu.VMEM((GLOBALS, BLOCK, HEAD_DIM), jnp.bfloat16),
            pltpu.VMEM((GLOBALS, BLOCK, HEAD_DIM), jnp.bfloat16),
            pltpu.VMEM((UNROLL, BLOCK, GLOBALS * BLOCK), jnp.bfloat16),
            pltpu.SemaphoreType.DMA((2,)),
        ],
        compiler_params=pltpu.CompilerParams(vmem_limit_bytes=20 << 20),
        cost_estimate=pl.CostEstimate(
            flops=4 * pairs * HEAD_DIM, bytes_accessed=8 << 20, transcendentals=pairs
        ),
        name="attend_global",
    )(where, rows, query, own, other, *near, *far)


def swapped(value):
    return lax.ppermute(value, "core", [(0, 1), (1, 0)])


def added(*values):
    return sum(value.astype(jnp.float32) for value in values).astype(jnp.bfloat16)


def shards(queries, key_vectors, value_vectors, key_blocks):
    depth = lax.axis_size("z")
    breadth = lax.axis_size("y")
    up = [(at, at + 1) for at in range(depth - 1)]
    down = [(at + 1, at) for at in range(depth - 1)]
    level = lax.axis_index("z")
    where = jnp.stack(
        [lax.axis_index("core"), level * PLANE, level % GLOBALS, lax.axis_index("y")]
    )

    tokens = queries.shape[0]
    kinds = jnp.stack(
        [
            jnp.swapaxes(array.reshape(tokens, HEADS, HEAD_DIM), 0, 1)
            for array in (key_vectors, value_vectors)
        ],
        axis=1,
    ).reshape(2 * HEADS, tokens, HEAD_DIM)
    own = lax.all_to_all(kinds, PLANE_AXES, 0, 0, tiled=True).reshape(PLANE, BLOCK, HEAD_DIM)

    rows = jnp.stack(
        [key_blocks]
        + [
            lax.ppermute(key_blocks, "y", [(at, (at + step) % breadth) for at in range(breadth)])
            for step in range(1, breadth)
        ]
    )
    above = lax.ppermute(key_blocks[-1, WSEL:], "z", down)
    own, rows, above = lax.optimization_barrier((own, rows, above))

    sent = jnp.transpose(
        queries.reshape(2, BLOCK, HEADS, HEAD_DIM), (2, 0, 1, 3)
    ).reshape(2 * HEADS, BLOCK, HEAD_DIM)
    query = lax.all_to_all(sent, PLANE_AXES, 0, 0, tiled=True)

    def within(step):
        return [(at, at - at % GLOBALS + (at + step) % GLOBALS) for at in range(depth)]

    def across(step):
        return [(at, (at + GLOBALS * step) % depth) for at in range(depth)]

    other = swapped(own)
    parts = pick_globals(where, rows, above, own)
    held = added(
        parts[0], *[lax.ppermute(parts[step], "z", within(step)) for step in range(1, GLOBALS)]
    )
    halo_own = lax.ppermute(own[PLANE - WIN :], "z", up)
    halo_other = swapped(halo_own)

    half = PLANE // 4
    arrived = [lax.ppermute(held, "z", across(step)) for step in range(1, depth // GLOBALS)]
    after, _ = lax.optimization_barrier((query, held))
    far = attend_window(half, half, CHUNK, PLANE, where, rows, after, own, other)
    far, held, arrived = lax.optimization_barrier((far, held, arrived))
    held = added(held, *arrived)
    arrived = [lax.ppermute(held, "z", within(step)) for step in range(1, GLOBALS)]
    after, _ = lax.optimization_barrier((query, held))
    near = attend_window(0, half, 0, 2 * half, where, rows, after, own, other, halo_own, halo_other)
    near, held, arrived = lax.optimization_barrier((near, held, arrived))
    global_own = jnp.stack([held] + list(arrived))
    global_other = swapped(global_own)
    context = attend_global(where, rows, query, global_own, global_other, near, far)
    back = lax.all_to_all(context, PLANE_AXES, 0, 0, tiled=True)
    return jnp.transpose(
        back.reshape(HEADS, 2, BLOCK, HEAD_DIM), (1, 2, 0, 3)
    ).reshape(tokens, HEADS * HEAD_DIM)


def solution(mesh):
    fine = Mesh(mesh.devices.reshape(-1, 4, 4, 2), ("z",) + PLANE_AXES)
    tokens = P(("z",) + PLANE_AXES, None)
    return jax.shard_map(
        shards,
        mesh=fine,
        in_specs=(tokens, tokens, tokens, P(("z", "y"), None)),
        out_specs=tokens,
        check_vma=False,
    )
```

time: 164 us -> 168 us (1.024)
  starting transfers between devices: 50.1 us -> 83.6 us
  blocking collectives: 45.3 us -> 24.6 us
  waiting for transfers between devices: 32 us -> 16.1 us
  Pallas kernels: 24.2 us -> 32.8 us
    ppermute x0 -> x9, starting transfers between devices: none -> 43.4 us  [the longest x3 24.7 us: shards(): lax.ppermute(held, 'z', across(step))]
    all_to_all x1 -> x0, blocking collectives: 24.7 us -> none  [shards(): pieces = lax.all_to_all(part, 'z', 0, 0, tiled=True)]
    all_to_all x2 -> x1, waiting for transfers between devices: 17.4 us -> 0.01 us  [shards(): query = lax.all_to_all(sent, PLANE_AXES, 0, 0, tiled=True)]
    all_to_all x2 -> x1, starting transfers between devices: 13.4 us -> 3.72 us  [shards(): query = lax.all_to_all(sent, PLANE_AXES, 0, 0, tiled=True)]
    pallas_call x2 -> x4, Pallas kernels: 24.2 us -> 32.8 us  [the longest x2 19.7 us: attend_window(): pl.pallas_call(functools.partial(window_kernel, start, low, high, bool(ha...]
    all_to_all x1, blocking collectives: 20.6 us -> 24.6 us  [shards(): back = lax.all_to_all(context, PLANE_AXES, 0, 0, tiled=True)]
    ppermute x3, starting transfers between devices: 8.62 us -> 10.8 us  [swapped(): return lax.ppermute(value, 'core', [(0, 1), (1, 0)])]
    ppermute x1, starting transfers between devices: 4.06 us -> 2.27 us  [shards(): halo_own = lax.ppermute(own[PLANE - WIN:], 'z', up)]
  transfers between devices with their start and end apart: 11 -> 19, of which waited for: 4 -> 3; matrix products, arithmetic and copies ran while one was open for 3% -> 2% of each run, Pallas kernels for 1% -> 13%
where the time goes in v2:
time: 168 us; the launch traced here: 167 us
  starting transfers between devices  83.6 us (50%)
  Pallas kernels  32.8 us (20%)
  blocking collectives  24.6 us (15%)
  waiting for transfers between devices  16.1 us (10%)
  local copies, waits for them, and re-layouts  9.19 us (5%)
    ppermute x3, starting transfers between devices, shards(): lax.ppermute(held, 'z', across(step))  24.7 us
    all_to_all x1, blocking collectives, shards(): back = lax.all_to_all(context, PLANE_AXES, 0, 0, tiled=True)  24.6 us
    pallas_call x2, Pallas kernels, attend_window(): pl.pallas_call(functools.partial(window_kernel, start, low, high, bool(ha...  19.7 us
    pallas_call x1, Pallas kernels, attend_global(): pl.pallas_call(global_kernel, out_shape=jax.ShapeDtypeStruct(query.shape,...  11.8 us
    ppermute x3, waiting for transfers between devices, shards(): lax.ppermute(key_blocks, 'y', [(at, (at + step) % breadth) for at in rang...  11.4 us
    ppermute x3, starting transfers between devices, shards(): lax.ppermute(key_blocks, 'y', [(at, (at + step) % breadth) for at in rang...  11.4 us
    ppermute x3, starting transfers between devices, swapped(): return lax.ppermute(value, 'core', [(0, 1), (1, 0)])  10.8 us
    ppermute x3, starting transfers between devices, shards(): lax.ppermute(parts[step], 'z', within(step))  10.8 us
  transfers between devices with their start and end apart: 19, of which 3 were waited for; matrix products, arithmetic and copies ran while one was open for 2% of the time, Pallas kernels for 13%

profile of v2, /device:TPU:1, one launch (start us, length us, event | category | flops | bytes accessed | tf_op | source)
XLA Modules:
  0.0 167.1 jit_solution(15763989589276604219)
XLA Ops:
  0.0 1.5 copy.8
  1.6 0.2 copy.9
  1.8 0.2 pad_maximum_fusion
  2.0 1.9 %copy.5 = bf16[16,2,256,128]{3,2,1,0:T(8,128)(2,1)} copy(bf16[16,2,256,128]{3,0,2,1:T(8,128)(2,1)S(1)} %pad_maximum_fusion) | data formatting | bytes 4194304 | tf_op jit(solution)/shard_map/stack | solution.py:319
  3.9 10.7 %all-to-all-start = ((bf16[32,256,128]{2,1,0:T(8,128)(2,1)}), bf16[32,256,128]{2,1,0:T(8,128)(2,1)S(1)}, u32[]{:S(2)}, u32[]{:S(2)}) async-start(bf16[32,256,128]{2,1,0:T(8,128)(2,1)} %bitcast.47), calls=%async_computation | async-start | bytes 4194304 | tf_op jit(solution)/shard_map/all_to_all | solution.py:326
  14.6 4.9 %collective-permute-start.1 = (s32[16,14]{1,0:T(8,128)S(1)}, s32[16,14]{1,0:T(8,128)S(1)}, u32[]{:S(2)}, u32[]{:S(2)}) collective-permute-start(s32[16,14]{1,0:T(8,128)S(1)} %copy-done.1), channel_id=1, source_target_pairs={{0,16},{8,24},{16,0},{24,8},{1,17},{9,25},{17,1},{25,9},{2,18},{10... | collective-permute-start | bytes 2696 | tf_op jit(solution)/shard_map/ppermute | solution.py:331
  19.5 2.2 %collective-permute-start = (s32[16,14]{1,0:T(8,128)S(1)}, s32[16,14]{1,0:T(8,128)S(1)}, u32[]{:S(2)}, u32[]{:S(2)}) collective-permute-start(s32[16,14]{1,0:T(8,128)S(1)} %copy-done.1), channel_id=1, source_target_pairs={{0,8},{8,16},{16,24},{24,0},{1,9},{9,17},{17,25},{25,1},{2,10},{10... | collective-permute-start | bytes 2696 | tf_op jit(solution)/shard_map/ppermute | solution.py:331
  21.7 4.2 %collective-permute-start.2 = (s32[16,14]{1,0:T(8,128)S(1)}, s32[16,14]{1,0:T(8,128)S(1)}, u32[]{:S(2)}, u32[]{:S(2)}) collective-permute-start(s32[16,14]{1,0:T(8,128)S(1)} %copy-done.1), channel_id=1, source_target_pairs={{0,24},{8,0},{16,8},{24,16},{1,25},{9,1},{17,9},{25,17},{2,26},{10... | collective-permute-start | bytes 2696 | tf_op jit(solution)/shard_map/ppermute | solution.py:331
  26.0 0.1 slice_bitcast_fusion
  26.1 1.3 collective-permute-start.3
  27.3 11.4 %collective-permute-done.1 = s32[16,14]{1,0:T(8,128)S(1)} collective-permute-done((s32[16,14]{1,0:T(8,128)S(1)}, s32[16,14]{1,0:T(8,128)S(1)}, u32[]{:S(2)}, u32[]{:S(2)}) %collective-permute-start.1) | collective-permute-done | bytes 928 | tf_op jit(solution)/shard_map/ppermute | solution.py:331
  38.8 0.0 collective-permute-done
  38.8 0.0 collective-permute-done.2
  38.8 0.0 collective-permute-done.3.above
  38.8 3.7 %all-to-all-done = bf16[32,256,128]{2,1,0:T(8,128)(2,1)S(1)} async-done(((bf16[32,256,128]{2,1,0:T(8,128)(2,1)}), bf16[32,256,128]{2,1,0:T(8,128)(2,1)S(1)}, u32[]{:S(2)}, u32[]{:S(2)}) %all-to-all-start) | async-done | bytes 2097184 | tf_op jit(solution)/shard_map/all_to_all | solution.py:326
  42.5 4.3 %collective-permute-start.7 = (bf16[64,128,128]{2,1,0:T(8,128)(2,1)S(1)}, bf16[64,128,128]{2,1,0:T(8,128)(2,1)}, u32[]{:S(2)}, u32[]{:S(2)}) collective-permute-start(bf16[64,128,128]{2,1,0:T(8,128)(2,1)S(1)} %bitcast.42), channel_id=1, source_target_pairs={{0,1},{1,0},{2,3},{3,2},{4,5},{5,4},{6,7},{7,6},{8,9},{9,8},{10,11... | collective-permute-start | bytes 6291464 | tf_op jit(solution)/shard_map/ppermute | solution.py:301
  46.8 1.5 copy.10
  48.2 1.2 copy.6
  49.5 3.7 %all-to-all-start.1 = ((bf16[32,128,128]{2,1,0:T(8,128)(2,1)}), bf16[32,128,128]{2,1,0:T(8,128)(2,1)S(1)}, u32[]{:S(2)}, u32[]{:S(2)}) async-start(bf16[32,128,128]{2,1,0:T(8,128)(2,1)} %bitcast.48), calls=%async_computation.1 | async-start | bytes 2097152 | tf_op jit(solution)/shard_map/all_to_all | solution.py:341
  53.2 0.8 slice.7
  54.1 2.3 %collective-permute-start.11 = (bf16[16,128,128]{2,1,0:T(8,128)(2,1)}, bf16[16,128,128]{2,1,0:T(8,128)(2,1)}, u32[]{:S(2)}, u32[]{:S(2)}) collective-permute-start(bf16[16,128,128]{2,1,0:T(8,128)(2,1)} %slice.7), channel_id=1, source_target_pairs={{0,32},{32,64},{64,96},{96,128},{128,160},{160,192},{192,224},{224... | collective-permute-start | bytes 1572872 | tf_op jit(solution)/shard_map/ppermute | solution.py:354
  56.3 0.1 pad_add_fusion.1.where
  56.4 1.4 pick_globals.1
  57.8 2.8 %collective-permute-start.4 = (bf16[128,128]{1,0:T(8,128)(2,1)S(1)}, bf16[128,128]{1,0:T(8,128)(2,1)S(1)}, u32[]{:S(2)}, u32[]{:S(2)}) collective-permute-start(bf16[128,128]{1,0:T(8,128)(2,1)S(1)} %get-tuple-element.38), channel_id=1, source_target_pairs={{0,32},{32,64},{64,96},{96,0},{128,160},{160,192},{192,224},{224,1... | collective-permute-start | bytes 98312 | tf_op jit(solution)/shard_map/ppermute | solution.py:352
  60.6 6.1 %collective-permute-start.5 = (bf16[128,128]{1,0:T(8,128)(2,1)S(1)}, bf16[128,128]{1,0:T(8,128)(2,1)S(1)}, u32[]{:S(2)}, u32[]{:S(2)}) collective-permute-start(bf16[128,128]{1,0:T(8,128)(2,1)S(1)} %get-tuple-element.39), channel_id=1, source_target_pairs={{0,64},{32,96},{64,0},{96,32},{128,192},{160,224},{192,128},{224,1... | collective-permute-start | bytes 98312 | tf_op jit(solution)/shard_map/ppermute | solution.py:352
  66.7 1.9 %collective-permute-start.6 = (bf16[128,128]{1,0:T(8,128)(2,1)S(1)}, bf16[128,128]{1,0:T(8,128)(2,1)S(1)}, u32[]{:S(2)}, u32[]{:S(2)}) collective-permute-start(bf16[128,128]{1,0:T(8,128)(2,1)S(1)} %get-tuple-element.40), channel_id=1, source_target_pairs={{0,96},{32,0},{64,32},{96,64},{128,224},{160,128},{192,160},{224,1... | collective-permute-start | bytes 98312 | tf_op jit(solution)/shard_map/ppermute | solution.py:352
  68.6 0.0 collective-permute-done.11.refs_0_
  68.6 3.0 %collective-permute-start.12 = (bf16[16,128,128]{2,1,0:T(8,128)(2,1)}, bf16[16,128,128]{2,1,0:T(8,128)(2,1)}, u32[]{:S(2)}, u32[]{:S(2)}) collective-permute-start(bf16[16,128,128]{2,1,0:T(8,128)(2,1)} %collective-permute-done.11.refs_0_), channel_id=1, source_target_pairs={{0,1},{1,0},{2,3},{3,2},{4,5},{5,4},{6,7},{7,6},{8,9},{9,8},{10,11... | collective-permute-start | bytes 1572872 | tf_op jit(solution)/shard_map/ppermute | solution.py:301
  71.6 0.0 collective-permute-done.4
  71.6 0.0 collective-permute-done.5
  71.6 0.0 collective-permute-done.6
  71.7 12.5 %collective-permute-start.10 = (bf16[128,128]{1,0:T(8,128)(2,1)S(1)}, bf16[128,128]{1,0:T(8,128)(2,1)S(1)}, u32[]{:S(2)}, u32[]{:S(2)}) collective-permute-start(bf16[128,128]{1,0:T(8,128)(2,1)S(1)} %add_convert_fusion.1), channel_id=1, source_target_pairs={{0,384},{32,416},{64,448},{96,480},{128,0},{160,32},{192,64},{224,... | collective-permute-start | bytes 98312 | tf_op jit(solution)/shard_map/ppermute | solution.py:358
  84.2 4.9 %collective-permute-start.9 = (bf16[128,128]{1,0:T(8,128)(2,1)S(1)}, bf16[128,128]{1,0:T(8,128)(2,1)S(1)}, u32[]{:S(2)}, u32[]{:S(2)}) collective-permute-start(bf16[128,128]{1,0:T(8,128)(2,1)S(1)} %add_convert_fusion.1), channel_id=1, source_target_pairs={{0,256},{32,288},{64,320},{96,352},{128,384},{160,416},{192,448},{... | collective-permute-start | bytes 98312 | tf_op jit(solution)/shard_map/ppermute | solution.py:358
  89.1 7.3 %collective-permute-start.8 = (bf16[128,128]{1,0:T(8,128)(2,1)S(1)}, bf16[128,128]{1,0:T(8,128)(2,1)S(1)}, u32[]{:S(2)}, u32[]{:S(2)}) collective-permute-start(bf16[128,128]{1,0:T(8,128)(2,1)S(1)} %add_convert_fusion.1), channel_id=1, source_target_pairs={{0,128},{32,160},{64,192},{96,224},{128,256},{160,288},{192,320},{... | collective-permute-start | bytes 98312 | tf_op jit(solution)/shard_map/ppermute | solution.py:358
  96.4 9.7 %attend_far.1 = (f32[16,128,128]{2,1,0:T(8,128)S(1)}, f32[16,128,128]{2,1,0:T(8,128)S(1)}, f32[16,128,128]{2,1,0:T(8,128)S(1)}) custom-call(s32[4]{0:T(128)S(1)} %pad_add_fusion.1.where, s32[4,16,14]{2,1,0:T(8,128)S(1)} %pad_add_fusion.rows, bf16[32,128,128]{2,1,0:T(8,128)(2,1)S(1)} %all-to-all-done.1.query, bf16[64,128,128]{2,1,0:T(8,128)(2,1)S(1)} %bitcast.45, ...), custom_call_target="tpu_custom_call" | custom-call | flops 1342177280 | bytes 8388608 | tf_op jit(solution)/shard_map/attend_far/pallas_call | solution.py:182
  106.1 0.0 collective-permute-done.9
  106.2 2.7 %collective-permute-start.15 = (bf16[128,128]{1,0:T(8,128)(2,1)S(1)}, bf16[128,128]{1,0:T(8,128)(2,1)S(1)}, u32[]{:S(2)}, u32[]{:S(2)}) collective-permute-start(bf16[128,128]{1,0:T(8,128)(2,1)S(1)} %add_convert_fusion), channel_id=1, source_target_pairs={{0,96},{32,0},{64,32},{96,64},{128,224},{160,128},{192,160},{224,1... | collective-permute-start | bytes 98312 | tf_op jit(solution)/shard_map/ppermute | solution.py:363
  108.9 2.5 %collective-permute-start.14 = (bf16[128,128]{1,0:T(8,128)(2,1)S(1)}, bf16[128,128]{1,0:T(8,128)(2,1)S(1)}, u32[]{:S(2)}, u32[]{:S(2)}) collective-permute-start(bf16[128,128]{1,0:T(8,128)(2,1)S(1)} %add_convert_fusion), channel_id=1, source_target_pairs={{0,64},{32,96},{64,0},{96,32},{128,192},{160,224},{192,128},{224,1... | collective-permute-start | bytes 98312 | tf_op jit(solution)/shard_map/ppermute | solution.py:363
  111.4 2.8 %collective-permute-start.13 = (bf16[128,128]{1,0:T(8,128)(2,1)S(1)}, bf16[128,128]{1,0:T(8,128)(2,1)S(1)}, u32[]{:S(2)}, u32[]{:S(2)}) collective-permute-start(bf16[128,128]{1,0:T(8,128)(2,1)S(1)} %add_convert_fusion), channel_id=1, source_target_pairs={{0,32},{32,64},{64,96},{96,0},{128,160},{160,192},{192,224},{224,1... | collective-permute-start | bytes 98312 | tf_op jit(solution)/shard_map/ppermute | solution.py:363
  114.2 0.0 collective-permute-done.12.refs_1_
  114.2 10.0 %attend_near.1 = (f32[16,128,128]{2,1,0:T(8,128)S(1)}, f32[16,128,128]{2,1,0:T(8,128)S(1)}, f32[16,128,128]{2,1,0:T(8,128)S(1)}) custom-call(s32[4]{0:T(128)S(1)} %pad_add_fusion.1.where, s32[4,16,14]{2,1,0:T(8,128)S(1)} %pad_add_fusion.rows, bf16[32,128,128]{2,1,0:T(8,128)(2,1)S(1)} %all-to-all-done.1.query, bf16[64,128,128]{2,1,0:T(8,128)(2,1)S(1)} %bitcast.46, ...), custom_call_target="tpu_custom_call" | custom-call | flops 1342177280 | bytes 8388608 | tf_op jit(solution)/shard_map/attend_near/pallas_call | solution.py:182
  124.2 0.0 collective-permute-done.13
  124.3 3.6 %collective-permute-start.16 = (bf16[4,128,128]{2,1,0:T(8,128)(2,1)S(1)}, bf16[4,128,128]{2,1,0:T(8,128)(2,1)S(1)}, u32[]{:S(2)}, u32[]{:S(2)}) collective-permute-start(bf16[4,128,128]{2,1,0:T(8,128)(2,1)S(1)} %pad_maximum_fusion.1.own), channel_id=1, source_target_pairs={{0,1},{1,0},{2,3},{3,2},{4,5},{5,4},{6,7},{7,6},{8,9},{9,8},{10,11... | collective-permute-start | bytes 393224 | tf_op jit(solution)/shard_map/ppermute | solution.py:301
  127.8 1.0 collective-permute-done.16.other
  128.8 11.8 %attend_global.1 = bf16[32,128,128]{2,1,0:T(8,128)(2,1)S(1)} custom-call(s32[4]{0:T(128)S(1)} %pad_add_fusion.1.where, s32[4,16,14]{2,1,0:T(8,128)S(1)} %pad_add_fusion.rows, bf16[32,128,128]{2,1,0:T(8,128)(2,1)S(1)} %all-to-all-done.1.query, bf16[4,128,128]{2,1,0:T(8,128)(2,1)S(1)} %pad_maximum_fusion.1.own, ...), custom_call_target="tpu_custom_call" | custom-call | flops 1073741824 | bytes 8388608 | tf_op jit(solution)/shard_map/attend_global/pallas_call | solution.py:281
  140.6 24.6 %all_to_all.15 = bf16[32,128,128]{2,1,0:T(8,128)(2,1)S(1)} all-to-all(bf16[32,128,128]{2,1,0:T(8,128)(2,1)S(1)} %attend_global.1), channel_id=1, replica_groups=mesh['z'=16,'y'=4,'x'=4,'core'=2] {'y','x','core'}, dimensions={0} | all-to-all | bytes 2097152 | tf_op jit(solution)/shard_map/all_to_all | solution.py:370
  165.2 0.7 copy.7
  165.9 1.2 copy.13
  (14 shorter events, 0.1 us)
Async XLA Ops:
  0.0 1.6 copy-start
  3.9 10.7 %copy-start.1 = (s32[16,14]{1,0:T(8,128)S(1)}, s32[16,14]{1,0:T(8,128)}, u32[]{:S(2)}) copy-start(s32[16,14]{1,0:T(8,128)} %param.7) | copy-start | bytes 2692
  3.9 38.6 %all-to-all-start = ((bf16[32,256,128]{2,1,0:T(8,128)(2,1)}), bf16[32,256,128]{2,1,0:T(8,128)(2,1)S(1)}, u32[]{:S(2)}, u32[]{:S(2)}) async-start(bf16[32,256,128]{2,1,0:T(8,128)(2,1)} %bitcast.47), calls=%async_computation | async-start | bytes 4194304 | tf_op jit(solution)/shard_map/all_to_all | solution.py:326
  14.6 24.2 %collective-permute-start.1 = (s32[16,14]{1,0:T(8,128)S(1)}, s32[16,14]{1,0:T(8,128)S(1)}, u32[]{:S(2)}, u32[]{:S(2)}) collective-permute-start(s32[16,14]{1,0:T(8,128)S(1)} %copy-done.1), channel_id=1, source_target_pairs={{0,16},{8,24},{16,0},{24,8},{1,17},{9,25},{17,1},{25,9},{2,18},{10... | collective-permute-start | bytes 2696 | tf_op jit(solution)/shard_map/ppermute | solution.py:331
  19.5 19.3 %collective-permute-start = (s32[16,14]{1,0:T(8,128)S(1)}, s32[16,14]{1,0:T(8,128)S(1)}, u32[]{:S(2)}, u32[]{:S(2)}) collective-permute-start(s32[16,14]{1,0:T(8,128)S(1)} %copy-done.1), channel_id=1, source_target_pairs={{0,8},{8,16},{16,24},{24,0},{1,9},{9,17},{17,25},{25,1},{2,10},{10... | collective-permute-start | bytes 2696 | tf_op jit(solution)/shard_map/ppermute | solution.py:331
  21.7 17.0 %collective-permute-start.2 = (s32[16,14]{1,0:T(8,128)S(1)}, s32[16,14]{1,0:T(8,128)S(1)}, u32[]{:S(2)}, u32[]{:S(2)}) collective-permute-start(s32[16,14]{1,0:T(8,128)S(1)} %copy-done.1), channel_id=1, source_target_pairs={{0,24},{8,0},{16,8},{24,16},{1,25},{9,1},{17,9},{25,17},{2,26},{10... | collective-permute-start | bytes 2696 | tf_op jit(solution)/shard_map/ppermute | solution.py:331
  26.1 12.7 %collective-permute-start.3 = (s32[4]{0:T(128)S(1)}, s32[4]{0:T(128)S(1)}, u32[]{:S(2)}, u32[]{:S(2)}) collective-permute-start(s32[4]{0:T(128)S(1)} %slice_bitcast_fusion), channel_id=1, source_target_pairs={{32,0},{64,32},{96,64},{128,96},{160,128},{192,160},{224,192},{256... | collective-permute-start | bytes 56 | tf_op jit(solution)/shard_map/ppermute | solution.py:335
  42.5 53.9 %collective-permute-start.7 = (bf16[64,128,128]{2,1,0:T(8,128)(2,1)S(1)}, bf16[64,128,128]{2,1,0:T(8,128)(2,1)}, u32[]{:S(2)}, u32[]{:S(2)}) collective-permute-start(bf16[64,128,128]{2,1,0:T(8,128)(2,1)S(1)} %bitcast.42), channel_id=1, source_target_pairs={{0,1},{1,0},{2,3},{3,2},{4,5},{5,4},{6,7},{7,6},{8,9},{9,8},{10,11... | collective-permute-start | bytes 6291464 | tf_op jit(solution)/shard_map/ppermute | solution.py:301
  49.5 46.9 %all-to-all-start.1 = ((bf16[32,128,128]{2,1,0:T(8,128)(2,1)}), bf16[32,128,128]{2,1,0:T(8,128)(2,1)S(1)}, u32[]{:S(2)}, u32[]{:S(2)}) async-start(bf16[32,128,128]{2,1,0:T(8,128)(2,1)} %bitcast.48), calls=%async_computation.1 | async-start | bytes 2097152 | tf_op jit(solution)/shard_map/all_to_all | solution.py:341
  54.1 14.6 %collective-permute-start.11 = (bf16[16,128,128]{2,1,0:T(8,128)(2,1)}, bf16[16,128,128]{2,1,0:T(8,128)(2,1)}, u32[]{:S(2)}, u32[]{:S(2)}) collective-permute-start(bf16[16,128,128]{2,1,0:T(8,128)(2,1)} %slice.7), channel_id=1, source_target_pairs={{0,32},{32,64},{64,96},{96,128},{128,160},{160,192},{192,224},{224... | collective-permute-start | bytes 1572872 | tf_op jit(solution)/shard_map/ppermute | solution.py:354
  57.8 13.8 %collective-permute-start.4 = (bf16[128,128]{1,0:T(8,128)(2,1)S(1)}, bf16[128,128]{1,0:T(8,128)(2,1)S(1)}, u32[]{:S(2)}, u32[]{:S(2)}) collective-permute-start(bf16[128,128]{1,0:T(8,128)(2,1)S(1)} %get-tuple-element.38), channel_id=1, source_target_pairs={{0,32},{32,64},{64,96},{96,0},{128,160},{160,192},{192,224},{224,1... | collective-permute-start | bytes 98312 | tf_op jit(solution)/shard_map/ppermute | solution.py:352
  60.6 11.1 %collective-permute-start.5 = (bf16[128,128]{1,0:T(8,128)(2,1)S(1)}, bf16[128,128]{1,0:T(8,128)(2,1)S(1)}, u32[]{:S(2)}, u32[]{:S(2)}) collective-permute-start(bf16[128,128]{1,0:T(8,128)(2,1)S(1)} %get-tuple-element.39), channel_id=1, source_target_pairs={{0,64},{32,96},{64,0},{96,32},{128,192},{160,224},{192,128},{224,1... | collective-permute-start | bytes 98312 | tf_op jit(solution)/shard_map/ppermute | solution.py:352
  66.7 4.9 %collective-permute-start.6 = (bf16[128,128]{1,0:T(8,128)(2,1)S(1)}, bf16[128,128]{1,0:T(8,128)(2,1)S(1)}, u32[]{:S(2)}, u32[]{:S(2)}) collective-permute-start(bf16[128,128]{1,0:T(8,128)(2,1)S(1)} %get-tuple-element.40), channel_id=1, source_target_pairs={{0,96},{32,0},{64,32},{96,64},{128,224},{160,128},{192,160},{224,1... | collective-permute-start | bytes 98312 | tf_op jit(solution)/shard_map/ppermute | solution.py:352
  68.6 45.5 %collective-permute-start.12 = (bf16[16,128,128]{2,1,0:T(8,128)(2,1)}, bf16[16,128,128]{2,1,0:T(8,128)(2,1)}, u32[]{:S(2)}, u32[]{:S(2)}) collective-permute-start(bf16[16,128,128]{2,1,0:T(8,128)(2,1)} %collective-permute-done.11.refs_0_), channel_id=1, source_target_pairs={{0,1},{1,0},{2,3},{3,2},{4,5},{5,4},{6,7},{7,6},{8,9},{9,8},{10,11... | collective-permute-start | bytes 1572872 | tf_op jit(solution)/shard_map/ppermute | solution.py:301
  71.7 34.5 %collective-permute-start.10 = (bf16[128,128]{1,0:T(8,128)(2,1)S(1)}, bf16[128,128]{1,0:T(8,128)(2,1)S(1)}, u32[]{:S(2)}, u32[]{:S(2)}) collective-permute-start(bf16[128,128]{1,0:T(8,128)(2,1)S(1)} %add_convert_fusion.1), channel_id=1, source_target_pairs={{0,384},{32,416},{64,448},{96,480},{128,0},{160,32},{192,64},{224,... | collective-permute-start | bytes 98312 | tf_op jit(solution)/shard_map/ppermute | solution.py:358
  84.2 21.9 %collective-permute-start.9 = (bf16[128,128]{1,0:T(8,128)(2,1)S(1)}, bf16[128,128]{1,0:T(8,128)(2,1)S(1)}, u32[]{:S(2)}, u32[]{:S(2)}) collective-permute-start(bf16[128,128]{1,0:T(8,128)(2,1)S(1)} %add_convert_fusion.1), channel_id=1, source_target_pairs={{0,256},{32,288},{64,320},{96,352},{128,384},{160,416},{192,448},{... | collective-permute-start | bytes 98312 | tf_op jit(solution)/shard_map/ppermute | solution.py:358
  89.1 17.0 %collective-permute-start.8 = (bf16[128,128]{1,0:T(8,128)(2,1)S(1)}, bf16[128,128]{1,0:T(8,128)(2,1)S(1)}, u32[]{:S(2)}, u32[]{:S(2)}) collective-permute-start(bf16[128,128]{1,0:T(8,128)(2,1)S(1)} %add_convert_fusion.1), channel_id=1, source_target_pairs={{0,128},{32,160},{64,192},{96,224},{128,256},{160,288},{192,320},{... | collective-permute-start | bytes 98312 | tf_op jit(solution)/shard_map/ppermute | solution.py:358
  106.2 18.0 %collective-permute-start.15 = (bf16[128,128]{1,0:T(8,128)(2,1)S(1)}, bf16[128,128]{1,0:T(8,128)(2,1)S(1)}, u32[]{:S(2)}, u32[]{:S(2)}) collective-permute-start(bf16[128,128]{1,0:T(8,128)(2,1)S(1)} %add_convert_fusion), channel_id=1, source_target_pairs={{0,96},{32,0},{64,32},{96,64},{128,224},{160,128},{192,160},{224,1... | collective-permute-start | bytes 98312 | tf_op jit(solution)/shard_map/ppermute | solution.py:363
  108.9 15.3 %collective-permute-start.14 = (bf16[128,128]{1,0:T(8,128)(2,1)S(1)}, bf16[128,128]{1,0:T(8,128)(2,1)S(1)}, u32[]{:S(2)}, u32[]{:S(2)}) collective-permute-start(bf16[128,128]{1,0:T(8,128)(2,1)S(1)} %add_convert_fusion), channel_id=1, source_target_pairs={{0,64},{32,96},{64,0},{96,32},{128,192},{160,224},{192,128},{224,1... | collective-permute-start | bytes 98312 | tf_op jit(solution)/shard_map/ppermute | solution.py:363
  111.4 12.8 %collective-permute-start.13 = (bf16[128,128]{1,0:T(8,128)(2,1)S(1)}, bf16[128,128]{1,0:T(8,128)(2,1)S(1)}, u32[]{:S(2)}, u32[]{:S(2)}) collective-permute-start(bf16[128,128]{1,0:T(8,128)(2,1)S(1)} %add_convert_fusion), channel_id=1, source_target_pairs={{0,32},{32,64},{64,96},{96,0},{128,160},{160,192},{192,224},{224,1... | collective-permute-start | bytes 98312 | tf_op jit(solution)/shard_map/ppermute | solution.py:363
  124.3 4.5 %collective-permute-start.16 = (bf16[4,128,128]{2,1,0:T(8,128)(2,1)S(1)}, bf16[4,128,128]{2,1,0:T(8,128)(2,1)S(1)}, u32[]{:S(2)}, u32[]{:S(2)}) collective-permute-start(bf16[4,128,128]{2,1,0:T(8,128)(2,1)S(1)} %pad_maximum_fusion.1.own), channel_id=1, source_target_pairs={{0,1},{1,0},{2,3},{3,2},{4,5},{5,4},{6,7},{7,6},{8,9},{9,8},{10,11... | collective-permute-start | bytes 393224 | tf_op jit(solution)/shard_map/ppermute | solution.py:301

commit v3 on v1

--- a/solution.py
+++ b/solution.py
@@ -22,24 +22,41 @@
 PLANE_AXES = ("y", "x", "core")
 
 
-def pick_kernel(ids, first, kinds, out):
+def row_of(where, row):
+    return (where[2] + 4 - row // WIN) % 4, row % WIN
+
+
+def pick_kernel(where, rows, above, kinds, out, buffer, sems):
+    group, last = row_of(where, PLANE - 1)
+    copies, present = [], []
     for slot in range(GLOBALS):
-        place = ids[slot] - first[0]
+        place = jnp.maximum(rows[group, last, WSEL + slot], above[slot]) - where[1]
         held = (place >= 0) & (place < PLANE)
-        block = kinds[jnp.where(held, place, 0)]
-        out[slot] = jnp.where(held, block, jnp.zeros_like(block))
-
-
-def pick_globals(ids, first, kinds):
+        source = kinds.at[jnp.where(held, place, 0)]
+        copies.append(pltpu.make_async_copy(source, buffer.at[slot], sems.at[slot]))
+        present.append(held)
+    for copy in copies:
+        copy.start()
+    for slot in range(GLOBALS):
+        copies[slot].wait()
+        block = buffer[slot].astype(jnp.float32)
+        out[slot] = jnp.where(present[slot], block, jnp.zeros_like(block))
+
+
+def pick_globals(where, rows, above, kinds):
     scalars = pl.BlockSpec(memory_space=pltpu.SMEM)
-    whole = pl.BlockSpec(memory_space=pltpu.VMEM)
     return pl.pallas_call(
         pick_kernel,
-        out_shape=jax.ShapeDtypeStruct((GLOBALS, BLOCK, HEAD_DIM), jnp.bfloat16),
-        in_specs=[scalars, scalars, whole],
-        out_specs=whole,
+        out_shape=jax.ShapeDtypeStruct((GLOBALS, BLOCK, HEAD_DIM), jnp.float32),
+        in_specs=[scalars, scalars, scalars, pl.BlockSpec(memory_space=pl.ANY)],
+        out_specs=pl.BlockSpec(memory_space=pltpu.VMEM),
+        scratch_shapes=[
+            pltpu.VMEM((GLOBALS, BLOCK, HEAD_DIM), jnp.bfloat16),
+            pltpu.SemaphoreType.DMA((GLOBALS,)),
+        ],
+        compiler_params=pltpu.CompilerParams(vmem_limit_bytes=20 << 20),
         name="pick_globals",
-    )(ids, first, kinds)
+    )(where, rows, above, kinds)
 
 
 def attend_kernel(
@@ -80,11 +97,11 @@
     )
 
     def attend_block(at, lane):
-        row = 2 * at + core
+        group, row = row_of(where, 2 * at + core)
         block_query = query[at]
         places, listed = [], []
         for slot in range(SLOTS):
-            block_id = rows[row, slot]
+            block_id = rows[group, row, slot]
             if slot < WSEL:
                 offset = block_id - first
                 place = jnp.where(offset >= 0, offset, offset + PLANE + WIN)
@@ -149,7 +166,7 @@
             pltpu.VMEM((UNROLL, BLOCK, SLOTS * BLOCK), jnp.bfloat16),
             pltpu.SemaphoreType.DMA((6,)),
         ],
-        compiler_params=pltpu.CompilerParams(vmem_limit_bytes=40 << 20),
+        compiler_params=pltpu.CompilerParams(vmem_limit_bytes=24 << 20),
         cost_estimate=pl.CostEstimate(
             flops=4 * pairs * HEAD_DIM, bytes_accessed=8 << 20, transcendentals=pairs
         ),
@@ -166,8 +183,9 @@
     breadth = lax.axis_size("y")
     up = [(at, at + 1) for at in range(depth - 1)]
     down = [(at + 1, at) for at in range(depth - 1)]
-    core = lax.axis_index("core")
-    first = lax.axis_index("z") * PLANE
+    where = jnp.stack(
+        [lax.axis_index("core"), lax.axis_index("z") * PLANE, lax.axis_index("y")]
+    )
 
     tokens = queries.shape[0]
     kinds = jnp.stack(
@@ -179,14 +197,15 @@
     ).reshape(2 * HEADS, tokens, HEAD_DIM)
     own = lax.all_to_all(kinds, PLANE_AXES, 0, 0, tiled=True).reshape(PLANE, BLOCK, HEAD_DIM)
 
-    turned = [key_blocks] + [
-        lax.ppermute(key_blocks, "y", [(at, (at + step) % breadth) for at in range(breadth)])
-        for step in range(1, breadth)
-    ]
-    here = lax.axis_index("y")
-    rows = jnp.stack(turned)[(here - jnp.arange(breadth)) % breadth].reshape(PLANE, SLOTS)
+    rows = jnp.stack(
+        [key_blocks]
+        + [
+            lax.ppermute(key_blocks, "y", [(at, (at + step) % breadth) for at in range(breadth)])
+            for step in range(1, breadth)
+        ]
+    )
     above = lax.ppermute(key_blocks[-1, WSEL:], "z", down)
-    ids = jnp.maximum(rows[-1, WSEL:], above)
+    own, rows, above = lax.optimization_barrier((own, rows, above))
 
     query = lax.all_to_all(
         jnp.transpose(
@@ -197,19 +216,15 @@
 
     other = swapped(own)
     halo_own = lax.ppermute(own[PLANE - WIN :], "z", up)
+
+    part = pick_globals(where, rows, above, own)
+    global_own = lax.psum(part, "z").astype(jnp.bfloat16)
+    halo_own, global_own = lax.optimization_barrier((halo_own, global_own))
+    global_other = swapped(global_own)
     halo_other = swapped(halo_own)
 
-    part = pick_globals(ids, first[None], own).reshape(depth, -1, HEAD_DIM)
-    pieces = lax.all_to_all(part, "z", 0, 0, tiled=True)
-    summed = jnp.sum(pieces.astype(jnp.float32), axis=0, keepdims=True).astype(jnp.bfloat16)
-    global_own = lax.all_to_all(
-        jnp.broadcast_to(summed, part.shape), "z", 0, 0, tiled=True
-    ).reshape(GLOBALS, BLOCK, HEAD_DIM)
-    global_other = swapped(global_own)
-
     context = attend(
-        jnp.stack([core, first]), rows, query,
-        own, other, halo_own, halo_other, global_own, global_other,
+        where, rows, query, own, other, halo_own, halo_other, global_own, global_other
     )
     back = lax.all_to_all(context, PLANE_AXES, 0, 0, tiled=True)
     return jnp.transpose(

time: 164 us -> 175 us (1.067)
  blocking collectives: 45.3 us -> 74.1 us
  waiting for transfers between devices: 32 us -> 16.7 us
    psum x0 -> x1, blocking collectives: none -> 51.5 us  [shards(): global_own = lax.psum(part, 'z').astype(jnp.bfloat16)]
    all_to_all x1 -> x0, blocking collectives: 24.7 us -> none  [shards(): pieces = lax.all_to_all(part, 'z', 0, 0, tiled=True)]
    all_to_all x1, waiting for transfers between devices: 12.8 us -> 0.01 us  [shards(): lax.all_to_all(jnp.transpose(queries.reshape(2, BLOCK, HEADS, HEAD_DIM),...]
    ppermute x3, starting transfers between devices: 8.62 us -> 20.8 us  [swapped(): return lax.ppermute(value, 'core', [(0, 1), (1, 0)])]
    all_to_all x1 -> x0, starting transfers between devices: 6.15 us -> none  [shards(): lax.all_to_all(jnp.broadcast_to(summed, part.shape), 'z', 0, 0, tiled=True)]
    all_to_all x1 -> x0, waiting for transfers between devices: 4.58 us -> none  [shards(): lax.all_to_all(jnp.broadcast_to(summed, part.shape), 'z', 0, 0, tiled=True)]
    all_to_all x1, starting transfers between devices: 7.28 us -> 3.88 us  [shards(): lax.all_to_all(jnp.transpose(queries.reshape(2, BLOCK, HEADS, HEAD_DIM),...]
    all_to_all x1, blocking collectives: 20.6 us -> 22.6 us  [shards(): back = lax.all_to_all(context, PLANE_AXES, 0, 0, tiled=True)]
  transfers between devices with their start and end apart: 11 -> 10, of which waited for: 4 -> 3; matrix products, arithmetic and copies ran while one was open for 3% -> 1% of each run, Pallas kernels for 1% -> 1%
where the time goes in v3:
time: 175 us; the launch traced here: 174 us
  blocking collectives  74.1 us (42%)
  starting transfers between devices  50.3 us (29%)
  Pallas kernels  23.6 us (13%)
  waiting for transfers between devices  16.7 us (10%)
  local copies, waits for them, and re-layouts  8.87 us (5%)
    psum x1, blocking collectives, shards(): global_own = lax.psum(part, 'z').astype(jnp.bfloat16)  51.5 us
    all_to_all x1, blocking collectives, shards(): back = lax.all_to_all(context, PLANE_AXES, 0, 0, tiled=True)  22.6 us
    pallas_call x1, Pallas kernels, attend(): pl.pallas_call(attend_kernel, out_shape=jax.ShapeDtypeStruct(query.shape,...  22.2 us
    ppermute x3, starting transfers between devices, swapped(): return lax.ppermute(value, 'core', [(0, 1), (1, 0)])  20.8 us
    ppermute x3, waiting for transfers between devices, shards(): lax.ppermute(key_blocks, 'y', [(at, (at + step) % breadth) for at in rang...  11.4 us
    ppermute x3, starting transfers between devices, shards(): lax.ppermute(key_blocks, 'y', [(at, (at + step) % breadth) for at in rang...  11.4 us
    all_to_all x1, starting transfers between devices, shards(): lax.all_to_all(kinds, PLANE_AXES, 0, 0, tiled=True)  10.7 us
    unnamed x12, local copies, waits for them, and re-layouts  4.15 us
  transfers between devices with their start and end apart: 10, of which 3 were waited for; matrix products, arithmetic and copies ran while one was open for 1% of the time, Pallas kernels for 1%

profile of v3, /device:TPU:1, one launch (start us, length us, event | category | flops | bytes accessed | tf_op | source)
XLA Modules:
  0.0 174.0 jit_solution(8854355490744270696)
XLA Ops:
  0.0 0.0 copy-start.1
  0.0 1.5 copy.8
  1.5 0.0 copy-done.1
  1.6 0.2 copy.9
  1.8 0.2 pad_maximum_fusion
  2.0 1.9 %copy.5 = bf16[16,2,256,128]{3,2,1,0:T(8,128)(2,1)} copy(bf16[16,2,256,128]{3,0,2,1:T(8,128)(2,1)S(1)} %pad_maximum_fusion) | data formatting | bytes 4194304 | tf_op jit(solution)/shard_map/stack | solution.py:191
  3.9 0.0 copy-start.3
  3.9 0.0 copy-start.2
  3.9 10.7 %all-to-all-start = ((bf16[32,256,128]{2,1,0:T(8,128)(2,1)}), bf16[32,256,128]{2,1,0:T(8,128)(2,1)S(1)}, u32[]{:S(2)}, u32[]{:S(2)}) async-start(bf16[32,256,128]{2,1,0:T(8,128)(2,1)} %bitcast.41), calls=%async_computation | async-start | bytes 4194304 | tf_op jit(solution)/shard_map/all_to_all | solution.py:198
  14.5 0.0 copy-done.3
  14.6 4.9 %collective-permute-start.1 = (s32[16,14]{1,0:T(8,128)S(1)}, s32[16,14]{1,0:T(8,128)S(1)}, u32[]{:S(2)}, u32[]{:S(2)}) collective-permute-start(s32[16,14]{1,0:T(8,128)S(1)} %copy-done.3), channel_id=1, source_target_pairs={{0,16},{8,24},{16,0},{24,8},{1,17},{9,25},{17,1},{25,9},{2,18},{10... | collective-permute-start | bytes 2696 | tf_op jit(solution)/shard_map/ppermute | solution.py:203
  19.5 2.2 %collective-permute-start = (s32[16,14]{1,0:T(8,128)S(1)}, s32[16,14]{1,0:T(8,128)S(1)}, u32[]{:S(2)}, u32[]{:S(2)}) collective-permute-start(s32[16,14]{1,0:T(8,128)S(1)} %copy-done.3), channel_id=1, source_target_pairs={{0,8},{8,16},{16,24},{24,0},{1,9},{9,17},{17,25},{25,1},{2,10},{10... | collective-permute-start | bytes 2696 | tf_op jit(solution)/shard_map/ppermute | solution.py:203
  21.7 4.2 %collective-permute-start.2 = (s32[16,14]{1,0:T(8,128)S(1)}, s32[16,14]{1,0:T(8,128)S(1)}, u32[]{:S(2)}, u32[]{:S(2)}) collective-permute-start(s32[16,14]{1,0:T(8,128)S(1)} %copy-done.3), channel_id=1, source_target_pairs={{0,24},{8,0},{16,8},{24,16},{1,25},{9,1},{17,9},{25,17},{2,26},{10... | collective-permute-start | bytes 2696 | tf_op jit(solution)/shard_map/ppermute | solution.py:203
  26.0 0.1 slice_bitcast_fusion
  26.0 1.3 collective-permute-start.3
  27.3 11.4 %collective-permute-done.1 = s32[16,14]{1,0:T(8,128)S(1)} collective-permute-done((s32[16,14]{1,0:T(8,128)S(1)}, s32[16,14]{1,0:T(8,128)S(1)}, u32[]{:S(2)}, u32[]{:S(2)}) %collective-permute-start.1) | collective-permute-done | bytes 928 | tf_op jit(solution)/shard_map/ppermute | solution.py:203
  38.8 0.0 collective-permute-done
  38.8 0.0 collective-permute-done.2
  38.8 0.0 collective-permute-done.3.above
  38.8 3.7 %all-to-all-done = bf16[32,256,128]{2,1,0:T(8,128)(2,1)S(1)} async-done(((bf16[32,256,128]{2,1,0:T(8,128)(2,1)}), bf16[32,256,128]{2,1,0:T(8,128)(2,1)S(1)}, u32[]{:S(2)}, u32[]{:S(2)}) %all-to-all-start) | async-done | bytes 2097184 | tf_op jit(solution)/shard_map/all_to_all | solution.py:198
  42.5 4.3 %collective-permute-start.4 = (bf16[64,128,128]{2,1,0:T(8,128)(2,1)S(1)}, bf16[64,128,128]{2,1,0:T(8,128)(2,1)}, u32[]{:S(2)}, u32[]{:S(2)}) collective-permute-start(bf16[64,128,128]{2,1,0:T(8,128)(2,1)S(1)} %bitcast.37), channel_id=1, source_target_pairs={{0,1},{1,0},{2,3},{3,2},{4,5},{5,4},{6,7},{7,6},{8,9},{9,8},{10,11... | collective-permute-start | bytes 6291464 | tf_op jit(solution)/shard_map/ppermute | solution.py:178
  46.8 0.9 slice.7
  47.6 2.3 %collective-permute-start.5 = (bf16[16,128,128]{2,1,0:T(8,128)(2,1)}, bf16[16,128,128]{2,1,0:T(8,128)(2,1)}, u32[]{:S(2)}, u32[]{:S(2)}) collective-permute-start(bf16[16,128,128]{2,1,0:T(8,128)(2,1)} %slice.7), channel_id=1, source_target_pairs={{0,32},{32,64},{64,96},{96,128},{128,160},{160,192},{192,224},{224... | collective-permute-start | bytes 1572872 | tf_op jit(solution)/shard_map/ppermute | solution.py:218
  49.9 0.0 copy-done.2
  49.9 0.2 copy.10
  50.2 1.2 copy.6
  51.4 3.9 %all-to-all-start.1 = ((bf16[32,128,128]{2,1,0:T(8,128)(2,1)}), bf16[32,128,128]{2,1,0:T(8,128)(2,1)S(1)}, u32[]{:S(2)}, u32[]{:S(2)}) async-start(bf16[32,128,128]{2,1,0:T(8,128)(2,1)} %bitcast.42), calls=%async_computation.1 | async-start | bytes 2097152 | tf_op jit(solution)/shard_map/all_to_all | solution.py:210
  55.3 0.1 pad_add_fusion.1.where
  55.4 1.3 pick_globals.1
  56.7 51.5 %all-reduce.1.global_own = bf16[4,128,128]{2,1,0:T(8,128)(2,1)} all-reduce(f32[4,128,128]{2,1,0:T(8,128)S(1)} %pick_globals.1), channel_id=1, replica_groups=mesh['z'=16,'y'=4,'x'=4,'core'=2] {'z'}, use_global_device_ids=true, to_apply=%region_0.0 | all-reduce | flops 65536 | bytes 393216 | tf_op jit(solution)/shard_map/psum | solution.py:221
  108.3 0.0 collective-permute-done.5.halo_own
  108.3 14.6 %collective-permute-start.6 = (bf16[16,128,128]{2,1,0:T(8,128)(2,1)}, bf16[16,128,128]{2,1,0:T(8,128)(2,1)}, u32[]{:S(2)}, u32[]{:S(2)}) collective-permute-start(bf16[16,128,128]{2,1,0:T(8,128)(2,1)} %collective-permute-done.5.halo_own), channel_id=1, source_target_pairs={{0,1},{1,0},{2,3},{3,2},{4,5},{5,4},{6,7},{7,6},{8,9},{9,8},{10,11... | collective-permute-start | bytes 1572872 | tf_op jit(solution)/shard_map/ppermute | solution.py:178
  122.9 1.9 %collective-permute-start.7 = (bf16[4,128,128]{2,1,0:T(8,128)(2,1)}, bf16[4,128,128]{2,1,0:T(8,128)(2,1)S(1)}, u32[]{:S(2)}, u32[]{:S(2)}) collective-permute-start(bf16[4,128,128]{2,1,0:T(8,128)(2,1)} %all-reduce.1.global_own), channel_id=1, source_target_pairs={{0,1},{1,0},{2,3},{3,2},{4,5},{5,4},{6,7},{7,6},{8,9},{9,8},{10,11... | collective-permute-start | bytes 393224 | tf_op jit(solution)/shard_map/ppermute | solution.py:178
  124.8 0.0 all-to-all-done.1.query
  124.8 1.5 collective-permute-done.7.global_other
  126.3 0.0 collective-permute-done.6.halo_other
  126.3 0.0 collective-permute-done.4.other
  126.3 0.0 copy-start
  126.3 0.9 copy-done
  127.2 22.2 %attend.1 = bf16[32,128,128]{2,1,0:T(8,128)(2,1)S(1)} custom-call(s32[3]{0:T(128)S(1)} %pad_add_fusion.1.where, s32[4,16,14]{2,1,0:T(8,128)S(1)} %pad_add_fusion.rows, bf16[32,128,128]{2,1,0:T(8,128)(2,1)S(1)} %all-to-all-done.1.query, bf16[64,128,128]{2,1,0:T(8,128)(2,1)S(1)} %bitcast.40, bf16[64,128,128]{2,1,0:T(8,128)(2,1)} %collective-permute-done.4.other, ...), custom_call_target="tpu_custom_call" | custom-call | flops 3758096384 | bytes 8388608 | tf_op jit(solution)/shard_map/attend/pallas_call | solution.py:157
  149.5 22.6 %all_to_all.15 = bf16[32,128,128]{2,1,0:T(8,128)(2,1)S(1)} all-to-all(bf16[32,128,128]{2,1,0:T(8,128)(2,1)S(1)} %attend.1), channel_id=1, replica_groups=mesh['z'=16,'y'=4,'x'=4,'core'=2] {'y','x','core'}, dimensions={0} | all-to-all | bytes 2097152 | tf_op jit(solution)/shard_map/all_to_all | solution.py:229
  172.1 0.7 copy.7
  172.8 1.2 copy.13
  (1 shorter events, 0.0 us)
Async XLA Ops:
  0.0 1.5 copy-start.1
  3.9 10.7 %copy-start.3 = (s32[16,14]{1,0:T(8,128)S(1)}, s32[16,14]{1,0:T(8,128)}, u32[]{:S(2)}) copy-start(s32[16,14]{1,0:T(8,128)} %param.7) | copy-start | bytes 2692
  3.9 46.1 %copy-start.2 = (bf16[256,2048]{1,0:T(8,128)(2,1)S(1)}, bf16[256,2048]{1,0:T(8,128)(2,1)}, u32[]{:S(2)}) copy-start(bf16[256,2048]{1,0:T(8,128)(2,1)} %param.4) | copy-start | bytes 3145732
  3.9 38.6 %all-to-all-start = ((bf16[32,256,128]{2,1,0:T(8,128)(2,1)}), bf16[32,256,128]{2,1,0:T(8,128)(2,1)S(1)}, u32[]{:S(2)}, u32[]{:S(2)}) async-start(bf16[32,256,128]{2,1,0:T(8,128)(2,1)} %bitcast.41), calls=%async_computation | async-start | bytes 4194304 | tf_op jit(solution)/shard_map/all_to_all | solution.py:198
  14.6 24.2 %collective-permute-start.1 = (s32[16,14]{1,0:T(8,128)S(1)}, s32[16,14]{1,0:T(8,128)S(1)}, u32[]{:S(2)}, u32[]{:S(2)}) collective-permute-start(s32[16,14]{1,0:T(8,128)S(1)} %copy-done.3), channel_id=1, source_target_pairs={{0,16},{8,24},{16,0},{24,8},{1,17},{9,25},{17,1},{25,9},{2,18},{10... | collective-permute-start | bytes 2696 | tf_op jit(solution)/shard_map/ppermute | solution.py:203
  19.5 19.3 %collective-permute-start = (s32[16,14]{1,0:T(8,128)S(1)}, s32[16,14]{1,0:T(8,128)S(1)}, u32[]{:S(2)}, u32[]{:S(2)}) collective-permute-start(s32[16,14]{1,0:T(8,128)S(1)} %copy-done.3), channel_id=1, source_target_pairs={{0,8},{8,16},{16,24},{24,0},{1,9},{9,17},{17,25},{25,1},{2,10},{10... | collective-permute-start | bytes 2696 | tf_op jit(solution)/shard_map/ppermute | solution.py:203
  21.7 17.0 %collective-permute-start.2 = (s32[16,14]{1,0:T(8,128)S(1)}, s32[16,14]{1,0:T(8,128)S(1)}, u32[]{:S(2)}, u32[]{:S(2)}) collective-permute-start(s32[16,14]{1,0:T(8,128)S(1)} %copy-done.3), channel_id=1, source_target_pairs={{0,24},{8,0},{16,8},{24,16},{1,25},{9,1},{17,9},{25,17},{2,26},{10... | collective-permute-start | bytes 2696 | tf_op jit(solution)/shard_map/ppermute | solution.py:203
  26.0 12.7 %collective-permute-start.3 = (s32[4]{0:T(128)S(1)}, s32[4]{0:T(128)S(1)}, u32[]{:S(2)}, u32[]{:S(2)}) collective-permute-start(s32[4]{0:T(128)S(1)} %slice_bitcast_fusion), channel_id=1, source_target_pairs={{32,0},{64,32},{96,64},{128,96},{160,128},{192,160},{224,192},{256... | collective-permute-start | bytes 56 | tf_op jit(solution)/shard_map/ppermute | solution.py:207
  42.5 83.8 %collective-permute-start.4 = (bf16[64,128,128]{2,1,0:T(8,128)(2,1)S(1)}, bf16[64,128,128]{2,1,0:T(8,128)(2,1)}, u32[]{:S(2)}, u32[]{:S(2)}) collective-permute-start(bf16[64,128,128]{2,1,0:T(8,128)(2,1)S(1)} %bitcast.37), channel_id=1, source_target_pairs={{0,1},{1,0},{2,3},{3,2},{4,5},{5,4},{6,7},{7,6},{8,9},{9,8},{10,11... | collective-permute-start | bytes 6291464 | tf_op jit(solution)/shard_map/ppermute | solution.py:178
  47.6 60.6 %collective-permute-start.5 = (bf16[16,128,128]{2,1,0:T(8,128)(2,1)}, bf16[16,128,128]{2,1,0:T(8,128)(2,1)}, u32[]{:S(2)}, u32[]{:S(2)}) collective-permute-start(bf16[16,128,128]{2,1,0:T(8,128)(2,1)} %slice.7), channel_id=1, source_target_pairs={{0,32},{32,64},{64,96},{96,128},{128,160},{160,192},{192,224},{224... | collective-permute-start | bytes 1572872 | tf_op jit(solution)/shard_map/ppermute | solution.py:218
  51.4 73.4 %all-to-all-start.1 = ((bf16[32,128,128]{2,1,0:T(8,128)(2,1)}), bf16[32,128,128]{2,1,0:T(8,128)(2,1)S(1)}, u32[]{:S(2)}, u32[]{:S(2)}) async-start(bf16[32,128,128]{2,1,0:T(8,128)(2,1)} %bitcast.42), calls=%async_computation.1 | async-start | bytes 2097152 | tf_op jit(solution)/shard_map/all_to_all | solution.py:210
  108.3 18.1 %collective-permute-start.6 = (bf16[16,128,128]{2,1,0:T(8,128)(2,1)}, bf16[16,128,128]{2,1,0:T(8,128)(2,1)}, u32[]{:S(2)}, u32[]{:S(2)}) collective-permute-start(bf16[16,128,128]{2,1,0:T(8,128)(2,1)} %collective-permute-done.5.halo_own), channel_id=1, source_target_pairs={{0,1},{1,0},{2,3},{3,2},{4,5},{5,4},{6,7},{7,6},{8,9},{9,8},{10,11... | collective-permute-start | bytes 1572872 | tf_op jit(solution)/shard_map/ppermute | solution.py:178
  122.9 3.5 %collective-permute-start.7 = (bf16[4,128,128]{2,1,0:T(8,128)(2,1)}, bf16[4,128,128]{2,1,0:T(8,128)(2,1)S(1)}, u32[]{:S(2)}, u32[]{:S(2)}) collective-permute-start(bf16[4,128,128]{2,1,0:T(8,128)(2,1)} %all-reduce.1.global_own), channel_id=1, source_target_pairs={{0,1},{1,0},{2,3},{3,2},{4,5},{5,4},{6,7},{7,6},{8,9},{9,8},{10,11... | collective-permute-start | bytes 393224 | tf_op jit(solution)/shard_map/ppermute | solution.py:178
  126.3 0.9 copy-start

commit v4 on v2

v4 whole, which is shorter than its diff:
```python
import functools
import math

import jax
import jax.numpy as jnp
from jax import lax
from jax.experimental import pallas as pl
from jax.experimental.pallas import tpu as pltpu
from jax.sharding import Mesh
from jax.sharding import PartitionSpec as P

HEAD_DIM = 128
BLOCK = 128
WIN = 16
WSEL = 10
GLOBALS = 4
SLOTS = WSEL + GLOBALS
HEADS = 16
PLANE = 64
CHUNK = 16
FACTOR = math.log2(math.e) / math.sqrt(HEAD_DIM)
UNROLL = 4
MERGED = 8
PLANE_AXES = ("y", "x", "core")

SCALARS = pl.BlockSpec(memory_space=pltpu.SMEM)
WHOLE = pl.BlockSpec(memory_space=pltpu.VMEM)
LEFT = pl.BlockSpec(memory_space=pl.ANY)


def pack_kernel(queries, keys, values, out, query_buf, key_buf, value_buf, arrived, sems):
    def moves():
        for head in range(HEADS):
            columns = pl.ds(head * HEAD_DIM, HEAD_DIM)
            yield 0, key_buf.at[:, :, columns], out.at[2 * head, pl.ds(0, 2)]
            yield 1, value_buf.at[:, :, columns], out.at[2 * head + 1, pl.ds(0, 2)]
            yield 2, query_buf.at[0, :, columns], out.at[2 * head, 2]
            yield 2, query_buf.at[1, :, columns], out.at[2 * head + 1, 2]

    loads = [
        pltpu.make_async_copy(source, target, arrived.at[at])
        for at, (source, target) in enumerate(
            [(keys, key_buf), (values, value_buf), (queries, query_buf)]
        )
    ]
    stores = [
        (array, pltpu.make_async_copy(source, target, sems.at[at]))
        for at, (array, source, target) in enumerate(moves())
    ]
    for load in loads:
        load.start()
    for at, load in enumerate(loads):
        load.wait()
        for array, store in stores:
            if array == at:
                store.start()
    for _, store in stores:
        store.wait()


def pack(*arrays):
    arrays = [array.reshape(2, BLOCK, HEADS * HEAD_DIM) for array in arrays]
    return pl.pallas_call(
        pack_kernel,
        out_shape=jax.ShapeDtypeStruct((2 * HEADS, 3, BLOCK, HEAD_DIM), jnp.bfloat16),
        in_specs=[LEFT] * 3,
        out_specs=LEFT,
        scratch_shapes=[pltpu.VMEM(array.shape, array.dtype) for array in arrays]
        + [pltpu.SemaphoreType.DMA((3,)), pltpu.SemaphoreType.DMA((4 * HEADS,))],
        compiler_params=pltpu.CompilerParams(vmem_limit_bytes=56 << 20),
        name="pack",
    )(*arrays)


def pick_kernel(where, rows, above, kinds, out, buffer, sems):
    group, last = row_of(where, PLANE // 2 - 1, 1)
    copies, present = [], []
    for slot in range(GLOBALS):
        place = jnp.maximum(rows[group, last, WSEL + slot], above[slot]) - where[1]
        held = (place >= 0) & (place < PLANE)
        place = jnp.where(held, place, 0)
        source = kinds.at[place // 2, place % 2]
        copies.append(pltpu.make_async_copy(source, buffer.at[slot], sems.at[slot]))
        present.append(held)
    for copy in copies:
        copy.start()
    for slot in range(GLOBALS):
        copies[slot].wait()
        block = buffer[slot]
        out[slot] = jnp.where(present[slot], block, jnp.zeros_like(block))


def pick_globals(where, rows, above, kinds):
    return pl.pallas_call(
        pick_kernel,
        out_shape=jax.ShapeDtypeStruct((GLOBALS, BLOCK, HEAD_DIM), jnp.bfloat16),
        in_specs=[SCALARS, SCALARS, SCALARS, LEFT],
        out_specs=WHOLE,
        scratch_shapes=[
            pltpu.VMEM((GLOBALS, BLOCK, HEAD_DIM), jnp.bfloat16),
            pltpu.SemaphoreType.DMA((GLOBALS,)),
        ],
        compiler_params=pltpu.CompilerParams(vmem_limit_bytes=12 << 20),
        name="pick_globals",
    )(where, rows, above, kinds)


def row_of(where, at, core):
    row = 2 * at + core
    return (where[2] + 4 - row // CHUNK) % 4, row % CHUNK


def two_blocks(blocks, one, two):
    return jnp.concatenate([blocks[one // 2, one % 2], blocks[two // 2, two % 2]], axis=0)


def window_kernel(start, low, high, with_halo, where, rows, own, other, *refs):
    if with_halo:
        halo_own, halo_other, *refs = refs
    out, out_stats, keys, values, scores, weights, sems = refs
    core, first = where[0], where[1]
    count = out.shape[0]
    chunks = (high - low) // CHUNK

    def copies(own_to, other_to, at):
        if at < chunks:
            source = pl.ds((low + at * CHUNK) // 2, CHUNK // 2)
            target = pl.ds(at * CHUNK // 2, CHUNK // 2)
            for kind, (array, to) in enumerate([(own, own_to), (other, other_to)]):
                yield pltpu.make_async_copy(
                    array.at[source, pl.ds(0, 2)], to.at[target], sems.at[kind, at]
                )
        else:
            target = pl.ds(at * CHUNK // 2, WIN // 2)
            yield pltpu.make_async_copy(halo_own, own_to.at[target], sems.at[0, at])
            yield pltpu.make_async_copy(halo_other, other_to.at[target], sems.at[1, at])

    parts = list(range(chunks)) + ([chunks] if with_halo else [])

    @pl.when(core == 0)
    def _():
        for part in parts:
            for copy in copies(keys, values, part):
                copy.start()

    @pl.when(core != 0)
    def _():
        for part in parts:
            for copy in copies(values, keys, part):
                copy.start()

    needed = {}
    for part in parts:
        step = 0
        if part < chunks:
            step = max(0, (low + part * CHUNK - 2 * start) // (2 * UNROLL))
        needed.setdefault(step, []).append(part)

    causal = lax.broadcasted_iota(jnp.int32, (BLOCK, BLOCK), 0) >= lax.broadcasted_iota(
        jnp.int32, (BLOCK, BLOCK), 1
    )

    left = lax.broadcasted_iota(jnp.int32, (BLOCK, BLOCK), 1) < BLOCK // 2

    def attend_block(at, lane):
        group, row = row_of(where, start + at, core)
        block_query = own[start + at, 2]
        places, listed = [], []
        for slot in range(WSEL):
            block_id = rows[group, row, slot]
            place = block_id - first - low
            if with_halo:
                place = jnp.where(place >= 0, place, place + high + WIN)
            listed.append(block_id >= 0)
            places.append(jnp.where(block_id >= 0, place, 0))
        highest = None
        for slot in range(0, WSEL, 2):
            pair = two_blocks(keys, places[slot], places[slot + 1])
            both = lax.dot_general(
                block_query, pair, (((1,), (1,)), ((), ())), preferred_element_type=jnp.float32
            )
            for part in range(2):
                score = both[:, part * BLOCK : (part + 1) * BLOCK]
                if slot + part == 0:
                    score = jnp.where(causal, score, -1e30)
                elif with_halo:
                    score = jnp.where(listed[slot + part], score, -1e30)
                scores[lane, slot + part] = score
                highest = score if highest is None else jnp.maximum(highest, score)
        row_max = jnp.max(highest, axis=1, keepdims=True) * FACTOR
        row_max = jnp.broadcast_to(row_max, (BLOCK, BLOCK))
        total = None
        for slot in range(WSEL):
            weight = jnp.exp2(scores[lane, slot] * FACTOR - row_max)
            total = weight if total is None else total + weight
            weights[lane, :, slot * BLOCK : (slot + 1) * BLOCK] = weight.astype(jnp.bfloat16)
        row_sum = jnp.broadcast_to(jnp.sum(total, axis=1, keepdims=True), (BLOCK, BLOCK))
        out_stats[at] = jnp.where(left, row_max, row_sum)
        mixed = None
        for slot in range(0, WSEL, 2):
            pair = two_blocks(values, places[slot], places[slot + 1])
            term = jnp.dot(
                weights[lane, :, slot * BLOCK : (slot + 2) * BLOCK],
                pair,
                preferred_element_type=jnp.float32,
            )
            mixed = term if mixed is None else mixed + term
        out[at] = mixed

    def step(at, carry):
        for when, needs in needed.items():

            @pl.when(at == when)
            def _(needs=needs):
                for part in needs:
                    for copy in copies(keys, values, part):
                        copy.wait()

        for lane in range(UNROLL):
            attend_block(at * UNROLL + lane, lane)
        return carry

    lax.fori_loop(0, count // UNROLL, step, 0)


def attend_window(start, count, low, high, where, rows, own, other, *halo):
    span = high - low + (WIN if halo else 0)
    sums = jax.ShapeDtypeStruct((count, BLOCK, HEAD_DIM), jnp.float32)
    pairs = count * WSEL * BLOCK * BLOCK
    return pl.pallas_call(
        functools.partial(window_kernel, start, low, high, bool(halo)),
        out_shape=[sums] * 2,
        in_specs=[SCALARS, SCALARS, WHOLE] + [LEFT] * (1 + len(halo)),
        out_specs=[WHOLE] * 2,
        scratch_shapes=[
            pltpu.VMEM((span // 2, 2, BLOCK, HEAD_DIM), jnp.bfloat16),
            pltpu.VMEM((span // 2, 2, BLOCK, HEAD_DIM), jnp.bfloat16),
            pltpu.VMEM((UNROLL, WSEL, BLOCK, BLOCK), jnp.float32),
            pltpu.VMEM((UNROLL, BLOCK, WSEL * BLOCK), jnp.bfloat16),
            pltpu.SemaphoreType.DMA((2, span // CHUNK)),
        ],
        compiler_params=pltpu.CompilerParams(vmem_limit_bytes=12 << 20),
        cost_estimate=pl.CostEstimate(
            flops=4 * pairs * HEAD_DIM, bytes_accessed=8 << 20, transcendentals=pairs
        ),
        name="attend_near" if halo else "attend_far",
    )(where, rows, own, other, *halo)


def global_kernel(
    where, rows, own, other, query, near_sum, near_stats, far_sum, far_stats,
    out, keys, values, weights, sems,
):
    core, at = where[0], pl.program_id(0)

    @pl.when(at == 0)
    def _():
        def fill(own_to, other_to):
            copies = [
                pltpu.make_async_copy(own, own_to, sems.at[0]),
                pltpu.make_async_copy(other, other_to, sems.at[1]),
            ]
            for copy in copies:
                copy.start()
            for copy in copies:
                copy.wait()

        @pl.when(core == 0)
        def _():
            fill(keys, values)

        @pl.when(core != 0)
        def _():
            fill(values, keys)

    def merge(lane, sums, stats):
        group, row = row_of(where, at * MERGED + lane, core)
        block_query = query[lane, 0]
        held, highest = [], None
        for slot in range(0, GLOBALS, 2):
            pair = jnp.concatenate([keys[slot], keys[slot + 1]], axis=0)
            both = lax.dot_general(
                block_query, pair, (((1,), (1,)), ((), ())), preferred_element_type=jnp.float32
            )
            for part in range(2):
                score = both[:, part * BLOCK : (part + 1) * BLOCK]
                listed = rows[group, row, WSEL + slot + part] >= 0
                score = jnp.where(listed, score, -1e30)
                held.append(score)
                highest = score if highest is None else jnp.maximum(highest, score)
        window_max = stats[lane, :, :1]
        row_max = jnp.maximum(jnp.max(highest, axis=1, keepdims=True) * FACTOR, window_max)
        shrink = jnp.exp2(window_max - row_max)
        row_max = jnp.broadcast_to(row_max, (BLOCK, BLOCK))
        total = None
        for slot in range(GLOBALS):
            weight = jnp.exp2(held[slot] * FACTOR - row_max)
            total = weight if total is None else total + weight
            weights[lane, :, slot * BLOCK : (slot + 1) * BLOCK] = weight.astype(jnp.bfloat16)
        mixed = sums[lane] * shrink
        for slot in range(0, GLOBALS, 2):
            pair = jnp.concatenate([values[slot], values[slot + 1]], axis=0)
            mixed = mixed + jnp.dot(
                weights[lane, :, slot * BLOCK : (slot + 2) * BLOCK],
                pair,
                preferred_element_type=jnp.float32,
            )
        window_sum = stats[lane, :, BLOCK // 2 : BLOCK // 2 + 1]
        denom = jnp.sum(total, axis=1, keepdims=True) + window_sum * shrink
        out[lane] = (mixed / denom).astype(jnp.bfloat16)

    @pl.when(at < pl.num_programs(0) // 2)
    def _():
        for lane in range(MERGED):
            merge(lane, near_sum, near_stats)

    @pl.when(at >= pl.num_programs(0) // 2)
    def _():
        for lane in range(MERGED):
            merge(lane, far_sum, far_stats)


def attend_global(where, rows, received, own, other, near, far):
    count = received.shape[0]
    steps = count // MERGED
    pairs = count * GLOBALS * BLOCK * BLOCK
    tile = (MERGED, BLOCK, HEAD_DIM)
    of_near = pl.BlockSpec(tile, lambda at: (jnp.minimum(at, steps // 2 - 1), 0, 0))
    of_far = pl.BlockSpec(tile, lambda at: (jnp.maximum(at - steps // 2, 0), 0, 0))
    return pl.pallas_call(
        global_kernel,
        grid=(steps,),
        out_shape=jax.ShapeDtypeStruct((count, BLOCK, HEAD_DIM), jnp.bfloat16),
        in_specs=[SCALARS, SCALARS, LEFT, LEFT]
        + [pl.BlockSpec((MERGED, 1, BLOCK, HEAD_DIM), lambda at: (at, 2, 0, 0))]
        + [of_near, of_near, of_far, of_far],
        out_specs=pl.BlockSpec(tile, lambda at: (at, 0, 0)),
        scratch_shapes=[
            pltpu.VMEM((GLOBALS, BLOCK, HEAD_DIM), jnp.bfloat16),
            pltpu.VMEM((GLOBALS, BLOCK, HEAD_DIM), jnp.bfloat16),
            pltpu.VMEM((MERGED, BLOCK, GLOBALS * BLOCK), jnp.bfloat16),
            pltpu.SemaphoreType.DMA((2,)),
        ],
        compiler_params=pltpu.CompilerParams(vmem_limit_bytes=57 << 20),
        cost_estimate=pl.CostEstimate(
            flops=4 * pairs * HEAD_DIM, bytes_accessed=8 << 20, transcendentals=pairs
        ),
        name="attend_global",
    )(where, rows, own, other, received, *near, *far)


def swapped(value):
    return lax.ppermute(value, "core", [(0, 1), (1, 0)])


def shards(queries, key_vectors, value_vectors, key_blocks):
    depth = lax.axis_size("z")
    breadth = lax.axis_size("y")
    up = [(at, at + 1) for at in range(depth - 1)]
    down = [(at + 1, at) for at in range(depth - 1)]
    where = jnp.stack(
        [lax.axis_index("core"), lax.axis_index("z") * PLANE, lax.axis_index("y")]
    )

    received = lax.all_to_all(
        pack(queries, key_vectors, value_vectors), PLANE_AXES, 0, 0, tiled=True
    )

    rows = jnp.stack(
        [key_blocks]
        + [
            lax.ppermute(key_blocks, "y", [(at, (at + step) % breadth) for at in range(breadth)])
            for step in range(1, breadth)
        ]
    )
    above = lax.ppermute(key_blocks[-1, WSEL:], "z", down)
    own, rows, above = lax.optimization_barrier((received, rows, above))
    other = swapped(own)
    halo_own = lax.ppermute(own[-WIN // 2 :, :2], "z", up)

    half = PLANE // 4
    part = pick_globals(where, rows, above, own).reshape(depth, -1, HEAD_DIM)
    after, _ = lax.optimization_barrier((own, part))
    pieces = lax.all_to_all(part, "z", 0, 0, tiled=True)
    far = attend_window(half, half, CHUNK, PLANE, where, rows, after, other)
    far, pieces, halo_own = lax.optimization_barrier((far, pieces, halo_own))
    halo_other = swapped(halo_own)
    summed = jnp.sum(pieces.astype(jnp.float32), axis=0, keepdims=True).astype(jnp.bfloat16)
    spread = jnp.broadcast_to(summed, part.shape)
    after, _ = lax.optimization_barrier((own, spread))
    gathered = lax.all_to_all(spread, "z", 0, 0, tiled=True)
    near = attend_window(0, half, 0, 2 * half, where, rows, after, other, halo_own, halo_other)
    near, gathered = lax.optimization_barrier((near, gathered))
    global_own = gathered.reshape(GLOBALS, BLOCK, HEAD_DIM)
    global_other = swapped(global_own)
    context = attend_global(where, rows, own, global_own, global_other, near, far)
    back = lax.all_to_all(context, PLANE_AXES, 0, 0, tiled=True)
    return jnp.transpose(
        back.reshape(HEADS, 2, BLOCK, HEAD_DIM), (1, 2, 0, 3)
    ).reshape(queries.shape)


def solution(mesh):
    fine = Mesh(mesh.devices.reshape(-1, 4, 4, 2), ("z",) + PLANE_AXES)
    tokens = P(("z",) + PLANE_AXES, None)
    return jax.shard_map(
        shards,
        mesh=fine,
        in_specs=(tokens, tokens, tokens, P(("z", "y"), None)),
        out_specs=tokens,
        check_vma=False,
    )
```

time: 168 us -> 162 us (0.964)
  starting transfers between devices: 83.6 us -> 61.4 us
  waiting for transfers between devices: 16.1 us -> 27.4 us
  Pallas kernels: 32.8 us -> 42.5 us
  blocking collectives: 24.6 us -> 21.2 us
    ppermute x10 -> x1, starting transfers between devices: 45.7 us -> 2.27 us  [shards(): halo_own = lax.ppermute(own[-WIN // 2:, :2], 'z', up)]
    all_to_all x2 -> x3, starting transfers between devices: 14.4 us -> 33.1 us  [the longest x1 13.2 us: shards(): pieces = lax.all_to_all(part, 'z', 0, 0, tiled=True)]
    ppermute x3, waiting for transfers between devices: 11.4 us -> 22.9 us  [shards(): lax.ppermute(key_blocks, 'y', [(at, (at + step) % breadth) for at in rang...]
    pallas_call x2 -> x3, Pallas kernels: 13.1 us -> 21.8 us  [the longest x1 16.4 us: attend_global(): pl.pallas_call(global_kernel, grid=(steps,), out_shape=jax.ShapeDtypeStru...]
    all_to_all x1, blocking collectives: 24.6 us -> 21.2 us  [shards(): back = lax.all_to_all(context, PLANE_AXES, 0, 0, tiled=True)]
    ppermute x3, starting transfers between devices: 10.8 us -> 13.4 us  [swapped(): return lax.ppermute(value, 'core', [(0, 1), (1, 0)])]
    another operation x1 -> x0, local copies, waits for them, and re-layouts: 1.88 us -> none  [shards(): jnp.stack([jnp.swapaxes(array.reshape(tokens, HEADS, HEAD_DIM), 0, 1) for...]
    unnamed x8 -> x21, local copies, waits for them, and re-layouts: 4.47 us -> 5.86 us
  transfers between devices with their start and end apart: 19 -> 11, of which waited for: 3 -> 3; matrix products, arithmetic and copies ran while one was open for 2% -> 1% of each run, Pallas kernels for 13% -> 14%
where the time goes in v4:
time: 162 us; the launch traced here: 161 us
  starting transfers between devices  61.4 us (38%)
  Pallas kernels  42.5 us (26%)
  waiting for transfers between devices  27.4 us (17%)
  blocking collectives  21.2 us (13%)
  local copies, waits for them, and re-layouts  8.12 us (5%)
    ppermute x3, waiting for transfers between devices, shards(): lax.ppermute(key_blocks, 'y', [(at, (at + step) % breadth) for at in rang...  22.9 us
    all_to_all x1, blocking collectives, shards(): back = lax.all_to_all(context, PLANE_AXES, 0, 0, tiled=True)  21.2 us
    pallas_call x2, Pallas kernels, attend_window(): pl.pallas_call(functools.partial(window_kernel, start, low, high, bool(ha...  20.6 us
    pallas_call x1, Pallas kernels, attend_global(): pl.pallas_call(global_kernel, grid=(steps,), out_shape=jax.ShapeDtypeStru...  16.4 us
    ppermute x3, starting transfers between devices, swapped(): return lax.ppermute(value, 'core', [(0, 1), (1, 0)])  13.4 us
    all_to_all x1, starting transfers between devices, shards(): pieces = lax.all_to_all(part, 'z', 0, 0, tiled=True)  13.2 us
    ppermute x3, starting transfers between devices, shards(): lax.ppermute(key_blocks, 'y', [(at, (at + step) % breadth) for at in rang...  11.4 us
    all_to_all x1, starting transfers between devices, shards(): lax.all_to_all(pack(queries, key_vectors, value_vectors), PLANE_AXES, 0,...  10.6 us
  transfers between devices with their start and end apart: 11, of which 3 were waited for; matrix products, arithmetic and copies ran while one was open for 1% of the time, Pallas kernels for 14%

profile of v4, /device:TPU:1, one launch (start us, length us, event | category | flops | bytes accessed | tf_op | source)
XLA Modules:
  0.0 161.0 jit_solution(2706923706113129978)
XLA Ops:
  0.0 3.5 %pack.1 = bf16[32,3,128,128]{3,2,1,0:T(8,128)(2,1)} custom-call(bf16[2,128,2048]{2,1,0:T(8,128)(2,1)} %bitcast.24, bf16[2,128,2048]{2,1,0:T(8,128)(2,1)} %bitcast.25, bf16[2,128,2048]{2,1,0:T(8,128)(2,1)} %bitcast.26), custom_call_target="tpu_custom_call" | custom-call | tf_op jit(solution)/shard_map/pack/pallas_call | solution.py:63
  3.5 0.0 copy-start.9
  3.5 10.6 %all-to-all-start = ((bf16[32,3,128,128]{3,2,1,0:T(8,128)(2,1)}), bf16[32,3,128,128]{3,2,1,0:T(8,128)(2,1)S(1)}, u32[]{:S(2)}, u32[]{:S(2)}) async-start(bf16[32,3,128,128]{3,2,1,0:T(8,128)(2,1)} %pack.1), calls=%async_computation | async-start | bytes 6291456 | tf_op jit(solution)/shard_map/all_to_all | solution.py:365
  14.1 0.0 copy-done.9
  14.1 4.9 %collective-permute-start.1 = (s32[16,14]{1,0:T(8,128)S(1)}, s32[16,14]{1,0:T(8,128)S(1)}, u32[]{:S(2)}, u32[]{:S(2)}) collective-permute-start(s32[16,14]{1,0:T(8,128)S(1)} %copy-done.9), channel_id=1, source_target_pairs={{0,16},{8,24},{16,0},{24,8},{1,17},{9,25},{17,1},{25,9},{2,18},{10... | collective-permute-start | bytes 2696 | tf_op jit(solution)/shard_map/ppermute | solution.py:372
  19.0 2.2 %collective-permute-start = (s32[16,14]{1,0:T(8,128)S(1)}, s32[16,14]{1,0:T(8,128)S(1)}, u32[]{:S(2)}, u32[]{:S(2)}) collective-permute-start(s32[16,14]{1,0:T(8,128)S(1)} %copy-done.9), channel_id=1, source_target_pairs={{0,8},{8,16},{16,24},{24,0},{1,9},{9,17},{17,25},{25,1},{2,10},{10... | collective-permute-start | bytes 2696 | tf_op jit(solution)/shard_map/ppermute | solution.py:372
  21.3 4.2 %collective-permute-start.2 = (s32[16,14]{1,0:T(8,128)S(1)}, s32[16,14]{1,0:T(8,128)S(1)}, u32[]{:S(2)}, u32[]{:S(2)}) collective-permute-start(s32[16,14]{1,0:T(8,128)S(1)} %copy-done.9), channel_id=1, source_target_pairs={{0,24},{8,0},{16,8},{24,16},{1,25},{9,1},{17,9},{25,17},{2,26},{10... | collective-permute-start | bytes 2696 | tf_op jit(solution)/shard_map/ppermute | solution.py:372
  25.5 0.1 slice_bitcast_fusion
  25.6 1.3 collective-permute-start.3
  26.9 22.9 %collective-permute-done.1 = s32[16,14]{1,0:T(8,128)S(1)} collective-permute-done((s32[16,14]{1,0:T(8,128)S(1)}, s32[16,14]{1,0:T(8,128)S(1)}, u32[]{:S(2)}, u32[]{:S(2)}) %collective-permute-start.1) | collective-permute-done | bytes 928 | tf_op jit(solution)/shard_map/ppermute | solution.py:372
  49.8 0.0 collective-permute-done
  49.8 0.0 collective-permute-done.2
  49.8 0.0 copy-start.5
  49.8 0.0 collective-permute-done.3.above
  49.8 3.5 %all-to-all-done.kinds.own.query = bf16[32,3,128,128]{3,2,1,0:T(8,128)(2,1)S(1)} async-done(((bf16[32,3,128,128]{3,2,1,0:T(8,128)(2,1)}), bf16[32,3,128,128]{3,2,1,0:T(8,128)(2,1)S(1)}, u32[]{:S(2)}, u32[]{:S(2)}) %all-to-all-start) | async-done | bytes 3145760 | tf_op jit(solution)/shard_map/all_to_all | solution.py:365
  53.4 4.8 %collective-permute-start.4 = (bf16[32,3,128,128]{3,2,1,0:T(8,128)(2,1)S(1)}, bf16[32,3,128,128]{3,2,1,0:T(8,128)(2,1)}, u32[]{:S(2)}, u32[]{:S(2)}) collective-permute-start(bf16[32,3,128,128]{3,2,1,0:T(8,128)(2,1)S(1)} %all-to-all-done.kinds.own.query), channel_id=1, source_target_pairs={{0,1},{1,0},{2,3},{3,2},{4,5},{5,4},{6,7},{7,6},{8,9},{9,8},{10,11... | collective-permute-start | bytes 9437192 | tf_op jit(solution)/shard_map/ppermute | solution.py:353
  58.1 0.8 slice.7
  59.0 2.3 %collective-permute-start.5 = (bf16[8,2,128,128]{3,2,1,0:T(8,128)(2,1)}, bf16[8,2,128,128]{3,2,1,0:T(8,128)(2,1)}, u32[]{:S(2)}, u32[]{:S(2)}) collective-permute-start(bf16[8,2,128,128]{3,2,1,0:T(8,128)(2,1)} %slice.7), channel_id=1, source_target_pairs={{0,32},{32,64},{64,96},{96,128},{128,160},{160,192},{192,224},{224... | collective-permute-start | bytes 1572872 | tf_op jit(solution)/shard_map/ppermute | solution.py:379
  61.2 0.1 pad_add_fusion.1.where
  61.3 2.0 %pick_globals.1 = bf16[4,128,128]{2,1,0:T(8,128)(2,1)} custom-call(s32[3]{0:T(128)S(1)} %pad_add_fusion.1.where, s32[4,16,14]{2,1,0:T(8,128)S(1)} %pad_add_fusion.rows, s32[4]{0:T(128)S(1)} %collective-permute-done.3.above, bf16[32,3,128,128]{3,2,1,0:T(8,128)(2,1)S(1)} %all-to-all-done.kinds.own.query), custom_call_target="tpu_custom_call" | custom-call | tf_op jit(solution)/shard_map/pick_globals/pallas_call | solution.py:94
  63.4 13.2 %all-to-all-start.1 = ((bf16[16,32,128]{2,1,0:T(8,128)(2,1)}), bf16[16,32,128]{2,1,0:T(8,128)(2,1)S(1)}, u32[]{:S(2)}, u32[]{:S(2)}) async-start(bf16[16,32,128]{2,1,0:T(8,128)(2,1)} %bitcast.11), calls=%async_computation.1 | async-start | bytes 262144 | tf_op jit(solution)/shard_map/all_to_all | solution.py:384
  76.5 0.0 collective-permute-done.4.other
  76.6 10.1 %attend_far.1 = (f32[16,128,128]{2,1,0:T(8,128)S(1)}, f32[16,128,128]{2,1,0:T(8,128)S(1)}) custom-call(s32[3]{0:T(128)S(1)} %pad_add_fusion.1.where, s32[4,16,14]{2,1,0:T(8,128)S(1)} %pad_add_fusion.rows, bf16[32,3,128,128]{3,2,1,0:T(8,128)(2,1)S(1)} %all-to-all-done.kinds.own.query, bf16[32,3,128,128]{3,2,1,0:T(8,128)(2,1)} %collective-permute-done.4.other), custom_call_target="tpu_custom_call" | custom-call | flops 1342177280 | bytes 8388608 | tf_op jit(solution)/shard_map/attend_far/pallas_call | solution.py:230
  86.7 0.0 copy-start.1
  86.7 1.0 copy-done.1
  87.7 1.1 copy-done.2
  88.7 0.0 all-to-all-done.1
  88.7 0.0 collective-permute-done.5.refs_0_
  88.7 4.9 %collective-permute-start.6 = (bf16[8,2,128,128]{3,2,1,0:T(8,128)(2,1)}, bf16[8,2,128,128]{3,2,1,0:T(8,128)(2,1)}, u32[]{:S(2)}, u32[]{:S(2)}) collective-permute-start(bf16[8,2,128,128]{3,2,1,0:T(8,128)(2,1)} %collective-permute-done.5.refs_0_), channel_id=1, source_target_pairs={{0,1},{1,0},{2,3},{3,2},{4,5},{5,4},{6,7},{7,6},{8,9},{9,8},{10,11... | collective-permute-start | bytes 1572872 | tf_op jit(solution)/shard_map/ppermute | solution.py:353
  93.7 0.7 broadcast_in_dim.2
  94.4 9.3 %all-to-all-start.2 = ((bf16[16,32,128]{2,1,0:T(8,128)(2,1)}), bf16[16,32,128]{2,1,0:T(8,128)(2,1)S(1)}, u32[]{:S(2)}, u32[]{:S(2)}) async-start(bf16[16,32,128]{2,1,0:T(8,128)(2,1)} %broadcast_in_dim.2), calls=%async_computation.2 | async-start | bytes 262144 | tf_op jit(solution)/shard_map/all_to_all | solution.py:391
  103.7 0.0 collective-permute-done.6.refs_1_
  103.7 0.0 copy-done.5
  103.7 0.0 copy-done
  103.7 0.0 copy-done.6
  103.7 10.5 %attend_near.1 = (f32[16,128,128]{2,1,0:T(8,128)S(1)}, f32[16,128,128]{2,1,0:T(8,128)S(1)}) custom-call(s32[3]{0:T(128)S(1)} %pad_add_fusion.1.where, s32[4,16,14]{2,1,0:T(8,128)S(1)} %pad_add_fusion.rows, bf16[32,3,128,128]{3,2,1,0:T(8,128)(2,1)S(1)} %all-to-all-done.kinds.own.query, bf16[32,3,128,128]{3,2,1,0:T(8,128)(2,1)} %collective-permute-done.4.other, ...), custom_call_target="tpu_custom_call" | custom-call | flops 1342177280 | bytes 8388608 | tf_op jit(solution)/shard_map/attend_near/pallas_call | solution.py:230
  114.2 0.0 copy-start.3
  114.2 1.0 copy-done.3
  115.2 1.0 copy-done.4
  116.1 0.0 all-to-all-done.2
  116.1 3.7 %collective-permute-start.7 = (bf16[4,128,128]{2,1,0:T(8,128)(2,1)S(1)}, bf16[4,128,128]{2,1,0:T(8,128)(2,1)S(1)}, u32[]{:S(2)}, u32[]{:S(2)}) collective-permute-start(bf16[4,128,128]{2,1,0:T(8,128)(2,1)S(1)} %bitcast.27), channel_id=1, source_target_pairs={{0,1},{1,0},{2,3},{3,2},{4,5},{5,4},{6,7},{7,6},{8,9},{9,8},{10,11... | collective-permute-start | bytes 393224 | tf_op jit(solution)/shard_map/ppermute | solution.py:353
  119.9 1.0 collective-permute-done.7.other
  120.9 0.0 copy-done.7
  120.9 0.7 copy-done.8
  121.5 16.4 %attend_global.1 = bf16[32,128,128]{2,1,0:T(8,128)(2,1)} custom-call(s32[3]{0:T(128)} %copy-done.6, s32[4,16,14]{2,1,0:T(8,128)} %copy-done.5, bf16[4,128,128]{2,1,0:T(8,128)(2,1)} %bitcast.28, bf16[4,128,128]{2,1,0:T(8,128)(2,1)} %copy-done.8, bf16[32,3,128,128]{3,2,1,0:T(8,128)(2,1)} %copy-done, f32[16,128,128]{2,1,0:T(8,128)} %copy-done.3, ...), custom_call_target="tpu_custom_call" | custom-call | flops 1073741824 | bytes 8388608 | tf_op jit(solution)/shard_map/attend_global/pallas_call | solution.py:330
  137.9 21.2 %all_to_all.20 = bf16[32,128,128]{2,1,0:T(8,128)(2,1)S(1)} all-to-all(bf16[32,128,128]{2,1,0:T(8,128)(2,1)} %attend_global.1), channel_id=1, replica_groups=mesh['z'=16,'y'=4,'x'=4,'core'=2] {'y','x','core'}, dimensions={0} | all-to-all | bytes 2097152 | tf_op jit(solution)/shard_map/all_to_all | solution.py:397
  159.1 0.7 copy.5
  159.8 1.2 copy.8
  (8 shorter events, 0.0 us)
Async XLA Ops:
  3.5 10.6 %copy-start.9 = (s32[16,14]{1,0:T(8,128)S(1)}, s32[16,14]{1,0:T(8,128)}, u32[]{:S(2)}) copy-start(s32[16,14]{1,0:T(8,128)} %param.7) | copy-start | bytes 2692
  3.5 49.9 %all-to-all-start = ((bf16[32,3,128,128]{3,2,1,0:T(8,128)(2,1)}), bf16[32,3,128,128]{3,2,1,0:T(8,128)(2,1)S(1)}, u32[]{:S(2)}, u32[]{:S(2)}) async-start(bf16[32,3,128,128]{3,2,1,0:T(8,128)(2,1)} %pack.1), calls=%async_computation | async-start | bytes 6291456 | tf_op jit(solution)/shard_map/all_to_all | solution.py:365
  14.1 35.7 %collective-permute-start.1 = (s32[16,14]{1,0:T(8,128)S(1)}, s32[16,14]{1,0:T(8,128)S(1)}, u32[]{:S(2)}, u32[]{:S(2)}) collective-permute-start(s32[16,14]{1,0:T(8,128)S(1)} %copy-done.9), channel_id=1, source_target_pairs={{0,16},{8,24},{16,0},{24,8},{1,17},{9,25},{17,1},{25,9},{2,18},{10... | collective-permute-start | bytes 2696 | tf_op jit(solution)/shard_map/ppermute | solution.py:372
  19.0 30.8 %collective-permute-start = (s32[16,14]{1,0:T(8,128)S(1)}, s32[16,14]{1,0:T(8,128)S(1)}, u32[]{:S(2)}, u32[]{:S(2)}) collective-permute-start(s32[16,14]{1,0:T(8,128)S(1)} %copy-done.9), channel_id=1, source_target_pairs={{0,8},{8,16},{16,24},{24,0},{1,9},{9,17},{17,25},{25,1},{2,10},{10... | collective-permute-start | bytes 2696 | tf_op jit(solution)/shard_map/ppermute | solution.py:372
  21.3 28.6 %collective-permute-start.2 = (s32[16,14]{1,0:T(8,128)S(1)}, s32[16,14]{1,0:T(8,128)S(1)}, u32[]{:S(2)}, u32[]{:S(2)}) collective-permute-start(s32[16,14]{1,0:T(8,128)S(1)} %copy-done.9), channel_id=1, source_target_pairs={{0,24},{8,0},{16,8},{24,16},{1,25},{9,1},{17,9},{25,17},{2,26},{10... | collective-permute-start | bytes 2696 | tf_op jit(solution)/shard_map/ppermute | solution.py:372
  25.6 24.2 %collective-permute-start.3 = (s32[4]{0:T(128)S(1)}, s32[4]{0:T(128)S(1)}, u32[]{:S(2)}, u32[]{:S(2)}) collective-permute-start(s32[4]{0:T(128)S(1)} %slice_bitcast_fusion), channel_id=1, source_target_pairs={{32,0},{64,32},{96,64},{128,96},{160,128},{192,160},{224,192},{256... | collective-permute-start | bytes 56 | tf_op jit(solution)/shard_map/ppermute | solution.py:376
  49.8 53.8 %copy-start.5 = (s32[4,16,14]{2,1,0:T(8,128)}, s32[4,16,14]{2,1,0:T(8,128)S(1)}, u32[]{:S(2)}) copy-start(s32[4,16,14]{2,1,0:T(8,128)S(1)} %pad_add_fusion.rows) | copy-start | bytes 10756
  53.4 50.3 %copy-start = (bf16[32,3,128,128]{3,2,1,0:T(8,128)(2,1)}, bf16[32,3,128,128]{3,2,1,0:T(8,128)(2,1)S(1)}, u32[]{:S(2)}) copy-start(bf16[32,3,128,128]{3,2,1,0:T(8,128)(2,1)S(1)} %all-to-all-done.kinds.own.query) | copy-start | bytes 9437188
  53.4 23.2 %collective-permute-start.4 = (bf16[32,3,128,128]{3,2,1,0:T(8,128)(2,1)S(1)}, bf16[32,3,128,128]{3,2,1,0:T(8,128)(2,1)}, u32[]{:S(2)}, u32[]{:S(2)}) collective-permute-start(bf16[32,3,128,128]{3,2,1,0:T(8,128)(2,1)S(1)} %all-to-all-done.kinds.own.query), channel_id=1, source_target_pairs={{0,1},{1,0},{2,3},{3,2},{4,5},{5,4},{6,7},{7,6},{8,9},{9,8},{10,11... | collective-permute-start | bytes 9437192 | tf_op jit(solution)/shard_map/ppermute | solution.py:353
  59.0 29.8 %collective-permute-start.5 = (bf16[8,2,128,128]{3,2,1,0:T(8,128)(2,1)}, bf16[8,2,128,128]{3,2,1,0:T(8,128)(2,1)}, u32[]{:S(2)}, u32[]{:S(2)}) collective-permute-start(bf16[8,2,128,128]{3,2,1,0:T(8,128)(2,1)} %slice.7), channel_id=1, source_target_pairs={{0,32},{32,64},{64,96},{96,128},{128,160},{160,192},{192,224},{224... | collective-permute-start | bytes 1572872 | tf_op jit(solution)/shard_map/ppermute | solution.py:379
  61.3 42.4 %copy-start.6 = (s32[3]{0:T(128)}, s32[3]{0:T(128)S(1)}, u32[]{:S(2)}) copy-start(s32[3]{0:T(128)S(1)} %pad_add_fusion.1.where) | copy-start | bytes 40
  63.4 25.4 %all-to-all-start.1 = ((bf16[16,32,128]{2,1,0:T(8,128)(2,1)}), bf16[16,32,128]{2,1,0:T(8,128)(2,1)S(1)}, u32[]{:S(2)}, u32[]{:S(2)}) async-start(bf16[16,32,128]{2,1,0:T(8,128)(2,1)} %bitcast.11), calls=%async_computation.1 | async-start | bytes 262144 | tf_op jit(solution)/shard_map/all_to_all | solution.py:384
  86.7 1.0 copy-start.1
  87.7 1.1 copy-start.2
  88.7 14.9 %collective-permute-start.6 = (bf16[8,2,128,128]{3,2,1,0:T(8,128)(2,1)}, bf16[8,2,128,128]{3,2,1,0:T(8,128)(2,1)}, u32[]{:S(2)}, u32[]{:S(2)}) collective-permute-start(bf16[8,2,128,128]{3,2,1,0:T(8,128)(2,1)} %collective-permute-done.5.refs_0_), channel_id=1, source_target_pairs={{0,1},{1,0},{2,3},{3,2},{4,5},{5,4},{6,7},{7,6},{8,9},{9,8},{10,11... | collective-permute-start | bytes 1572872 | tf_op jit(solution)/shard_map/ppermute | solution.py:353
  94.4 21.8 %all-to-all-start.2 = ((bf16[16,32,128]{2,1,0:T(8,128)(2,1)}), bf16[16,32,128]{2,1,0:T(8,128)(2,1)S(1)}, u32[]{:S(2)}, u32[]{:S(2)}) async-start(bf16[16,32,128]{2,1,0:T(8,128)(2,1)} %broadcast_in_dim.2), calls=%async_computation.2 | async-start | bytes 262144 | tf_op jit(solution)/shard_map/all_to_all | solution.py:391
  114.2 1.0 copy-start.3
  115.2 1.0 copy-start.4
  116.1 4.7 %copy-start.7 = (bf16[16,32,128]{2,1,0:T(8,128)(2,1)}, bf16[16,32,128]{2,1,0:T(8,128)(2,1)S(1)}, u32[]{:S(2)}) copy-start(bf16[16,32,128]{2,1,0:T(8,128)(2,1)S(1)} %all-to-all-done.2) | copy-start | bytes 393220
  116.1 4.7 %collective-permute-start.7 = (bf16[4,128,128]{2,1,0:T(8,128)(2,1)S(1)}, bf16[4,128,128]{2,1,0:T(8,128)(2,1)S(1)}, u32[]{:S(2)}, u32[]{:S(2)}) collective-permute-start(bf16[4,128,128]{2,1,0:T(8,128)(2,1)S(1)} %bitcast.27), channel_id=1, source_target_pairs={{0,1},{1,0},{2,3},{3,2},{4,5},{5,4},{6,7},{7,6},{8,9},{9,8},{10,11... | collective-permute-start | bytes 393224 | tf_op jit(solution)/shard_map/ppermute | solution.py:353
  120.9 0.7 copy-start.8

commit v5 on v4

v5 whole, which is shorter than its diff:
```python
import functools
import math

import jax
import jax.numpy as jnp
from jax import lax
from jax.experimental import pallas as pl
from jax.experimental.pallas import tpu as pltpu
from jax.sharding import Mesh
from jax.sharding import PartitionSpec as P

HEAD_DIM = 128
BLOCK = 128
WIN = 16
WSEL = 10
GLOBALS = 4
SLOTS = WSEL + GLOBALS
HEADS = 16
PLANE = 64
CHUNK = 16
FACTOR = math.log2(math.e) / math.sqrt(HEAD_DIM)
UNROLL = 4
PLANE_AXES = ("y", "x", "core")
Z_AXES = ("far", "near")

SCALARS = pl.BlockSpec(memory_space=pltpu.SMEM)
WHOLE = pl.BlockSpec(memory_space=pltpu.VMEM)
LEFT = pl.BlockSpec(memory_space=pl.ANY)


def pack_kernel(queries, keys, values, out, query_buf, key_buf, value_buf, arrived, sems):
    def moves():
        for head in range(HEADS):
            columns = pl.ds(head * HEAD_DIM, HEAD_DIM)
            yield 0, key_buf.at[:, :, columns], out.at[2 * head, pl.ds(0, 2)]
            yield 1, value_buf.at[:, :, columns], out.at[2 * head + 1, pl.ds(0, 2)]
            yield 2, query_buf.at[0, :, columns], out.at[2 * head, 2]
            yield 2, query_buf.at[1, :, columns], out.at[2 * head + 1, 2]

    loads = [
        pltpu.make_async_copy(source, target, arrived.at[at])
        for at, (source, target) in enumerate(
            [(keys, key_buf), (values, value_buf), (queries, query_buf)]
        )
    ]
    stores = [
        (array, pltpu.make_async_copy(source, target, sems.at[at]))
        for at, (array, source, target) in enumerate(moves())
    ]
    for load in loads:
        load.start()
    for at, load in enumerate(loads):
        load.wait()
        for array, store in stores:
            if array == at:
                store.start()
    for _, store in stores:
        store.wait()


def pack(*arrays):
    arrays = [array.reshape(2, BLOCK, HEADS * HEAD_DIM) for array in arrays]
    return pl.pallas_call(
        pack_kernel,
        out_shape=jax.ShapeDtypeStruct((2 * HEADS, 3, BLOCK, HEAD_DIM), jnp.bfloat16),
        in_specs=[LEFT] * 3,
        out_specs=LEFT,
        scratch_shapes=[pltpu.VMEM(array.shape, array.dtype) for array in arrays]
        + [pltpu.SemaphoreType.DMA((3,)), pltpu.SemaphoreType.DMA((4 * HEADS,))],
        compiler_params=pltpu.CompilerParams(vmem_limit_bytes=56 << 20),
        name="pack",
    )(*arrays)


def pick_kernel(where, rows, above, kinds, out, buffer, sems):
    group, last = row_of(where, PLANE // 2 - 1, 1)
    copies, present = [], []
    for slot in range(GLOBALS):
        place = jnp.maximum(rows[group, last, WSEL + slot], above[slot]) - where[1]
        held = (place >= 0) & (place < PLANE)
        place = jnp.where(held, place, 0)
        source = kinds.at[place // 2, place % 2]
        copies.append(pltpu.make_async_copy(source, buffer.at[slot], sems.at[slot]))
        present.append(held)
    for copy in copies:
        copy.start()
    for slot in range(GLOBALS):
        copies[slot].wait()
        block = buffer[slot]
        out[slot] = jnp.where(present[slot], block, jnp.zeros_like(block))


def pick_globals(where, rows, above, kinds):
    return pl.pallas_call(
        pick_kernel,
        out_shape=jax.ShapeDtypeStruct((GLOBALS, BLOCK, HEAD_DIM), jnp.bfloat16),
        in_specs=[SCALARS, SCALARS, SCALARS, LEFT],
        out_specs=WHOLE,
        scratch_shapes=[
            pltpu.VMEM((GLOBALS, BLOCK, HEAD_DIM), jnp.bfloat16),
            pltpu.SemaphoreType.DMA((GLOBALS,)),
        ],
        compiler_params=pltpu.CompilerParams(vmem_limit_bytes=12 << 20),
        name="pick_globals",
    )(where, rows, above, kinds)


def row_of(where, at, core):
    row = 2 * at + core
    return (where[2] + 4 - row // CHUNK) % 4, row % CHUNK


def two_blocks(blocks, one, two):
    return jnp.concatenate([blocks[one // 2, one % 2], blocks[two // 2, two % 2]], axis=0)


def attend_kernel(start, high, kept, where, rows, own, other, global_own, global_other, *refs):
    if kept:
        halo_own, halo_other, before, *refs = refs
    out, keys, values, scores, weights, sems = refs
    core, first = where[0], where[1]
    chunks = high // CHUNK
    halo_at = high
    global_at = high + (WIN if kept else 0)
    count = kept if kept else out.shape[0]

    def copies(own_to, other_to, at):
        if at < chunks:
            source = pl.ds(at * CHUNK // 2, CHUNK // 2)
            pairs = [(own.at[source, pl.ds(0, 2)], own_to), (other.at[source, pl.ds(0, 2)], other_to)]
            target = source
        elif at == chunks:
            pairs = [(global_own, own_to), (global_other, other_to)]
            target = pl.ds(global_at // 2, GLOBALS // 2)
        else:
            pairs = [(halo_own, own_to), (halo_other, other_to)]
            target = pl.ds(halo_at // 2, WIN // 2)
        for kind, (array, to) in enumerate(pairs):
            yield pltpu.make_async_copy(array, to.at[target], sems.at[kind, at])

    parts = list(range(chunks + (2 if kept else 1)))

    @pl.when(core == 0)
    def _():
        for part in parts:
            for copy in copies(keys, values, part):
                copy.start()

    @pl.when(core != 0)
    def _():
        for part in parts:
            for copy in copies(values, keys, part):
                copy.start()

    if kept:
        out[kept:] = before[...]

    needed = {}
    for part in parts:
        step = 0
        if part < chunks:
            step = max(0, (part * CHUNK - 2 * start) // (2 * UNROLL))
        needed.setdefault(step, []).append(part)

    causal = lax.broadcasted_iota(jnp.int32, (BLOCK, BLOCK), 0) >= lax.broadcasted_iota(
        jnp.int32, (BLOCK, BLOCK), 1
    )

    def place_of(at, slot):
        group, row = row_of(where, start + at, core)
        block_id = rows[group, row, slot]
        if slot < WSEL:
            place = block_id - first
            if kept:
                place = jnp.where(place >= 0, place, place + halo_at + WIN)
        else:
            place = global_at + slot - WSEL
        return jnp.where(block_id >= 0, place, 0), block_id >= 0

    def score_phase(at, lane):
        block_query = own[start + at, 2]
        highest = None
        for slot in range(0, SLOTS, 2):
            one, listed_one = place_of(at, slot)
            two, listed_two = place_of(at, slot + 1)
            both = lax.dot_general(
                block_query, two_blocks(keys, one, two), (((1,), (1,)), ((), ())),
                preferred_element_type=jnp.float32,
            )
            for part, listed in enumerate([listed_one, listed_two]):
                score = both[:, part * BLOCK : (part + 1) * BLOCK]
                if slot + part == 0:
                    score = jnp.where(causal, score, -1e30)
                elif kept or slot + part >= WSEL:
                    score = jnp.where(listed, score, -1e30)
                scores[lane, slot + part] = score
                highest = score if highest is None else jnp.maximum(highest, score)
        row_max = jnp.max(highest, axis=1, keepdims=True) * FACTOR
        return jnp.broadcast_to(row_max, (BLOCK, BLOCK))

    def weight_phase(lane, row_max):
        total = None
        for slot in range(SLOTS):
            weight = jnp.exp2(scores[lane, slot] * FACTOR - row_max)
            total = weight if total is None else total + weight
            weights[lane, :, slot * BLOCK : (slot + 1) * BLOCK] = weight.astype(jnp.bfloat16)
        return jnp.sum(total, axis=1, keepdims=True)

    def value_phase(at, lane, denom):
        mixed = None
        for slot in range(0, SLOTS, 2):
            one, two = place_of(at, slot)[0], place_of(at, slot + 1)[0]
            term = jnp.dot(
                weights[lane, :, slot * BLOCK : (slot + 2) * BLOCK],
                two_blocks(values, one, two),
                preferred_element_type=jnp.float32,
            )
            mixed = term if mixed is None else mixed + term
        out[at] = (mixed / denom).astype(jnp.bfloat16)

    def step(at, carry):
        for when, needs in needed.items():

            @pl.when(at == when)
            def _(needs=needs):
                for part in needs:
                    for copy in copies(keys, values, part):
                        copy.wait()

        at = at * UNROLL
        row_max, denom = score_phase(at, 0), None
        for lane in range(UNROLL):
            following = score_phase(at + lane + 1, lane + 1) if lane + 1 < UNROLL else None
            found = weight_phase(lane, row_max)
            if lane:
                value_phase(at + lane - 1, lane - 1, denom)
            row_max, denom = following, found
        value_phase(at + UNROLL - 1, UNROLL - 1, denom)
        return carry

    lax.fori_loop(0, count // UNROLL, step, 0)


def attend(start, high, where, rows, own, other, global_own, global_other, *halo):
    total = own.shape[0] - start
    kept = total - halo[-1].shape[0] if halo else 0
    count = kept if kept else total
    span = high + GLOBALS + (WIN if kept else 0)
    pairs = count * SLOTS * BLOCK * BLOCK
    return pl.pallas_call(
        functools.partial(attend_kernel, start, high, kept),
        out_shape=jax.ShapeDtypeStruct((total, BLOCK, HEAD_DIM), jnp.bfloat16),
        in_specs=[SCALARS, SCALARS, WHOLE]
        + [LEFT] * 3
        + ([LEFT, LEFT, WHOLE] if kept else []),
        out_specs=WHOLE,
        scratch_shapes=[
            pltpu.VMEM((span // 2, 2, BLOCK, HEAD_DIM), jnp.bfloat16),
            pltpu.VMEM((span // 2, 2, BLOCK, HEAD_DIM), jnp.bfloat16),
            pltpu.VMEM((UNROLL, SLOTS, BLOCK, BLOCK), jnp.float32),
            pltpu.VMEM((UNROLL, BLOCK, SLOTS * BLOCK), jnp.bfloat16),
            pltpu.SemaphoreType.DMA((2, high // CHUNK + 2)),
        ],
        compiler_params=pltpu.CompilerParams(vmem_limit_bytes=24 << 20),
        cost_estimate=pl.CostEstimate(
            flops=4 * pairs * HEAD_DIM, bytes_accessed=8 << 20, transcendentals=pairs
        ),
        name="attend_first" if kept else "attend_rest",
    )(where, rows, own, other, global_own, global_other, *halo)


def swapped(value):
    return lax.ppermute(value, "core", [(0, 1), (1, 0)])


def shards(queries, key_vectors, value_vectors, key_blocks):
    depth = lax.axis_size(Z_AXES)
    breadth = lax.axis_size("y")
    up = [(at, at + 1) for at in range(depth - 1)]
    down = [(at + 1, at) for at in range(depth - 1)]
    where = jnp.stack(
        [lax.axis_index("core"), lax.axis_index(Z_AXES) * PLANE, lax.axis_index("y")]
    )

    received = lax.all_to_all(
        pack(queries, key_vectors, value_vectors), PLANE_AXES, 0, 0, tiled=True
    )

    rows = jnp.stack(
        [key_blocks]
        + [
            lax.ppermute(key_blocks, "y", [(at, (at + step) % breadth) for at in range(breadth)])
            for step in range(1, breadth)
        ]
    )
    above = lax.ppermute(key_blocks[-1, WSEL:], Z_AXES, down)
    own, rows, above = lax.optimization_barrier((received, rows, above))
    other = swapped(own)

    def spread(value, axis):
        copies = jnp.broadcast_to(value[None], (GLOBALS,) + value.shape)
        return lax.all_to_all(copies, axis, 0, 0, tiled=True)

    def summed(values):
        return jnp.sum(values.astype(jnp.float32), axis=0).astype(jnp.bfloat16)

    part = pick_globals(where, rows, above, own)
    held = summed(lax.all_to_all(part, "near", 0, 0, tiled=True))
    held = summed(spread(held, "far"))
    global_own = spread(held, "near")
    last, global_own = lax.optimization_barrier((own[-WIN // 2 :, :2], global_own))
    pair = (GLOBALS // 2, 2, BLOCK, HEAD_DIM)
    global_own = global_own.reshape(pair)
    global_other = swapped(global_own)
    halo_own = lax.ppermute(last, Z_AXES, up)
    rest = attend(
        WIN // 2, PLANE, where, rows, own, other, global_own, global_other
    )
    rest, halo_own = lax.optimization_barrier((rest, halo_own))
    context = attend(
        0, CHUNK, where, rows, own, other, global_own, global_other,
        halo_own, swapped(halo_own), rest,
    )
    back = lax.all_to_all(context, PLANE_AXES, 0, 0, tiled=True)
    return jnp.transpose(
        back.reshape(HEADS, 2, BLOCK, HEAD_DIM), (1, 2, 0, 3)
    ).reshape(queries.shape)


def solution(mesh):
    fine = Mesh(mesh.devices.reshape(-1, GLOBALS, 4, 4, 2), Z_AXES + PLANE_AXES)
    tokens = P(Z_AXES + PLANE_AXES, None)
    return jax.shard_map(
        shards,
        mesh=fine,
        in_specs=(tokens, tokens, tokens, P(Z_AXES + ("y",), None)),
        out_specs=tokens,
        check_vma=False,
    )
```

time: 162 us -> 159 us (0.981)
  blocking collectives: 21.2 us -> 54 us
  starting transfers between devices: 61.4 us -> 42.9 us
  Pallas kernels: 42.5 us -> 25.1 us
  waiting for transfers between devices: 27.4 us -> 32.9 us
  local copies, waits for them, and re-layouts: 8.12 us -> 3.53 us
    all_to_all x0 -> x2, blocking collectives: none -> 33.7 us  [the longest x1 25.5 us: spread(): return lax.all_to_all(copies, axis, 0, 0, tiled=True)]
    all_to_all x2 -> x1, starting transfers between devices: 22.5 us -> 3.32 us  [spread(): return lax.all_to_all(copies, axis, 0, 0, tiled=True)]
    pallas_call x3 -> x2, Pallas kernels: 37 us -> 20.3 us  [attend(): pl.pallas_call(functools.partial(attend_kernel, start, high, kept), out_s...]
    unnamed x21 -> x3, local copies, waits for them, and re-layouts: 5.86 us -> 1.25 us
    all_to_all x2 -> x1, waiting for transfers between devices: 0.01 us -> 3.89 us  [spread(): return lax.all_to_all(copies, axis, 0, 0, tiled=True)]
  transfers between devices with their start and end apart: 11 -> 10, of which waited for: 3 -> 5; matrix products, arithmetic and copies ran while one was open for 1% -> 1% of each run, Pallas kernels for 14% -> 10%
where the time goes in v5:
time: 159 us
  blocking collectives  54 us (34%)
  starting transfers between devices  42.9 us (27%)
  waiting for transfers between devices  32.9 us (21%)
  Pallas kernels  25.1 us (16%)
  local copies, waits for them, and re-layouts  3.53 us (2%)
    all_to_all x1, blocking collectives, spread(): return lax.all_to_all(copies, axis, 0, 0, tiled=True)  25.5 us
    ppermute x3, waiting for transfers between devices, shards(): lax.ppermute(key_blocks, 'y', [(at, (at + step) % breadth) for at in rang...  22.9 us
    pallas_call x2, Pallas kernels, attend(): pl.pallas_call(functools.partial(attend_kernel, start, high, kept), out_s...  20.3 us
    all_to_all x1, blocking collectives, shards(): back = lax.all_to_all(context, PLANE_AXES, 0, 0, tiled=True)  20.3 us
    ppermute x3, starting transfers between devices, swapped(): return lax.ppermute(value, 'core', [(0, 1), (1, 0)])  13.4 us
    ppermute x3, starting transfers between devices, shards(): lax.ppermute(key_blocks, 'y', [(at, (at + step) % breadth) for at in rang...  11.4 us
    all_to_all x1, starting transfers between devices, shards(): lax.all_to_all(pack(queries, key_vectors, value_vectors), PLANE_AXES, 0,...  10.6 us
    all_to_all x1, blocking collectives, shards(): held = summed(lax.all_to_all(part, 'near', 0, 0, tiled=True))  8.17 us
  transfers between devices with their start and end apart: 10, of which 5 were waited for; matrix products, arithmetic and copies ran while one was open for 1% of the time, Pallas kernels for 10%

profile of v5, /device:TPU:1, one launch (start us, length us, event | category | flops | bytes accessed | tf_op | source)
XLA Modules:
  0.0 158.7 jit_solution(3019797860619282590)
XLA Ops:
  0.0 3.5 %pack.1 = bf16[32,3,128,128]{3,2,1,0:T(8,128)(2,1)} custom-call(bf16[2,128,2048]{2,1,0:T(8,128)(2,1)} %bitcast.26, bf16[2,128,2048]{2,1,0:T(8,128)(2,1)} %bitcast.27, bf16[2,128,2048]{2,1,0:T(8,128)(2,1)} %bitcast.28), custom_call_target="tpu_custom_call" | custom-call | tf_op jit(solution)/shard_map/pack/pallas_call | solution.py:63
  3.5 0.0 copy-start
  3.5 10.6 %all-to-all-start = ((bf16[32,3,128,128]{3,2,1,0:T(8,128)(2,1)}), bf16[32,3,128,128]{3,2,1,0:T(8,128)(2,1)S(1)}, u32[]{:S(2)}, u32[]{:S(2)}) async-start(bf16[32,3,128,128]{3,2,1,0:T(8,128)(2,1)} %pack.1), calls=%async_computation | async-start | bytes 6291456 | tf_op jit(solution)/shard_map/all_to_all | solution.py:285
  14.1 0.0 copy-done
  14.1 4.9 %collective-permute-start.1 = (s32[16,14]{1,0:T(8,128)S(1)}, s32[16,14]{1,0:T(8,128)S(1)}, u32[]{:S(2)}, u32[]{:S(2)}) collective-permute-start(s32[16,14]{1,0:T(8,128)S(1)} %copy-done), channel_id=1, source_target_pairs={{0,16},{8,24},{16,0},{24,8},{1,17},{9,25},{17,1},{25,9},{2,18},{10... | collective-permute-start | bytes 2696 | tf_op jit(solution)/shard_map/ppermute | solution.py:292
  19.0 2.2 %collective-permute-start = (s32[16,14]{1,0:T(8,128)S(1)}, s32[16,14]{1,0:T(8,128)S(1)}, u32[]{:S(2)}, u32[]{:S(2)}) collective-permute-start(s32[16,14]{1,0:T(8,128)S(1)} %copy-done), channel_id=1, source_target_pairs={{0,8},{8,16},{16,24},{24,0},{1,9},{9,17},{17,25},{25,1},{2,10},{10... | collective-permute-start | bytes 2696 | tf_op jit(solution)/shard_map/ppermute | solution.py:292
  21.3 4.2 %collective-permute-start.2 = (s32[16,14]{1,0:T(8,128)S(1)}, s32[16,14]{1,0:T(8,128)S(1)}, u32[]{:S(2)}, u32[]{:S(2)}) collective-permute-start(s32[16,14]{1,0:T(8,128)S(1)} %copy-done), channel_id=1, source_target_pairs={{0,24},{8,0},{16,8},{24,16},{1,25},{9,1},{17,9},{25,17},{2,26},{10... | collective-permute-start | bytes 2696 | tf_op jit(solution)/shard_map/ppermute | solution.py:292
  25.5 0.1 slice_bitcast_fusion
  25.6 1.3 collective-permute-start.3
  26.9 22.9 %collective-permute-done.1 = s32[16,14]{1,0:T(8,128)S(1)} collective-permute-done((s32[16,14]{1,0:T(8,128)S(1)}, s32[16,14]{1,0:T(8,128)S(1)}, u32[]{:S(2)}, u32[]{:S(2)}) %collective-permute-start.1) | collective-permute-done | bytes 928 | tf_op jit(solution)/shard_map/ppermute | solution.py:292
  49.8 0.0 collective-permute-done
  49.8 0.0 collective-permute-done.2
  49.8 0.0 collective-permute-done.3.above
  49.9 3.5 %all-to-all-done.kinds.own = bf16[32,3,128,128]{3,2,1,0:T(8,128)(2,1)S(1)} async-done(((bf16[32,3,128,128]{3,2,1,0:T(8,128)(2,1)}), bf16[32,3,128,128]{3,2,1,0:T(8,128)(2,1)S(1)}, u32[]{:S(2)}, u32[]{:S(2)}) %all-to-all-start) | async-done | bytes 3145760 | tf_op jit(solution)/shard_map/all_to_all | solution.py:285
  53.4 4.8 %collective-permute-start.4 = (bf16[32,3,128,128]{3,2,1,0:T(8,128)(2,1)S(1)}, bf16[32,3,128,128]{3,2,1,0:T(8,128)(2,1)}, u32[]{:S(2)}, u32[]{:S(2)}) collective-permute-start(bf16[32,3,128,128]{3,2,1,0:T(8,128)(2,1)S(1)} %all-to-all-done.kinds.own), channel_id=1, source_target_pairs={{0,1},{1,0},{2,3},{3,2},{4,5},{5,4},{6,7},{7,6},{8,9},{9,8},{10,11... | collective-permute-start | bytes 9437192 | tf_op jit(solution)/shard_map/ppermute | solution.py:273
  58.1 0.1 pad_add_fusion.1.where
  58.2 1.4 pick_globals.1
  59.6 8.2 %all_to_all.25 = bf16[4,128,128]{2,1,0:T(8,128)(2,1)S(1)} all-to-all(bf16[4,128,128]{2,1,0:T(8,128)(2,1)S(1)} %pick_globals.1), channel_id=1, replica_groups=mesh['far'=4,'near'=4,'y'=4,'x'=4,'core'=2] {'near'}, dimensions={0} | all-to-all | bytes 262144 | tf_op jit(solution)/shard_map/all_to_all | solution.py:308
  67.8 25.5 %all_to_all.26 = bf16[4,128,128]{2,1,0:T(8,128)(2,1)S(1)} all-to-all(bf16[4,128,128]{2,1,0:T(8,128)(2,1)S(1)} %broadcast_in_dim.4), channel_id=1, replica_groups=mesh['far'=4,'near'=4,'y'=4,'x'=4,'core'=2] {'far'}, dimensions={0} | all-to-all | bytes 262144 | tf_op jit(solution)/shard_map/all_to_all | solution.py:302
  93.4 0.7 broadcast_in_dim.5
  94.0 3.3 %all-to-all-start.3 = ((bf16[4,128,128]{2,1,0:T(8,128)(2,1)}), bf16[4,128,128]{2,1,0:T(8,128)(2,1)S(1)}, u32[]{:S(2)}, u32[]{:S(2)}) async-start(bf16[4,128,128]{2,1,0:T(8,128)(2,1)} %broadcast_in_dim.5), calls=%async_computation.3 | async-start | bytes 262144 | tf_op jit(solution)/shard_map/all_to_all | solution.py:302
  97.4 0.8 slice.7
  98.2 3.9 %all-to-all-done.3 = bf16[4,128,128]{2,1,0:T(8,128)(2,1)S(1)} async-done(((bf16[4,128,128]{2,1,0:T(8,128)(2,1)}), bf16[4,128,128]{2,1,0:T(8,128)(2,1)S(1)}, u32[]{:S(2)}, u32[]{:S(2)}) %all-to-all-start.3) | async-done | bytes 131104 | tf_op jit(solution)/shard_map/all_to_all | solution.py:302
  102.1 2.9 %collective-permute-start.6 = (bf16[8,2,128,128]{3,2,1,0:T(8,128)(2,1)}, bf16[8,2,128,128]{3,2,1,0:T(8,128)(2,1)S(1)}, u32[]{:S(2)}, u32[]{:S(2)}) collective-permute-start(bf16[8,2,128,128]{3,2,1,0:T(8,128)(2,1)} %slice.7), channel_id=1, source_target_pairs={{0,32},{32,64},{64,96},{96,128},{128,160},{160,192},{192,224},{224... | collective-permute-start | bytes 1572872 | tf_op jit(solution)/shard_map/ppermute | solution.py:315
  105.0 6.3 %collective-permute-start.5 = (bf16[2,2,128,128]{3,2,1,0:T(8,128)(2,1)S(1)}, bf16[2,2,128,128]{3,2,1,0:T(8,128)(2,1)S(1)}, u32[]{:S(2)}, u32[]{:S(2)}) collective-permute-start(bf16[2,2,128,128]{3,2,1,0:T(8,128)(2,1)S(1)} %bitcast.21), channel_id=1, source_target_pairs={{0,1},{1,0},{2,3},{3,2},{4,5},{5,4},{6,7},{7,6},{8,9},{9,8},{10,11... | collective-permute-start | bytes 393224 | tf_op jit(solution)/shard_map/ppermute | solution.py:273
  111.4 1.0 collective-permute-done.5.global_other
  112.3 0.0 collective-permute-done.4.other
  112.3 13.9 %attend_rest.1.refs_2_ = bf16[24,128,128]{2,1,0:T(8,128)(2,1)S(1)} custom-call(s32[3]{0:T(128)S(1)} %pad_add_fusion.1.where, s32[4,16,14]{2,1,0:T(8,128)S(1)} %pad_add_fusion.rows, bf16[32,3,128,128]{3,2,1,0:T(8,128)(2,1)S(1)} %all-to-all-done.kinds.own, bf16[32,3,128,128]{3,2,1,0:T(8,128)(2,1)} %collective-permute-done.4.other, ...), custom_call_target="tpu_custom_call" | custom-call | flops 2818572288 | bytes 8388608 | tf_op jit(solution)/shard_map/attend_rest/pallas_call | solution.py:250
  126.2 0.0 collective-permute-done.6.refs_0_
  126.2 2.3 %collective-permute-start.7 = (bf16[8,2,128,128]{3,2,1,0:T(8,128)(2,1)S(1)}, bf16[8,2,128,128]{3,2,1,0:T(8,128)(2,1)S(1)}, u32[]{:S(2)}, u32[]{:S(2)}) collective-permute-start(bf16[8,2,128,128]{3,2,1,0:T(8,128)(2,1)S(1)} %collective-permute-done.6.refs_0_), channel_id=1, source_target_pairs={{0,1},{1,0},{2,3},{3,2},{4,5},{5,4},{6,7},{7,6},{8,9},{9,8},{10,11... | collective-permute-start | bytes 1572872 | tf_op jit(solution)/shard_map/ppermute | solution.py:273
  128.5 1.5 collective-permute-done.7.refs_1_
  130.0 6.4 %attend_first.1 = bf16[32,128,128]{2,1,0:T(8,128)(2,1)S(1)} custom-call(s32[3]{0:T(128)S(1)} %pad_add_fusion.1.where, s32[4,16,14]{2,1,0:T(8,128)S(1)} %pad_add_fusion.rows, bf16[32,3,128,128]{3,2,1,0:T(8,128)(2,1)S(1)} %all-to-all-done.kinds.own, bf16[32,3,128,128]{3,2,1,0:T(8,128)(2,1)} %collective-permute-done.4.other, ...), custom_call_target="tpu_custom_call" | custom-call | flops 939524096 | bytes 8388608 | tf_op jit(solution)/shard_map/attend_first/pallas_call | solution.py:250
  136.5 20.3 %all_to_all.27 = bf16[32,128,128]{2,1,0:T(8,128)(2,1)S(1)} all-to-all(bf16[32,128,128]{2,1,0:T(8,128)(2,1)S(1)} %attend_first.1), channel_id=1, replica_groups=mesh['far'=4,'near'=4,'y'=4,'x'=4,'core'=2] {'y','x','core'}, dimensions={0} | all-to-all | bytes 2097152 | tf_op jit(solution)/shard_map/all_to_all | solution.py:324
  156.7 0.7 copy.6
  157.4 1.2 copy.9
  (4 shorter events, 0.1 us)
Async XLA Ops:
  3.5 10.6 %copy-start = (s32[16,14]{1,0:T(8,128)S(1)}, s32[16,14]{1,0:T(8,128)}, u32[]{:S(2)}) copy-start(s32[16,14]{1,0:T(8,128)} %param.7) | copy-start | bytes 2692
  3.5 49.9 %all-to-all-start = ((bf16[32,3,128,128]{3,2,1,0:T(8,128)(2,1)}), bf16[32,3,128,128]{3,2,1,0:T(8,128)(2,1)S(1)}, u32[]{:S(2)}, u32[]{:S(2)}) async-start(bf16[32,3,128,128]{3,2,1,0:T(8,128)(2,1)} %pack.1), calls=%async_computation | async-start | bytes 6291456 | tf_op jit(solution)/shard_map/all_to_all | solution.py:285
  14.1 35.7 %collective-permute-start.1 = (s32[16,14]{1,0:T(8,128)S(1)}, s32[16,14]{1,0:T(8,128)S(1)}, u32[]{:S(2)}, u32[]{:S(2)}) collective-permute-start(s32[16,14]{1,0:T(8,128)S(1)} %copy-done), channel_id=1, source_target_pairs={{0,16},{8,24},{16,0},{24,8},{1,17},{9,25},{17,1},{25,9},{2,18},{10... | collective-permute-start | bytes 2696 | tf_op jit(solution)/shard_map/ppermute | solution.py:292
  19.0 30.8 %collective-permute-start = (s32[16,14]{1,0:T(8,128)S(1)}, s32[16,14]{1,0:T(8,128)S(1)}, u32[]{:S(2)}, u32[]{:S(2)}) collective-permute-start(s32[16,14]{1,0:T(8,128)S(1)} %copy-done), channel_id=1, source_target_pairs={{0,8},{8,16},{16,24},{24,0},{1,9},{9,17},{17,25},{25,1},{2,10},{10... | collective-permute-start | bytes 2696 | tf_op jit(solution)/shard_map/ppermute | solution.py:292
  21.3 28.6 %collective-permute-start.2 = (s32[16,14]{1,0:T(8,128)S(1)}, s32[16,14]{1,0:T(8,128)S(1)}, u32[]{:S(2)}, u32[]{:S(2)}) collective-permute-start(s32[16,14]{1,0:T(8,128)S(1)} %copy-done), channel_id=1, source_target_pairs={{0,24},{8,0},{16,8},{24,16},{1,25},{9,1},{17,9},{25,17},{2,26},{10... | collective-permute-start | bytes 2696 | tf_op jit(solution)/shard_map/ppermute | solution.py:292
  25.6 24.2 %collective-permute-start.3 = (s32[4]{0:T(128)S(1)}, s32[4]{0:T(128)S(1)}, u32[]{:S(2)}, u32[]{:S(2)}) collective-permute-start(s32[4]{0:T(128)S(1)} %slice_bitcast_fusion), channel_id=1, source_target_pairs={{32,0},{64,32},{96,64},{128,96},{160,128},{192,160},{224,192},{256... | collective-permute-start | bytes 56 | tf_op jit(solution)/shard_map/ppermute | solution.py:296
  53.4 59.0 %collective-permute-start.4 = (bf16[32,3,128,128]{3,2,1,0:T(8,128)(2,1)S(1)}, bf16[32,3,128,128]{3,2,1,0:T(8,128)(2,1)}, u32[]{:S(2)}, u32[]{:S(2)}) collective-permute-start(bf16[32,3,128,128]{3,2,1,0:T(8,128)(2,1)S(1)} %all-to-all-done.kinds.own), channel_id=1, source_target_pairs={{0,1},{1,0},{2,3},{3,2},{4,5},{5,4},{6,7},{7,6},{8,9},{9,8},{10,11... | collective-permute-start | bytes 9437192 | tf_op jit(solution)/shard_map/ppermute | solution.py:273
  94.0 8.1 %all-to-all-start.3 = ((bf16[4,128,128]{2,1,0:T(8,128)(2,1)}), bf16[4,128,128]{2,1,0:T(8,128)(2,1)S(1)}, u32[]{:S(2)}, u32[]{:S(2)}) async-start(bf16[4,128,128]{2,1,0:T(8,128)(2,1)} %broadcast_in_dim.5), calls=%async_computation.3 | async-start | bytes 262144 | tf_op jit(solution)/shard_map/all_to_all | solution.py:302
  102.1 24.1 %collective-permute-start.6 = (bf16[8,2,128,128]{3,2,1,0:T(8,128)(2,1)}, bf16[8,2,128,128]{3,2,1,0:T(8,128)(2,1)S(1)}, u32[]{:S(2)}, u32[]{:S(2)}) collective-permute-start(bf16[8,2,128,128]{3,2,1,0:T(8,128)(2,1)} %slice.7), channel_id=1, source_target_pairs={{0,32},{32,64},{64,96},{96,128},{128,160},{160,192},{192,224},{224... | collective-permute-start | bytes 1572872 | tf_op jit(solution)/shard_map/ppermute | solution.py:315
  105.0 7.3 %collective-permute-start.5 = (bf16[2,2,128,128]{3,2,1,0:T(8,128)(2,1)S(1)}, bf16[2,2,128,128]{3,2,1,0:T(8,128)(2,1)S(1)}, u32[]{:S(2)}, u32[]{:S(2)}) collective-permute-start(bf16[2,2,128,128]{3,2,1,0:T(8,128)(2,1)S(1)} %bitcast.21), channel_id=1, source_target_pairs={{0,1},{1,0},{2,3},{3,2},{4,5},{5,4},{6,7},{7,6},{8,9},{9,8},{10,11... | collective-permute-start | bytes 393224 | tf_op jit(solution)/shard_map/ppermute | solution.py:273
  126.2 3.8 %collective-permute-start.7 = (bf16[8,2,128,128]{3,2,1,0:T(8,128)(2,1)S(1)}, bf16[8,2,128,128]{3,2,1,0:T(8,128)(2,1)S(1)}, u32[]{:S(2)}, u32[]{:S(2)}) collective-permute-start(bf16[8,2,128,128]{3,2,1,0:T(8,128)(2,1)S(1)} %collective-permute-done.6.refs_0_), channel_id=1, source_target_pairs={{0,1},{1,0},{2,3},{3,2},{4,5},{5,4},{6,7},{7,6},{8,9},{9,8},{10,11... | collective-permute-start | bytes 1572872 | tf_op jit(solution)/shard_map/ppermute | solution.py:273

commit v6 on v5

v6 whole, which is shorter than its diff:
```python
import functools
import math

import jax
import jax.numpy as jnp
from jax import lax
from jax.experimental import pallas as pl
from jax.experimental.pallas import tpu as pltpu
from jax.sharding import Mesh
from jax.sharding import PartitionSpec as P

HEAD_DIM = 128
BLOCK = 128
WIN = 16
WSEL = 10
GLOBALS = 4
SLOTS = WSEL + GLOBALS
HEADS = 16
PLANE = 64
CHUNK = 16
FACTOR = math.log2(math.e) / math.sqrt(HEAD_DIM)
UNROLL = 4
PLANE_AXES = ("y", "x", "core")

SCALARS = pl.BlockSpec(memory_space=pltpu.SMEM)
WHOLE = pl.BlockSpec(memory_space=pltpu.VMEM)
LEFT = pl.BlockSpec(memory_space=pl.ANY)


def pack_kernel(queries, keys, values, out, sent, query_buf, key_buf, value_buf, arrived, sems):
    def moves():
        for head in range(HEADS):
            columns = pl.ds(head * HEAD_DIM, HEAD_DIM)
            yield 0, key_buf.at[:, :, columns], out.at[2 * head]
            yield 1, value_buf.at[:, :, columns], out.at[2 * head + 1]
            yield 2, query_buf.at[0, :, columns], sent.at[2 * head]
            yield 2, query_buf.at[1, :, columns], sent.at[2 * head + 1]

    loads = [
        pltpu.make_async_copy(source, target, arrived.at[at])
        for at, (source, target) in enumerate(
            [(keys, key_buf), (values, value_buf), (queries, query_buf)]
        )
    ]
    stores = [
        (array, pltpu.make_async_copy(source, target, sems.at[at]))
        for at, (array, source, target) in enumerate(moves())
    ]
    for load in loads:
        load.start()
    for at, load in enumerate(loads):
        load.wait()
        for array, store in stores:
            if array == at:
                store.start()
    for _, store in stores:
        store.wait()


def pack(*arrays):
    arrays = [array.reshape(2, BLOCK, HEADS * HEAD_DIM) for array in arrays]
    return pl.pallas_call(
        pack_kernel,
        out_shape=[
            jax.ShapeDtypeStruct((2 * HEADS, 2, BLOCK, HEAD_DIM), jnp.bfloat16),
            jax.ShapeDtypeStruct((2 * HEADS, BLOCK, HEAD_DIM), jnp.bfloat16),
        ],
        in_specs=[LEFT] * 3,
        out_specs=[LEFT] * 2,
        scratch_shapes=[pltpu.VMEM(array.shape, array.dtype) for array in arrays]
        + [pltpu.SemaphoreType.DMA((3,)), pltpu.SemaphoreType.DMA((4 * HEADS,))],
        compiler_params=pltpu.CompilerParams(vmem_limit_bytes=56 << 20),
        name="pack",
    )(*arrays)


def pick_kernel(where, rows, above, kinds, *refs):
    outs, (buffer, sems) = refs[:GLOBALS], refs[GLOBALS:]
    group, last = row_of(where, PLANE // 2 - 1, 1)
    copies, present = [], []
    for step in range(GLOBALS):
        slot = (where[3] + step) % GLOBALS
        place = jnp.maximum(rows[group, last, WSEL + slot], above[slot]) - where[1]
        held = (place >= 0) & (place < PLANE)
        place = jnp.where(held, place, 0)
        source = kinds.at[place // 2, place % 2]
        copies.append(pltpu.make_async_copy(source, buffer.at[step], sems.at[step]))
        present.append(held)
    for copy in copies:
        copy.start()
    for step in range(GLOBALS):
        copies[step].wait()
        block = buffer[step]
        outs[step][...] = jnp.where(present[step], block, jnp.zeros_like(block))


def pick_globals(where, rows, above, kinds):
    return pl.pallas_call(
        pick_kernel,
        out_shape=[jax.ShapeDtypeStruct((BLOCK, HEAD_DIM), jnp.bfloat16)] * GLOBALS,
        in_specs=[SCALARS, SCALARS, SCALARS, LEFT],
        out_specs=[WHOLE] * GLOBALS,
        scratch_shapes=[
            pltpu.VMEM((GLOBALS, BLOCK, HEAD_DIM), jnp.bfloat16),
            pltpu.SemaphoreType.DMA((GLOBALS,)),
        ],
        compiler_params=pltpu.CompilerParams(vmem_limit_bytes=12 << 20),
        name="pick_globals",
    )(where, rows, above, kinds)


def row_of(where, at, core):
    row = 2 * at + core
    return (where[2] + 4 - row // CHUNK) % 4, row % CHUNK


def two_blocks(blocks, one, two):
    return jnp.concatenate([blocks[one // 2, one % 2], blocks[two // 2, two % 2]], axis=0)


def attend_kernel(
    where, rows, query, own, other, halo_own, halo_other, global_own, global_other,
    out, keys, values, scores, weights, sems,
):
    core, first = where[0], where[1]
    chunks = PLANE // CHUNK
    global_at = PLANE + WIN

    def copies(own_to, other_to, at):
        if at < chunks:
            target = pl.ds(at * CHUNK // 2, CHUNK // 2)
            pairs = [(own.at[target], own_to), (other.at[target], other_to)]
        elif at == chunks:
            target = pl.ds(PLANE // 2, WIN // 2)
            pairs = [(halo_own, own_to), (halo_other, other_to)]
        else:
            target = pl.ds(global_at // 2, GLOBALS // 2)
            pairs = [(global_own, own_to), (global_other, other_to)]
        for kind, (array, to) in enumerate(pairs):
            yield pltpu.make_async_copy(array, to.at[target], sems.at[kind, at])

    needed = {0: [0, chunks, chunks + 1]}
    for part in range(1, chunks):
        needed.setdefault(part * CHUNK // (2 * UNROLL), []).append(part)
    parts = [part for step in sorted(needed) for part in needed[step]]

    @pl.when(core == 0)
    def _():
        for part in parts:
            for copy in copies(keys, values, part):
                copy.start()

    @pl.when(core != 0)
    def _():
        for part in parts:
            for copy in copies(values, keys, part):
                copy.start()

    causal = lax.broadcasted_iota(jnp.int32, (BLOCK, BLOCK), 0) >= lax.broadcasted_iota(
        jnp.int32, (BLOCK, BLOCK), 1
    )

    def place_of(at, slot):
        group, row = row_of(where, at, core)
        block_id = rows[group, row, slot]
        if slot < WSEL:
            place = block_id - first
            place = jnp.where(place >= 0, place, place + PLANE + WIN)
        else:
            place = global_at + (where[3] + SLOTS - slot) % GLOBALS
        return jnp.where(block_id >= 0, place, 0), block_id >= 0

    def score_phase(at, lane):
        block_query = query[at]
        highest = None
        for slot in range(0, SLOTS, 2):
            one, listed_one = place_of(at, slot)
            two, listed_two = place_of(at, slot + 1)
            both = lax.dot_general(
                block_query, two_blocks(keys, one, two), (((1,), (1,)), ((), ())),
                preferred_element_type=jnp.float32,
            )
            for part, listed in enumerate([listed_one, listed_two]):
                score = both[:, part * BLOCK : (part + 1) * BLOCK]
                if slot + part == 0:
                    score = jnp.where(causal, score, -1e30)
                else:
                    score = jnp.where(listed, score, -1e30)
                scores[lane, slot + part] = score
                highest = score if highest is None else jnp.maximum(highest, score)
        row_max = jnp.max(highest, axis=1, keepdims=True) * FACTOR
        return jnp.broadcast_to(row_max, (BLOCK, BLOCK))

    def weight_phase(lane, row_max):
        total = None
        for slot in range(SLOTS):
            weight = jnp.exp2(scores[lane, slot] * FACTOR - row_max)
            total = weight if total is None else total + weight
            weights[lane, :, slot * BLOCK : (slot + 1) * BLOCK] = weight.astype(jnp.bfloat16)
        return jnp.sum(total, axis=1, keepdims=True)

    def value_phase(at, lane, denom):
        mixed = None
        for slot in range(0, SLOTS, 2):
            one, two = place_of(at, slot)[0], place_of(at, slot + 1)[0]
            term = jnp.dot(
                weights[lane, :, slot * BLOCK : (slot + 2) * BLOCK],
                two_blocks(values, one, two),
                preferred_element_type=jnp.float32,
            )
            mixed = term if mixed is None else mixed + term
        out[at] = (mixed / denom).astype(jnp.bfloat16)

    def step(at, carry):
        for when, needs in needed.items():

            @pl.when(at == when)
            def _(needs=needs):
                for part in needs:
                    for copy in copies(keys, values, part):
                        copy.wait()

        at = at * UNROLL
        row_max, denom = score_phase(at, 0), None
        for lane in range(UNROLL):
            following = score_phase(at + lane + 1, lane + 1) if lane + 1 < UNROLL else None
            found = weight_phase(lane, row_max)
            if lane:
                value_phase(at + lane - 1, lane - 1, denom)
            row_max, denom = following, found
        value_phase(at + UNROLL - 1, UNROLL - 1, denom)
        return carry

    lax.fori_loop(0, query.shape[0] // UNROLL, step, 0)


def attend(where, rows, query, *blocks):
    span = PLANE + WIN + GLOBALS
    pairs = query.shape[0] * SLOTS * BLOCK * BLOCK
    return pl.pallas_call(
        attend_kernel,
        out_shape=jax.ShapeDtypeStruct(query.shape, jnp.bfloat16),
        in_specs=[SCALARS, SCALARS, WHOLE] + [LEFT] * len(blocks),
        out_specs=WHOLE,
        scratch_shapes=[
            pltpu.VMEM((span // 2, 2, BLOCK, HEAD_DIM), jnp.bfloat16),
            pltpu.VMEM((span // 2, 2, BLOCK, HEAD_DIM), jnp.bfloat16),
            pltpu.VMEM((UNROLL, SLOTS, BLOCK, BLOCK), jnp.float32),
            pltpu.VMEM((UNROLL, BLOCK, SLOTS * BLOCK), jnp.bfloat16),
            pltpu.SemaphoreType.DMA((2, PLANE // CHUNK + 2)),
        ],
        compiler_params=pltpu.CompilerParams(vmem_limit_bytes=24 << 20),
        cost_estimate=pl.CostEstimate(
            flops=4 * pairs * HEAD_DIM, bytes_accessed=8 << 20, transcendentals=pairs
        ),
        name="attend",
    )(where, rows, query, *blocks)


def swapped(value):
    return lax.ppermute(value, "core", [(0, 1), (1, 0)])


def added(*values):
    return sum(value.astype(jnp.float32) for value in values).astype(jnp.bfloat16)


def shards(queries, key_vectors, value_vectors, key_blocks):
    depth = lax.axis_size("z")
    breadth = lax.axis_size("y")
    up = [(at, at + 1) for at in range(depth - 1)]
    down = [(at + 1, at) for at in range(depth - 1)]
    level = lax.axis_index("z")
    where = jnp.stack(
        [lax.axis_index("core"), level * PLANE, lax.axis_index("y"), level % GLOBALS]
    )

    kinds, sent = pack(queries, key_vectors, value_vectors)
    own = lax.all_to_all(kinds, PLANE_AXES, 0, 0, tiled=True)

    rows = jnp.stack(
        [key_blocks]
        + [
            lax.ppermute(key_blocks, "y", [(at, (at + step) % breadth) for at in range(breadth)])
            for step in range(1, breadth)
        ]
    )
    above = lax.ppermute(key_blocks[-1, WSEL:], "z", down)
    own, rows, above = lax.optimization_barrier((own, rows, above))
    query = lax.all_to_all(sent, PLANE_AXES, 0, 0, tiled=True)
    other = swapped(own)

    def within(step):
        return [(at, at - at % GLOBALS + (at + step) % GLOBALS) for at in range(depth)]

    def across(step):
        return [(at, (at + GLOBALS * step) % depth) for at in range(depth)]

    parts = pick_globals(where, rows, above, own)
    last, mine = lax.optimization_barrier((own[-WIN // 2 :], parts[0]))
    held = added(
        mine, *[lax.ppermute(parts[step], "z", within(step)) for step in range(1, GLOBALS)]
    )
    halo_own = lax.ppermute(last, "z", up)
    held = added(
        held, *[lax.ppermute(held, "z", across(step)) for step in range(1, depth // GLOBALS)]
    )
    halo_own, held = lax.optimization_barrier((halo_own, held))
    shared = [lax.ppermute(held, "z", within(step)) for step in range(1, GLOBALS)]
    halo_other = swapped(halo_own)
    global_own = jnp.stack([held] + shared).reshape(GLOBALS // 2, 2, BLOCK, HEAD_DIM)
    global_other = swapped(global_own)
    context = attend(
        where, rows, query, own, other, halo_own, halo_other, global_own, global_other
    )
    back = lax.all_to_all(context, PLANE_AXES, 0, 0, tiled=True)
    return jnp.transpose(
        back.reshape(HEADS, 2, BLOCK, HEAD_DIM), (1, 2, 0, 3)
    ).reshape(queries.shape)


def solution(mesh):
    fine = Mesh(mesh.devices.reshape(-1, 4, 4, 2), ("z",) + PLANE_AXES)
    tokens = P(("z",) + PLANE_AXES, None)
    return jax.shard_map(
        shards,
        mesh=fine,
        in_specs=(tokens, tokens, tokens, P(("z", "y"), None)),
        out_specs=tokens,
        check_vma=False,
    )
```

time: 159 us -> 160 us (level)
  starting transfers between devices: 42.9 us -> 83.6 us
  blocking collectives: 54 us -> 24.1 us
  waiting for transfers between devices: 32.9 us -> 23.7 us
    ppermute x2 -> x11, starting transfers between devices: 4.19 us -> 46 us  [the longest x3 21.7 us: shards(): lax.ppermute(held, 'z', across(step))]
    all_to_all x2 -> x0, blocking collectives: 33.7 us -> none  [the longest x1 25.5 us: spread(): return lax.all_to_all(copies, axis, 0, 0, tiled=True)]
    ppermute x3, waiting for transfers between devices: 22.9 us -> 11.4 us  [shards(): lax.ppermute(key_blocks, 'y', [(at, (at + step) % breadth) for at in rang...]
    ppermute x2 -> x11, waiting for transfers between devices: 0.01 us -> 7.64 us  [the longest x3 4.25 us: shards(): lax.ppermute(held, 'z', within(step))]
    all_to_all x1, blocking collectives: 20.3 us -> 24.1 us  [shards(): back = lax.all_to_all(context, PLANE_AXES, 0, 0, tiled=True)]
    all_to_all x2, waiting for transfers between devices: 7.41 us -> 3.72 us  [the longest x1 3.72 us: shards(): own = lax.all_to_all(kinds, PLANE_AXES, 0, 0, tiled=True)]
    ppermute x3, starting transfers between devices: 13.4 us -> 11.2 us  [swapped(): return lax.ppermute(value, 'core', [(0, 1), (1, 0)])]
    pallas_call x4 -> x3, Pallas kernels: 25.1 us -> 24.9 us  [the longest x1 20.1 us: attend(): pl.pallas_call(attend_kernel, out_shape=jax.ShapeDtypeStruct(query.shape,...]
  transfers between devices with their start and end apart: 10 -> 19, of which waited for: 5 -> 7; matrix products, arithmetic and copies ran while one was open for 1% -> 1% of each run, Pallas kernels for 10% -> 1%
where the time goes in v6:
time: 160 us
  starting transfers between devices  83.6 us (52%)
  Pallas kernels  24.9 us (16%)
  blocking collectives  24.1 us (15%)
  waiting for transfers between devices  23.7 us (15%)
  local copies, waits for them, and re-layouts  2.84 us (2%)
    all_to_all x1, blocking collectives, shards(): back = lax.all_to_all(context, PLANE_AXES, 0, 0, tiled=True)  24.1 us
    ppermute x3, starting transfers between devices, shards(): lax.ppermute(held, 'z', across(step))  21.7 us
    pallas_call x1, Pallas kernels, attend(): pl.pallas_call(attend_kernel, out_shape=jax.ShapeDtypeStruct(query.shape,...  20.1 us
    ppermute x3, waiting for transfers between devices, shards(): lax.ppermute(key_blocks, 'y', [(at, (at + step) % breadth) for at in rang...  11.4 us
    ppermute x3, starting transfers between devices, shards(): lax.ppermute(key_blocks, 'y', [(at, (at + step) % breadth) for at in rang...  11.4 us
    ppermute x3, starting transfers between devices, swapped(): return lax.ppermute(value, 'core', [(0, 1), (1, 0)])  11.2 us
    ppermute x3, starting transfers between devices, shards(): lax.ppermute(parts[step], 'z', within(step))  10.8 us
    all_to_all x1, starting transfers between devices, shards(): own = lax.all_to_all(kinds, PLANE_AXES, 0, 0, tiled=True)  10.6 us
  transfers between devices with their start and end apart: 19, of which 7 were waited for; matrix products, arithmetic and copies ran while one was open for 1% of the time, Pallas kernels for 1%

profile of v6, /device:TPU:1, one launch (start us, length us, event | category | flops | bytes accessed | tf_op | source)
XLA Modules:
  0.0 159.6 jit_solution(17919454482021520008)
XLA Ops:
  0.0 3.4 %pack.1 = (bf16[32,2,128,128]{3,2,1,0:T(8,128)(2,1)}, bf16[32,128,128]{2,1,0:T(8,128)(2,1)}) custom-call(bf16[2,128,2048]{2,1,0:T(8,128)(2,1)} %bitcast.30, bf16[2,128,2048]{2,1,0:T(8,128)(2,1)} %bitcast.31, bf16[2,128,2048]{2,1,0:T(8,128)(2,1)} %bitcast.32), custom_call_target="tpu_custom_call" | custom-call | tf_op jit(solution)/shard_map/pack/pallas_call | solution.py:62
  3.4 0.0 copy-start
  3.5 10.6 %all-to-all-start = ((bf16[32,2,128,128]{3,2,1,0:T(8,128)(2,1)}), bf16[32,2,128,128]{3,2,1,0:T(8,128)(2,1)S(1)}, u32[]{:S(2)}, u32[]{:S(2)}) async-start(bf16[32,2,128,128]{3,2,1,0:T(8,128)(2,1)} %get-tuple-element.18), calls=%async_computation | async-start | bytes 4194304 | tf_op jit(solution)/shard_map/all_to_all | solution.py:279
  14.0 4.9 %collective-permute-start.1 = (s32[16,14]{1,0:T(8,128)S(1)}, s32[16,14]{1,0:T(8,128)S(1)}, u32[]{:S(2)}, u32[]{:S(2)}) collective-permute-start(s32[16,14]{1,0:T(8,128)S(1)} %copy-done), channel_id=1, source_target_pairs={{0,16},{8,24},{16,0},{24,8},{1,17},{9,25},{17,1},{25,9},{2,18},{10... | collective-permute-start | bytes 2696 | tf_op jit(solution)/shard_map/ppermute | solution.py:284
  18.9 2.2 %collective-permute-start = (s32[16,14]{1,0:T(8,128)S(1)}, s32[16,14]{1,0:T(8,128)S(1)}, u32[]{:S(2)}, u32[]{:S(2)}) collective-permute-start(s32[16,14]{1,0:T(8,128)S(1)} %copy-done), channel_id=1, source_target_pairs={{0,8},{8,16},{16,24},{24,0},{1,9},{9,17},{17,25},{25,1},{2,10},{10... | collective-permute-start | bytes 2696 | tf_op jit(solution)/shard_map/ppermute | solution.py:284
  21.2 4.2 %collective-permute-start.2 = (s32[16,14]{1,0:T(8,128)S(1)}, s32[16,14]{1,0:T(8,128)S(1)}, u32[]{:S(2)}, u32[]{:S(2)}) collective-permute-start(s32[16,14]{1,0:T(8,128)S(1)} %copy-done), channel_id=1, source_target_pairs={{0,24},{8,0},{16,8},{24,16},{1,25},{9,1},{17,9},{25,17},{2,26},{10... | collective-permute-start | bytes 2696 | tf_op jit(solution)/shard_map/ppermute | solution.py:284
  25.4 0.1 slice_bitcast_fusion
  25.5 1.3 collective-permute-start.3
  26.8 11.4 %collective-permute-done.1 = s32[16,14]{1,0:T(8,128)S(1)} collective-permute-done((s32[16,14]{1,0:T(8,128)S(1)}, s32[16,14]{1,0:T(8,128)S(1)}, u32[]{:S(2)}, u32[]{:S(2)}) %collective-permute-start.1) | collective-permute-done | bytes 928 | tf_op jit(solution)/shard_map/ppermute | solution.py:284
  38.2 0.0 collective-permute-done
  38.2 0.0 collective-permute-done.2
  38.2 0.0 collective-permute-done.3.above
  38.2 3.7 %all-to-all-done.kinds.own = bf16[32,2,128,128]{3,2,1,0:T(8,128)(2,1)S(1)} async-done(((bf16[32,2,128,128]{3,2,1,0:T(8,128)(2,1)}), bf16[32,2,128,128]{3,2,1,0:T(8,128)(2,1)S(1)}, u32[]{:S(2)}, u32[]{:S(2)}) %all-to-all-start) | async-done | bytes 2097184 | tf_op jit(solution)/shard_map/all_to_all | solution.py:279
  42.0 4.3 %collective-permute-start.4 = (bf16[32,2,128,128]{3,2,1,0:T(8,128)(2,1)S(1)}, bf16[32,2,128,128]{3,2,1,0:T(8,128)(2,1)}, u32[]{:S(2)}, u32[]{:S(2)}) collective-permute-start(bf16[32,2,128,128]{3,2,1,0:T(8,128)(2,1)S(1)} %all-to-all-done.kinds.own), channel_id=1, source_target_pairs={{0,1},{1,0},{2,3},{3,2},{4,5},{5,4},{6,7},{7,6},{8,9},{9,8},{10,11... | collective-permute-start | bytes 6291464 | tf_op jit(solution)/shard_map/ppermute | solution.py:261
  46.3 0.1 pad_add_fusion.1.where
  46.3 0.8 slice.7
  47.2 1.4 pick_globals.1
  48.6 2.3 %collective-permute-start.5 = (bf16[8,2,128,128]{3,2,1,0:T(8,128)(2,1)}, bf16[8,2,128,128]{3,2,1,0:T(8,128)(2,1)}, u32[]{:S(2)}, u32[]{:S(2)}) collective-permute-start(bf16[8,2,128,128]{3,2,1,0:T(8,128)(2,1)} %slice.7), channel_id=1, source_target_pairs={{0,32},{32,64},{64,96},{96,128},{128,160},{160,192},{192,224},{224... | collective-permute-start | bytes 1572872 | tf_op jit(solution)/shard_map/ppermute | solution.py:304
  50.9 2.8 %collective-permute-start.6 = (bf16[128,128]{1,0:T(8,128)(2,1)S(1)}, bf16[128,128]{1,0:T(8,128)(2,1)S(1)}, u32[]{:S(2)}, u32[]{:S(2)}) collective-permute-start(bf16[128,128]{1,0:T(8,128)(2,1)S(1)} %get-tuple-element.26), channel_id=1, source_target_pairs={{0,32},{32,64},{64,96},{96,0},{128,160},{160,192},{192,224},{224,1... | collective-permute-start | bytes 98312 | tf_op jit(solution)/shard_map/ppermute | solution.py:302
  53.6 6.1 %collective-permute-start.7 = (bf16[128,128]{1,0:T(8,128)(2,1)S(1)}, bf16[128,128]{1,0:T(8,128)(2,1)S(1)}, u32[]{:S(2)}, u32[]{:S(2)}) collective-permute-start(bf16[128,128]{1,0:T(8,128)(2,1)S(1)} %get-tuple-element.27), channel_id=1, source_target_pairs={{0,64},{32,96},{64,0},{96,32},{128,192},{160,224},{192,128},{224,1... | collective-permute-start | bytes 98312 | tf_op jit(solution)/shard_map/ppermute | solution.py:302
  59.7 1.9 %collective-permute-start.8 = (bf16[128,128]{1,0:T(8,128)(2,1)S(1)}, bf16[128,128]{1,0:T(8,128)(2,1)S(1)}, u32[]{:S(2)}, u32[]{:S(2)}) collective-permute-start(bf16[128,128]{1,0:T(8,128)(2,1)S(1)} %get-tuple-element.28), channel_id=1, source_target_pairs={{0,96},{32,0},{64,32},{96,64},{128,224},{160,128},{192,160},{224,1... | collective-permute-start | bytes 98312 | tf_op jit(solution)/shard_map/ppermute | solution.py:302
  61.7 4.4 %all-to-all-start.1 = ((bf16[32,128,128]{2,1,0:T(8,128)(2,1)}), bf16[32,128,128]{2,1,0:T(8,128)(2,1)S(1)}, u32[]{:S(2)}, u32[]{:S(2)}) async-start(bf16[32,128,128]{2,1,0:T(8,128)(2,1)} %get-tuple-element.20), calls=%async_computation.1 | async-start | bytes 2097152 | tf_op jit(solution)/shard_map/all_to_all | solution.py:290
  66.1 0.0 collective-permute-done.6
  66.1 0.0 collective-permute-done.7
  66.1 0.0 collective-permute-done.8
  66.2 9.5 %collective-permute-start.11 = (bf16[128,128]{1,0:T(8,128)(2,1)S(1)}, bf16[128,128]{1,0:T(8,128)(2,1)S(1)}, u32[]{:S(2)}, u32[]{:S(2)}) collective-permute-start(bf16[128,128]{1,0:T(8,128)(2,1)S(1)} %add_convert_fusion.1), channel_id=1, source_target_pairs={{0,384},{32,416},{64,448},{96,480},{128,0},{160,32},{192,64},{224,... | collective-permute-start | bytes 98312 | tf_op jit(solution)/shard_map/ppermute | solution.py:306
  75.7 6.3 %collective-permute-start.10 = (bf16[128,128]{1,0:T(8,128)(2,1)S(1)}, bf16[128,128]{1,0:T(8,128)(2,1)S(1)}, u32[]{:S(2)}, u32[]{:S(2)}) collective-permute-start(bf16[128,128]{1,0:T(8,128)(2,1)S(1)} %add_convert_fusion.1), channel_id=1, source_target_pairs={{0,256},{32,288},{64,320},{96,352},{128,384},{160,416},{192,448},{... | collective-permute-start | bytes 98312 | tf_op jit(solution)/shard_map/ppermute | solution.py:306
  82.0 5.9 %collective-permute-start.9 = (bf16[128,128]{1,0:T(8,128)(2,1)S(1)}, bf16[128,128]{1,0:T(8,128)(2,1)S(1)}, u32[]{:S(2)}, u32[]{:S(2)}) collective-permute-start(bf16[128,128]{1,0:T(8,128)(2,1)S(1)} %add_convert_fusion.1), channel_id=1, source_target_pairs={{0,128},{32,160},{64,192},{96,224},{128,256},{160,288},{192,320},{... | collective-permute-start | bytes 98312 | tf_op jit(solution)/shard_map/ppermute | solution.py:306
  87.9 0.0 collective-permute-done.11
  87.9 1.2 collective-permute-done.10
  89.1 2.2 %collective-permute-done.9 = bf16[128,128]{1,0:T(8,128)(2,1)S(1)} collective-permute-done((bf16[128,128]{1,0:T(8,128)(2,1)S(1)}, bf16[128,128]{1,0:T(8,128)(2,1)S(1)}, u32[]{:S(2)}, u32[]{:S(2)}) %collective-permute-start.9) | collective-permute-done | bytes 32800 | tf_op jit(solution)/shard_map/ppermute | solution.py:306
  91.3 0.0 collective-permute-done.5.halo_own
  91.4 3.6 %collective-permute-start.12 = (bf16[8,2,128,128]{3,2,1,0:T(8,128)(2,1)}, bf16[8,2,128,128]{3,2,1,0:T(8,128)(2,1)}, u32[]{:S(2)}, u32[]{:S(2)}) collective-permute-start(bf16[8,2,128,128]{3,2,1,0:T(8,128)(2,1)} %collective-permute-done.5.halo_own), channel_id=1, source_target_pairs={{0,1},{1,0},{2,3},{3,2},{4,5},{5,4},{6,7},{7,6},{8,9},{9,8},{10,11... | collective-permute-start | bytes 1572872 | tf_op jit(solution)/shard_map/ppermute | solution.py:261
  94.9 5.8 %collective-permute-start.15 = (bf16[128,128]{1,0:T(8,128)(2,1)S(1)}, bf16[128,128]{1,0:T(8,128)(2,1)S(1)}, u32[]{:S(2)}, u32[]{:S(2)}) collective-permute-start(bf16[128,128]{1,0:T(8,128)(2,1)S(1)} %add_convert_fusion), channel_id=1, source_target_pairs={{0,96},{32,0},{64,32},{96,64},{128,224},{160,128},{192,160},{224,1... | collective-permute-start | bytes 98312 | tf_op jit(solution)/shard_map/ppermute | solution.py:309
  100.8 1.9 %collective-permute-start.14 = (bf16[128,128]{1,0:T(8,128)(2,1)S(1)}, bf16[128,128]{1,0:T(8,128)(2,1)S(1)}, u32[]{:S(2)}, u32[]{:S(2)}) collective-permute-start(bf16[128,128]{1,0:T(8,128)(2,1)S(1)} %add_convert_fusion), channel_id=1, source_target_pairs={{0,64},{32,96},{64,0},{96,32},{128,192},{160,224},{192,128},{224,1... | collective-permute-start | bytes 98312 | tf_op jit(solution)/shard_map/ppermute | solution.py:309
  102.7 2.2 %collective-permute-start.13 = (bf16[128,128]{1,0:T(8,128)(2,1)S(1)}, bf16[128,128]{1,0:T(8,128)(2,1)S(1)}, u32[]{:S(2)}, u32[]{:S(2)}) collective-permute-start(bf16[128,128]{1,0:T(8,128)(2,1)S(1)} %add_convert_fusion), channel_id=1, source_target_pairs={{0,32},{32,64},{64,96},{96,0},{128,160},{160,192},{192,224},{224,1... | collective-permute-start | bytes 98312 | tf_op jit(solution)/shard_map/ppermute | solution.py:309
  104.9 0.0 collective-permute-done.15
  104.9 1.4 collective-permute-done.14
  106.3 2.8 %collective-permute-done.13 = bf16[128,128]{1,0:T(8,128)(2,1)S(1)} collective-permute-done((bf16[128,128]{1,0:T(8,128)(2,1)S(1)}, bf16[128,128]{1,0:T(8,128)(2,1)S(1)}, u32[]{:S(2)}, u32[]{:S(2)}) %collective-permute-start.13) | collective-permute-done | bytes 32800 | tf_op jit(solution)/shard_map/ppermute | solution.py:309
  109.2 3.4 %collective-permute-start.16 = (bf16[2,2,128,128]{3,2,1,0:T(8,128)(2,1)S(1)}, bf16[2,2,128,128]{3,2,1,0:T(8,128)(2,1)S(1)}, u32[]{:S(2)}, u32[]{:S(2)}) collective-permute-start(bf16[2,2,128,128]{3,2,1,0:T(8,128)(2,1)S(1)} %bitcast.26), channel_id=1, source_target_pairs={{0,1},{1,0},{2,3},{3,2},{4,5},{5,4},{6,7},{7,6},{8,9},{9,8},{10,11... | collective-permute-start | bytes 393224 | tf_op jit(solution)/shard_map/ppermute | solution.py:261
  112.5 0.0 all-to-all-done.1.query
  112.5 1.0 collective-permute-done.16.global_other
  113.5 0.0 collective-permute-done.12.halo_other
  113.5 0.0 collective-permute-done.4.other
  113.5 20.1 %attend.1 = bf16[32,128,128]{2,1,0:T(8,128)(2,1)S(1)} custom-call(s32[4]{0:T(128)S(1)} %pad_add_fusion.1.where, s32[4,16,14]{2,1,0:T(8,128)S(1)} %pad_add_fusion.rows, bf16[32,128,128]{2,1,0:T(8,128)(2,1)S(1)} %all-to-all-done.1.query, bf16[32,2,128,128]{3,2,1,0:T(8,128)(2,1)S(1)} %all-to-all-done.kinds.own, ...), custom_call_target="tpu_custom_call" | custom-call | flops 3758096384 | bytes 8388608 | tf_op jit(solution)/shard_map/attend/pallas_call | solution.py:240
  133.6 24.1 %all_to_all.15 = bf16[32,128,128]{2,1,0:T(8,128)(2,1)S(1)} all-to-all(bf16[32,128,128]{2,1,0:T(8,128)(2,1)S(1)} %attend.1), channel_id=1, replica_groups=mesh['z'=16,'y'=4,'x'=4,'core'=2] {'y','x','core'}, dimensions={0} | all-to-all | bytes 2097152 | tf_op jit(solution)/shard_map/all_to_all | solution.py:316
  157.7 0.7 copy.5
  158.4 1.2 copy.8
  (5 shorter events, 0.1 us)
Async XLA Ops:
  3.4 10.6 %copy-start = (s32[16,14]{1,0:T(8,128)S(1)}, s32[16,14]{1,0:T(8,128)}, u32[]{:S(2)}) copy-start(s32[16,14]{1,0:T(8,128)} %param.7) | copy-start | bytes 2692
  3.5 38.5 %all-to-all-start = ((bf16[32,2,128,128]{3,2,1,0:T(8,128)(2,1)}), bf16[32,2,128,128]{3,2,1,0:T(8,128)(2,1)S(1)}, u32[]{:S(2)}, u32[]{:S(2)}) async-start(bf16[32,2,128,128]{3,2,1,0:T(8,128)(2,1)} %get-tuple-element.18), calls=%async_computation | async-start | bytes 4194304 | tf_op jit(solution)/shard_map/all_to_all | solution.py:279
  14.0 24.2 %collective-permute-start.1 = (s32[16,14]{1,0:T(8,128)S(1)}, s32[16,14]{1,0:T(8,128)S(1)}, u32[]{:S(2)}, u32[]{:S(2)}) collective-permute-start(s32[16,14]{1,0:T(8,128)S(1)} %copy-done), channel_id=1, source_target_pairs={{0,16},{8,24},{16,0},{24,8},{1,17},{9,25},{17,1},{25,9},{2,18},{10... | collective-permute-start | bytes 2696 | tf_op jit(solution)/shard_map/ppermute | solution.py:284
  18.9 19.3 %collective-permute-start = (s32[16,14]{1,0:T(8,128)S(1)}, s32[16,14]{1,0:T(8,128)S(1)}, u32[]{:S(2)}, u32[]{:S(2)}) collective-permute-start(s32[16,14]{1,0:T(8,128)S(1)} %copy-done), channel_id=1, source_target_pairs={{0,8},{8,16},{16,24},{24,0},{1,9},{9,17},{17,25},{25,1},{2,10},{10... | collective-permute-start | bytes 2696 | tf_op jit(solution)/shard_map/ppermute | solution.py:284
  21.2 17.0 %collective-permute-start.2 = (s32[16,14]{1,0:T(8,128)S(1)}, s32[16,14]{1,0:T(8,128)S(1)}, u32[]{:S(2)}, u32[]{:S(2)}) collective-permute-start(s32[16,14]{1,0:T(8,128)S(1)} %copy-done), channel_id=1, source_target_pairs={{0,24},{8,0},{16,8},{24,16},{1,25},{9,1},{17,9},{25,17},{2,26},{10... | collective-permute-start | bytes 2696 | tf_op jit(solution)/shard_map/ppermute | solution.py:284
  25.5 12.7 %collective-permute-start.3 = (s32[4]{0:T(128)S(1)}, s32[4]{0:T(128)S(1)}, u32[]{:S(2)}, u32[]{:S(2)}) collective-permute-start(s32[4]{0:T(128)S(1)} %slice_bitcast_fusion), channel_id=1, source_target_pairs={{32,0},{64,32},{96,64},{128,96},{160,128},{192,160},{224,192},{256... | collective-permute-start | bytes 56 | tf_op jit(solution)/shard_map/ppermute | solution.py:288
  42.0 71.5 %collective-permute-start.4 = (bf16[32,2,128,128]{3,2,1,0:T(8,128)(2,1)S(1)}, bf16[32,2,128,128]{3,2,1,0:T(8,128)(2,1)}, u32[]{:S(2)}, u32[]{:S(2)}) collective-permute-start(bf16[32,2,128,128]{3,2,1,0:T(8,128)(2,1)S(1)} %all-to-all-done.kinds.own), channel_id=1, source_target_pairs={{0,1},{1,0},{2,3},{3,2},{4,5},{5,4},{6,7},{7,6},{8,9},{9,8},{10,11... | collective-permute-start | bytes 6291464 | tf_op jit(solution)/shard_map/ppermute | solution.py:261
  48.6 42.8 %collective-permute-start.5 = (bf16[8,2,128,128]{3,2,1,0:T(8,128)(2,1)}, bf16[8,2,128,128]{3,2,1,0:T(8,128)(2,1)}, u32[]{:S(2)}, u32[]{:S(2)}) collective-permute-start(bf16[8,2,128,128]{3,2,1,0:T(8,128)(2,1)} %slice.7), channel_id=1, source_target_pairs={{0,32},{32,64},{64,96},{96,128},{128,160},{160,192},{192,224},{224... | collective-permute-start | bytes 1572872 | tf_op jit(solution)/shard_map/ppermute | solution.py:304
  50.9 15.3 %collective-permute-start.6 = (bf16[128,128]{1,0:T(8,128)(2,1)S(1)}, bf16[128,128]{1,0:T(8,128)(2,1)S(1)}, u32[]{:S(2)}, u32[]{:S(2)}) collective-permute-start(bf16[128,128]{1,0:T(8,128)(2,1)S(1)} %get-tuple-element.26), channel_id=1, source_target_pairs={{0,32},{32,64},{64,96},{96,0},{128,160},{160,192},{192,224},{224,1... | collective-permute-start | bytes 98312 | tf_op jit(solution)/shard_map/ppermute | solution.py:302
  53.6 12.5 %collective-permute-start.7 = (bf16[128,128]{1,0:T(8,128)(2,1)S(1)}, bf16[128,128]{1,0:T(8,128)(2,1)S(1)}, u32[]{:S(2)}, u32[]{:S(2)}) collective-permute-start(bf16[128,128]{1,0:T(8,128)(2,1)S(1)} %get-tuple-element.27), channel_id=1, source_target_pairs={{0,64},{32,96},{64,0},{96,32},{128,192},{160,224},{192,128},{224,1... | collective-permute-start | bytes 98312 | tf_op jit(solution)/shard_map/ppermute | solution.py:302
  59.7 6.4 %collective-permute-start.8 = (bf16[128,128]{1,0:T(8,128)(2,1)S(1)}, bf16[128,128]{1,0:T(8,128)(2,1)S(1)}, u32[]{:S(2)}, u32[]{:S(2)}) collective-permute-start(bf16[128,128]{1,0:T(8,128)(2,1)S(1)} %get-tuple-element.28), channel_id=1, source_target_pairs={{0,96},{32,0},{64,32},{96,64},{128,224},{160,128},{192,160},{224,1... | collective-permute-start | bytes 98312 | tf_op jit(solution)/shard_map/ppermute | solution.py:302
  61.7 50.9 %all-to-all-start.1 = ((bf16[32,128,128]{2,1,0:T(8,128)(2,1)}), bf16[32,128,128]{2,1,0:T(8,128)(2,1)S(1)}, u32[]{:S(2)}, u32[]{:S(2)}) async-start(bf16[32,128,128]{2,1,0:T(8,128)(2,1)} %get-tuple-element.20), calls=%async_computation.1 | async-start | bytes 2097152 | tf_op jit(solution)/shard_map/all_to_all | solution.py:290
  66.2 21.7 %collective-permute-start.11 = (bf16[128,128]{1,0:T(8,128)(2,1)S(1)}, bf16[128,128]{1,0:T(8,128)(2,1)S(1)}, u32[]{:S(2)}, u32[]{:S(2)}) collective-permute-start(bf16[128,128]{1,0:T(8,128)(2,1)S(1)} %add_convert_fusion.1), channel_id=1, source_target_pairs={{0,384},{32,416},{64,448},{96,480},{128,0},{160,32},{192,64},{224,... | collective-permute-start | bytes 98312 | tf_op jit(solution)/shard_map/ppermute | solution.py:306
  75.7 13.4 %collective-permute-start.10 = (bf16[128,128]{1,0:T(8,128)(2,1)S(1)}, bf16[128,128]{1,0:T(8,128)(2,1)S(1)}, u32[]{:S(2)}, u32[]{:S(2)}) collective-permute-start(bf16[128,128]{1,0:T(8,128)(2,1)S(1)} %add_convert_fusion.1), channel_id=1, source_target_pairs={{0,256},{32,288},{64,320},{96,352},{128,384},{160,416},{192,448},{... | collective-permute-start | bytes 98312 | tf_op jit(solution)/shard_map/ppermute | solution.py:306
  82.0 9.3 %collective-permute-start.9 = (bf16[128,128]{1,0:T(8,128)(2,1)S(1)}, bf16[128,128]{1,0:T(8,128)(2,1)S(1)}, u32[]{:S(2)}, u32[]{:S(2)}) collective-permute-start(bf16[128,128]{1,0:T(8,128)(2,1)S(1)} %add_convert_fusion.1), channel_id=1, source_target_pairs={{0,128},{32,160},{64,192},{96,224},{128,256},{160,288},{192,320},{... | collective-permute-start | bytes 98312 | tf_op jit(solution)/shard_map/ppermute | solution.py:306
  91.4 22.2 %collective-permute-start.12 = (bf16[8,2,128,128]{3,2,1,0:T(8,128)(2,1)}, bf16[8,2,128,128]{3,2,1,0:T(8,128)(2,1)}, u32[]{:S(2)}, u32[]{:S(2)}) collective-permute-start(bf16[8,2,128,128]{3,2,1,0:T(8,128)(2,1)} %collective-permute-done.5.halo_own), channel_id=1, source_target_pairs={{0,1},{1,0},{2,3},{3,2},{4,5},{5,4},{6,7},{7,6},{8,9},{9,8},{10,11... | collective-permute-start | bytes 1572872 | tf_op jit(solution)/shard_map/ppermute | solution.py:261
  94.9 10.0 %collective-permute-start.15 = (bf16[128,128]{1,0:T(8,128)(2,1)S(1)}, bf16[128,128]{1,0:T(8,128)(2,1)S(1)}, u32[]{:S(2)}, u32[]{:S(2)}) collective-permute-start(bf16[128,128]{1,0:T(8,128)(2,1)S(1)} %add_convert_fusion), channel_id=1, source_target_pairs={{0,96},{32,0},{64,32},{96,64},{128,224},{160,128},{192,160},{224,1... | collective-permute-start | bytes 98312 | tf_op jit(solution)/shard_map/ppermute | solution.py:309
  100.8 5.6 %collective-permute-start.14 = (bf16[128,128]{1,0:T(8,128)(2,1)S(1)}, bf16[128,128]{1,0:T(8,128)(2,1)S(1)}, u32[]{:S(2)}, u32[]{:S(2)}) collective-permute-start(bf16[128,128]{1,0:T(8,128)(2,1)S(1)} %add_convert_fusion), channel_id=1, source_target_pairs={{0,64},{32,96},{64,0},{96,32},{128,192},{160,224},{192,128},{224,1... | collective-permute-start | bytes 98312 | tf_op jit(solution)/shard_map/ppermute | solution.py:309
  102.7 6.5 %collective-permute-start.13 = (bf16[128,128]{1,0:T(8,128)(2,1)S(1)}, bf16[128,128]{1,0:T(8,128)(2,1)S(1)}, u32[]{:S(2)}, u32[]{:S(2)}) collective-permute-start(bf16[128,128]{1,0:T(8,128)(2,1)S(1)} %add_convert_fusion), channel_id=1, source_target_pairs={{0,32},{32,64},{64,96},{96,0},{128,160},{160,192},{192,224},{224,1... | collective-permute-start | bytes 98312 | tf_op jit(solution)/shard_map/ppermute | solution.py:309
  109.2 4.3 %collective-permute-start.16 = (bf16[2,2,128,128]{3,2,1,0:T(8,128)(2,1)S(1)}, bf16[2,2,128,128]{3,2,1,0:T(8,128)(2,1)S(1)}, u32[]{:S(2)}, u32[]{:S(2)}) collective-permute-start(bf16[2,2,128,128]{3,2,1,0:T(8,128)(2,1)S(1)} %bitcast.26), channel_id=1, source_target_pairs={{0,1},{1,0},{2,3},{3,2},{4,5},{5,4},{6,7},{7,6},{8,9},{9,8},{10,11... | collective-permute-start | bytes 393224 | tf_op jit(solution)/shard_map/ppermute | solution.py:261

commit v7 on v5

--- a/solution.py
+++ b/solution.py
@@ -21,7 +21,6 @@
 FACTOR = math.log2(math.e) / math.sqrt(HEAD_DIM)
 UNROLL = 4
 PLANE_AXES = ("y", "x", "core")
-Z_AXES = ("far", "near")
 
 SCALARS = pl.BlockSpec(memory_space=pltpu.SMEM)
 WHOLE = pl.BlockSpec(memory_space=pltpu.VMEM)
@@ -274,12 +273,12 @@
 
 
 def shards(queries, key_vectors, value_vectors, key_blocks):
-    depth = lax.axis_size(Z_AXES)
+    depth = lax.axis_size("z")
     breadth = lax.axis_size("y")
     up = [(at, at + 1) for at in range(depth - 1)]
     down = [(at + 1, at) for at in range(depth - 1)]
     where = jnp.stack(
-        [lax.axis_index("core"), lax.axis_index(Z_AXES) * PLANE, lax.axis_index("y")]
+        [lax.axis_index("core"), lax.axis_index("z") * PLANE, lax.axis_index("y")]
     )
 
     received = lax.all_to_all(
@@ -293,26 +292,19 @@
             for step in range(1, breadth)
         ]
     )
-    above = lax.ppermute(key_blocks[-1, WSEL:], Z_AXES, down)
+    above = lax.ppermute(key_blocks[-1, WSEL:], "z", down)
     own, rows, above = lax.optimization_barrier((received, rows, above))
     other = swapped(own)
 
-    def spread(value, axis):
-        copies = jnp.broadcast_to(value[None], (GLOBALS,) + value.shape)
-        return lax.all_to_all(copies, axis, 0, 0, tiled=True)
-
-    def summed(values):
-        return jnp.sum(values.astype(jnp.float32), axis=0).astype(jnp.bfloat16)
-
-    part = pick_globals(where, rows, above, own)
-    held = summed(lax.all_to_all(part, "near", 0, 0, tiled=True))
-    held = summed(spread(held, "far"))
-    global_own = spread(held, "near")
+    part = pick_globals(where, rows, above, own).reshape(depth, -1, HEAD_DIM)
+    pieces = lax.all_to_all(part, "z", 0, 0, tiled=True)
+    summed = jnp.sum(pieces.astype(jnp.float32), axis=0, keepdims=True).astype(jnp.bfloat16)
+    global_own = lax.all_to_all(jnp.broadcast_to(summed, part.shape), "z", 0, 0, tiled=True)
     last, global_own = lax.optimization_barrier((own[-WIN // 2 :, :2], global_own))
     pair = (GLOBALS // 2, 2, BLOCK, HEAD_DIM)
     global_own = global_own.reshape(pair)
     global_other = swapped(global_own)
-    halo_own = lax.ppermute(last, Z_AXES, up)
+    halo_own = lax.ppermute(last, "z", up)
     rest = attend(
         WIN // 2, PLANE, where, rows, own, other, global_own, global_other
     )
@@ -328,12 +320,12 @@
 
 
 def solution(mesh):
-    fine = Mesh(mesh.devices.reshape(-1, GLOBALS, 4, 4, 2), Z_AXES + PLANE_AXES)
-    tokens = P(Z_AXES + PLANE_AXES, None)
+    fine = Mesh(mesh.devices.reshape(-1, 4, 4, 2), ("z",) + PLANE_AXES)
+    tokens = P(("z",) + PLANE_AXES, None)
     return jax.shard_map(
         shards,
         mesh=fine,
-        in_specs=(tokens, tokens, tokens, P(Z_AXES + ("y",), None)),
+        in_specs=(tokens, tokens, tokens, P(("z", "y"), None)),
         out_specs=tokens,
         check_vma=False,
     )

time: 159 us -> 161 us (1.013)
  blocking collectives: 54 us -> 45.3 us
  waiting for transfers between devices: 32.9 us -> 40.1 us
  starting transfers between devices: 42.9 us -> 45.6 us
    all_to_all x2 -> x1, blocking collectives: 33.7 us -> 25 us  [shards(): pieces = lax.all_to_all(part, 'z', 0, 0, tiled=True)]
    all_to_all x1, waiting for transfers between devices: 3.89 us -> 11.2 us  [shards(): lax.all_to_all(jnp.broadcast_to(summed, part.shape), 'z', 0, 0, tiled=True)]
    all_to_all x1, starting transfers between devices: 3.32 us -> 6.16 us  [shards(): lax.all_to_all(jnp.broadcast_to(summed, part.shape), 'z', 0, 0, tiled=True)]
where the time goes in v7:
time: 161 us; the launch traced here: 160 us
  starting transfers between devices  45.6 us (28%)
  blocking collectives  45.3 us (28%)
  waiting for transfers between devices  40.1 us (25%)
  Pallas kernels  25.1 us (16%)
  local copies, waits for them, and re-layouts  3.52 us (2%)
    all_to_all x1, blocking collectives, shards(): pieces = lax.all_to_all(part, 'z', 0, 0, tiled=True)  25 us
    ppermute x3, waiting for transfers between devices, shards(): lax.ppermute(key_blocks, 'y', [(at, (at + step) % breadth) for at in rang...  22.9 us
    all_to_all x1, blocking collectives, shards(): back = lax.all_to_all(context, PLANE_AXES, 0, 0, tiled=True)  20.3 us
    pallas_call x2, Pallas kernels, attend(): pl.pallas_call(functools.partial(attend_kernel, start, high, kept), out_s...  20.3 us
    ppermute x3, starting transfers between devices, swapped(): return lax.ppermute(value, 'core', [(0, 1), (1, 0)])  12.4 us
    ppermute x3, starting transfers between devices, shards(): lax.ppermute(key_blocks, 'y', [(at, (at + step) % breadth) for at in rang...  11.4 us
    all_to_all x1, waiting for transfers between devices, shards(): lax.all_to_all(jnp.broadcast_to(summed, part.shape), 'z', 0, 0, tiled=True)  11.2 us
    all_to_all x1, starting transfers between devices, shards(): lax.all_to_all(pack(queries, key_vectors, value_vectors), PLANE_AXES, 0,...  10.6 us
  transfers between devices with their start and end apart: 10, of which 5 were waited for; matrix products, arithmetic and copies ran while one was open for 1% of the time, Pallas kernels for 10%

profile of v7, /device:TPU:1, one launch (start us, length us, event | category | flops | bytes accessed | tf_op | source)
XLA Modules:
  0.0 159.9 jit_solution(14151052074695157268)
XLA Ops:
  0.0 3.5 %pack.1 = bf16[32,3,128,128]{3,2,1,0:T(8,128)(2,1)} custom-call(bf16[2,128,2048]{2,1,0:T(8,128)(2,1)} %bitcast.28, bf16[2,128,2048]{2,1,0:T(8,128)(2,1)} %bitcast.29, bf16[2,128,2048]{2,1,0:T(8,128)(2,1)} %bitcast.30), custom_call_target="tpu_custom_call" | custom-call | tf_op jit(solution)/shard_map/pack/pallas_call | solution.py:62
  3.5 0.0 copy-start
  3.5 10.6 %all-to-all-start = ((bf16[32,3,128,128]{3,2,1,0:T(8,128)(2,1)}), bf16[32,3,128,128]{3,2,1,0:T(8,128)(2,1)S(1)}, u32[]{:S(2)}, u32[]{:S(2)}) async-start(bf16[32,3,128,128]{3,2,1,0:T(8,128)(2,1)} %pack.1), calls=%async_computation | async-start | bytes 6291456 | tf_op jit(solution)/shard_map/all_to_all | solution.py:284
  14.1 0.0 copy-done
  14.1 4.9 %collective-permute-start.1 = (s32[16,14]{1,0:T(8,128)S(1)}, s32[16,14]{1,0:T(8,128)S(1)}, u32[]{:S(2)}, u32[]{:S(2)}) collective-permute-start(s32[16,14]{1,0:T(8,128)S(1)} %copy-done), channel_id=1, source_target_pairs={{0,16},{8,24},{16,0},{24,8},{1,17},{9,25},{17,1},{25,9},{2,18},{10... | collective-permute-start | bytes 2696 | tf_op jit(solution)/shard_map/ppermute | solution.py:291
  19.0 2.2 %collective-permute-start = (s32[16,14]{1,0:T(8,128)S(1)}, s32[16,14]{1,0:T(8,128)S(1)}, u32[]{:S(2)}, u32[]{:S(2)}) collective-permute-start(s32[16,14]{1,0:T(8,128)S(1)} %copy-done), channel_id=1, source_target_pairs={{0,8},{8,16},{16,24},{24,0},{1,9},{9,17},{17,25},{25,1},{2,10},{10... | collective-permute-start | bytes 2696 | tf_op jit(solution)/shard_map/ppermute | solution.py:291
  21.3 4.2 %collective-permute-start.2 = (s32[16,14]{1,0:T(8,128)S(1)}, s32[16,14]{1,0:T(8,128)S(1)}, u32[]{:S(2)}, u32[]{:S(2)}) collective-permute-start(s32[16,14]{1,0:T(8,128)S(1)} %copy-done), channel_id=1, source_target_pairs={{0,24},{8,0},{16,8},{24,16},{1,25},{9,1},{17,9},{25,17},{2,26},{10... | collective-permute-start | bytes 2696 | tf_op jit(solution)/shard_map/ppermute | solution.py:291
  25.5 0.1 slice_bitcast_fusion
  25.6 1.3 collective-permute-start.3
  26.9 22.9 %collective-permute-done.1 = s32[16,14]{1,0:T(8,128)S(1)} collective-permute-done((s32[16,14]{1,0:T(8,128)S(1)}, s32[16,14]{1,0:T(8,128)S(1)}, u32[]{:S(2)}, u32[]{:S(2)}) %collective-permute-start.1) | collective-permute-done | bytes 928 | tf_op jit(solution)/shard_map/ppermute | solution.py:291
  49.8 0.0 collective-permute-done
  49.8 0.0 collective-permute-done.2
  49.9 0.0 collective-permute-done.3.above
  49.9 3.5 %all-to-all-done.kinds.own = bf16[32,3,128,128]{3,2,1,0:T(8,128)(2,1)S(1)} async-done(((bf16[32,3,128,128]{3,2,1,0:T(8,128)(2,1)}), bf16[32,3,128,128]{3,2,1,0:T(8,128)(2,1)S(1)}, u32[]{:S(2)}, u32[]{:S(2)}) %all-to-all-start) | async-done | bytes 3145760 | tf_op jit(solution)/shard_map/all_to_all | solution.py:284
  53.4 4.8 %collective-permute-start.4 = (bf16[32,3,128,128]{3,2,1,0:T(8,128)(2,1)S(1)}, bf16[32,3,128,128]{3,2,1,0:T(8,128)(2,1)}, u32[]{:S(2)}, u32[]{:S(2)}) collective-permute-start(bf16[32,3,128,128]{3,2,1,0:T(8,128)(2,1)S(1)} %all-to-all-done.kinds.own), channel_id=1, source_target_pairs={{0,1},{1,0},{2,3},{3,2},{4,5},{5,4},{6,7},{7,6},{8,9},{9,8},{10,11... | collective-permute-start | bytes 9437192 | tf_op jit(solution)/shard_map/ppermute | solution.py:272
  58.2 0.1 pad_add_fusion.1.where
  58.2 1.4 pick_globals.1
  59.6 25.0 %all_to_all.20 = bf16[16,32,128]{2,1,0:T(8,128)(2,1)S(1)} all-to-all(bf16[16,32,128]{2,1,0:T(8,128)(2,1)S(1)} %bitcast.25), channel_id=1, replica_groups=mesh['z'=16,'y'=4,'x'=4,'core'=2] {'z'}, dimensions={0} | all-to-all | bytes 262144 | tf_op jit(solution)/shard_map/all_to_all | solution.py:300
  84.7 0.7 broadcast_in_dim.2
  85.3 6.2 %all-to-all-start.2 = ((bf16[16,32,128]{2,1,0:T(8,128)(2,1)}), bf16[16,32,128]{2,1,0:T(8,128)(2,1)S(1)}, u32[]{:S(2)}, u32[]{:S(2)}) async-start(bf16[16,32,128]{2,1,0:T(8,128)(2,1)} %broadcast_in_dim.2), calls=%async_computation.2 | async-start | bytes 262144 | tf_op jit(solution)/shard_map/all_to_all | solution.py:302
  91.5 0.8 slice.7
  92.4 11.2 %all-to-all-done.2 = bf16[16,32,128]{2,1,0:T(8,128)(2,1)S(1)} async-done(((bf16[16,32,128]{2,1,0:T(8,128)(2,1)}), bf16[16,32,128]{2,1,0:T(8,128)(2,1)S(1)}, u32[]{:S(2)}, u32[]{:S(2)}) %all-to-all-start.2) | async-done | bytes 131104 | tf_op jit(solution)/shard_map/all_to_all | solution.py:302
  103.5 3.7 %collective-permute-start.6 = (bf16[8,2,128,128]{3,2,1,0:T(8,128)(2,1)}, bf16[8,2,128,128]{3,2,1,0:T(8,128)(2,1)S(1)}, u32[]{:S(2)}, u32[]{:S(2)}) collective-permute-start(bf16[8,2,128,128]{3,2,1,0:T(8,128)(2,1)} %slice.7), channel_id=1, source_target_pairs={{0,32},{32,64},{64,96},{96,128},{128,160},{160,192},{192,224},{224... | collective-permute-start | bytes 1572872 | tf_op jit(solution)/shard_map/ppermute | solution.py:307
  107.2 5.4 %collective-permute-start.5 = (bf16[2,2,128,128]{3,2,1,0:T(8,128)(2,1)S(1)}, bf16[2,2,128,128]{3,2,1,0:T(8,128)(2,1)S(1)}, u32[]{:S(2)}, u32[]{:S(2)}) collective-permute-start(bf16[2,2,128,128]{3,2,1,0:T(8,128)(2,1)S(1)} %bitcast.22), channel_id=1, source_target_pairs={{0,1},{1,0},{2,3},{3,2},{4,5},{5,4},{6,7},{7,6},{8,9},{9,8},{10,11... | collective-permute-start | bytes 393224 | tf_op jit(solution)/shard_map/ppermute | solution.py:272
  112.6 1.0 collective-permute-done.5.global_other
  113.6 0.0 collective-permute-done.4.other
  113.6 13.9 %attend_rest.1.refs_2_ = bf16[24,128,128]{2,1,0:T(8,128)(2,1)S(1)} custom-call(s32[3]{0:T(128)S(1)} %pad_add_fusion.1.where, s32[4,16,14]{2,1,0:T(8,128)S(1)} %pad_add_fusion.rows, bf16[32,3,128,128]{3,2,1,0:T(8,128)(2,1)S(1)} %all-to-all-done.kinds.own, bf16[32,3,128,128]{3,2,1,0:T(8,128)(2,1)} %collective-permute-done.4.other, ...), custom_call_target="tpu_custom_call" | custom-call | flops 2818572288 | bytes 8388608 | tf_op jit(solution)/shard_map/attend_rest/pallas_call | solution.py:249
  127.5 0.0 collective-permute-done.6.refs_0_
  127.5 2.3 %collective-permute-start.7 = (bf16[8,2,128,128]{3,2,1,0:T(8,128)(2,1)S(1)}, bf16[8,2,128,128]{3,2,1,0:T(8,128)(2,1)S(1)}, u32[]{:S(2)}, u32[]{:S(2)}) collective-permute-start(bf16[8,2,128,128]{3,2,1,0:T(8,128)(2,1)S(1)} %collective-permute-done.6.refs_0_), channel_id=1, source_target_pairs={{0,1},{1,0},{2,3},{3,2},{4,5},{5,4},{6,7},{7,6},{8,9},{9,8},{10,11... | collective-permute-start | bytes 1572872 | tf_op jit(solution)/shard_map/ppermute | solution.py:272
  129.8 1.5 collective-permute-done.7.refs_1_
  131.3 6.4 %attend_first.1 = bf16[32,128,128]{2,1,0:T(8,128)(2,1)S(1)} custom-call(s32[3]{0:T(128)S(1)} %pad_add_fusion.1.where, s32[4,16,14]{2,1,0:T(8,128)S(1)} %pad_add_fusion.rows, bf16[32,3,128,128]{3,2,1,0:T(8,128)(2,1)S(1)} %all-to-all-done.kinds.own, bf16[32,3,128,128]{3,2,1,0:T(8,128)(2,1)} %collective-permute-done.4.other, ...), custom_call_target="tpu_custom_call" | custom-call | flops 939524096 | bytes 8388608 | tf_op jit(solution)/shard_map/attend_first/pallas_call | solution.py:249
  137.7 20.3 %all_to_all.21 = bf16[32,128,128]{2,1,0:T(8,128)(2,1)S(1)} all-to-all(bf16[32,128,128]{2,1,0:T(8,128)(2,1)S(1)} %attend_first.1), channel_id=1, replica_groups=mesh['z'=16,'y'=4,'x'=4,'core'=2] {'y','x','core'}, dimensions={0} | all-to-all | bytes 2097152 | tf_op jit(solution)/shard_map/all_to_all | solution.py:316
  158.0 0.7 copy.5
  158.7 1.2 copy.8
  (2 shorter events, 0.0 us)
Async XLA Ops:
  3.5 10.6 %copy-start = (s32[16,14]{1,0:T(8,128)S(1)}, s32[16,14]{1,0:T(8,128)}, u32[]{:S(2)}) copy-start(s32[16,14]{1,0:T(8,128)} %param.7) | copy-start | bytes 2692
  3.5 49.9 %all-to-all-start = ((bf16[32,3,128,128]{3,2,1,0:T(8,128)(2,1)}), bf16[32,3,128,128]{3,2,1,0:T(8,128)(2,1)S(1)}, u32[]{:S(2)}, u32[]{:S(2)}) async-start(bf16[32,3,128,128]{3,2,1,0:T(8,128)(2,1)} %pack.1), calls=%async_computation | async-start | bytes 6291456 | tf_op jit(solution)/shard_map/all_to_all | solution.py:284
  14.1 35.7 %collective-permute-start.1 = (s32[16,14]{1,0:T(8,128)S(1)}, s32[16,14]{1,0:T(8,128)S(1)}, u32[]{:S(2)}, u32[]{:S(2)}) collective-permute-start(s32[16,14]{1,0:T(8,128)S(1)} %copy-done), channel_id=1, source_target_pairs={{0,16},{8,24},{16,0},{24,8},{1,17},{9,25},{17,1},{25,9},{2,18},{10... | collective-permute-start | bytes 2696 | tf_op jit(solution)/shard_map/ppermute | solution.py:291
  19.0 30.8 %collective-permute-start = (s32[16,14]{1,0:T(8,128)S(1)}, s32[16,14]{1,0:T(8,128)S(1)}, u32[]{:S(2)}, u32[]{:S(2)}) collective-permute-start(s32[16,14]{1,0:T(8,128)S(1)} %copy-done), channel_id=1, source_target_pairs={{0,8},{8,16},{16,24},{24,0},{1,9},{9,17},{17,25},{25,1},{2,10},{10... | collective-permute-start | bytes 2696 | tf_op jit(solution)/shard_map/ppermute | solution.py:291
  21.3 28.6 %collective-permute-start.2 = (s32[16,14]{1,0:T(8,128)S(1)}, s32[16,14]{1,0:T(8,128)S(1)}, u32[]{:S(2)}, u32[]{:S(2)}) collective-permute-start(s32[16,14]{1,0:T(8,128)S(1)} %copy-done), channel_id=1, source_target_pairs={{0,24},{8,0},{16,8},{24,16},{1,25},{9,1},{17,9},{25,17},{2,26},{10... | collective-permute-start | bytes 2696 | tf_op jit(solution)/shard_map/ppermute | solution.py:291
  25.6 24.2 %collective-permute-start.3 = (s32[4]{0:T(128)S(1)}, s32[4]{0:T(128)S(1)}, u32[]{:S(2)}, u32[]{:S(2)}) collective-permute-start(s32[4]{0:T(128)S(1)} %slice_bitcast_fusion), channel_id=1, source_target_pairs={{32,0},{64,32},{96,64},{128,96},{160,128},{192,160},{224,192},{256... | collective-permute-start | bytes 56 | tf_op jit(solution)/shard_map/ppermute | solution.py:295
  53.4 60.2 %collective-permute-start.4 = (bf16[32,3,128,128]{3,2,1,0:T(8,128)(2,1)S(1)}, bf16[32,3,128,128]{3,2,1,0:T(8,128)(2,1)}, u32[]{:S(2)}, u32[]{:S(2)}) collective-permute-start(bf16[32,3,128,128]{3,2,1,0:T(8,128)(2,1)S(1)} %all-to-all-done.kinds.own), channel_id=1, source_target_pairs={{0,1},{1,0},{2,3},{3,2},{4,5},{5,4},{6,7},{7,6},{8,9},{9,8},{10,11... | collective-permute-start | bytes 9437192 | tf_op jit(solution)/shard_map/ppermute | solution.py:272
  85.3 18.2 %all-to-all-start.2 = ((bf16[16,32,128]{2,1,0:T(8,128)(2,1)}), bf16[16,32,128]{2,1,0:T(8,128)(2,1)S(1)}, u32[]{:S(2)}, u32[]{:S(2)}) async-start(bf16[16,32,128]{2,1,0:T(8,128)(2,1)} %broadcast_in_dim.2), calls=%async_computation.2 | async-start | bytes 262144 | tf_op jit(solution)/shard_map/all_to_all | solution.py:302
  103.5 24.0 %collective-permute-start.6 = (bf16[8,2,128,128]{3,2,1,0:T(8,128)(2,1)}, bf16[8,2,128,128]{3,2,1,0:T(8,128)(2,1)S(1)}, u32[]{:S(2)}, u32[]{:S(2)}) collective-permute-start(bf16[8,2,128,128]{3,2,1,0:T(8,128)(2,1)} %slice.7), channel_id=1, source_target_pairs={{0,32},{32,64},{64,96},{96,128},{128,160},{160,192},{192,224},{224... | collective-permute-start | bytes 1572872 | tf_op jit(solution)/shard_map/ppermute | solution.py:307
  107.2 6.4 %collective-permute-start.5 = (bf16[2,2,128,128]{3,2,1,0:T(8,128)(2,1)S(1)}, bf16[2,2,128,128]{3,2,1,0:T(8,128)(2,1)S(1)}, u32[]{:S(2)}, u32[]{:S(2)}) collective-permute-start(bf16[2,2,128,128]{3,2,1,0:T(8,128)(2,1)S(1)} %bitcast.22), channel_id=1, source_target_pairs={{0,1},{1,0},{2,3},{3,2},{4,5},{5,4},{6,7},{7,6},{8,9},{9,8},{10,11... | collective-permute-start | bytes 393224 | tf_op jit(solution)/shard_map/ppermute | solution.py:272
  127.5 3.8 %collective-permute-start.7 = (bf16[8,2,128,128]{3,2,1,0:T(8,128)(2,1)S(1)}, bf16[8,2,128,128]{3,2,1,0:T(8,128)(2,1)S(1)}, u32[]{:S(2)}, u32[]{:S(2)}) collective-permute-start(bf16[8,2,128,128]{3,2,1,0:T(8,128)(2,1)S(1)} %collective-permute-done.6.refs_0_), channel_id=1, source_target_pairs={{0,1},{1,0},{2,3},{3,2},{4,5},{5,4},{6,7},{7,6},{8,9},{9,8},{10,11... | collective-permute-start | bytes 1572872 | tf_op jit(solution)/shard_map/ppermute | solution.py:272

commit v8 on v7

--- a/solution.py
+++ b/solution.py
@@ -71,6 +71,90 @@
     )(*arrays)
 
 
+def early_kernel(ids, base, keys, values, out, key_buf, value_buf, arrived, sems):
+    even = ids[0] == base[0]
+    for slot in range(1, GLOBALS):
+        even = even | (ids[slot] == base[0])
+    which = jnp.where(even, 0, 1)
+    loads = [
+        pltpu.make_async_copy(keys.at[which], key_buf, arrived.at[0]),
+        pltpu.make_async_copy(values.at[which], value_buf, arrived.at[1]),
+    ]
+    stores = [[], []]
+    for head in range(HEADS):
+        columns = pl.ds(head * HEAD_DIM, HEAD_DIM)
+        for kind, buf in enumerate([key_buf, value_buf]):
+            stores[kind].append(
+                pltpu.make_async_copy(
+                    buf.at[:, columns], out.at[2 * head + kind], sems.at[kind, head]
+                )
+            )
+    for load in loads:
+        load.start()
+    for load, each in zip(loads, stores):
+        load.wait()
+        for store in each:
+            store.start()
+    for each in stores:
+        for store in each:
+            store.wait()
+
+
+def pack_early(ids, base, *arrays):
+    arrays = [array.reshape(2, BLOCK, HEADS * HEAD_DIM) for array in arrays]
+    return pl.pallas_call(
+        early_kernel,
+        out_shape=jax.ShapeDtypeStruct((2 * HEADS, BLOCK, HEAD_DIM), jnp.bfloat16),
+        in_specs=[SCALARS, SCALARS, LEFT, LEFT],
+        out_specs=LEFT,
+        scratch_shapes=[pltpu.VMEM(array.shape[1:], array.dtype) for array in arrays]
+        + [pltpu.SemaphoreType.DMA((2,)), pltpu.SemaphoreType.DMA((2, HEADS))],
+        compiler_params=pltpu.CompilerParams(vmem_limit_bytes=56 << 20),
+        name="pack_early",
+    )(ids, base, *arrays)
+
+
+def early_pick_kernel(where, rows, above, kinds, *refs):
+    outs, (buffer, sems) = refs[:GLOBALS], refs[GLOBALS:]
+    group, last = row_of(where, PLANE // 2 - 1, 1)
+    copies, present, sources = [], [], []
+    for step in range(GLOBALS):
+        slot = (where[3] + step) % GLOBALS
+        place = jnp.maximum(rows[group, last, WSEL + slot], above[slot]) - where[1]
+        held = (place >= 0) & (place < PLANE)
+        source = jnp.where(held, place, 0) // 2
+        copies.append(pltpu.make_async_copy(kinds.at[source], buffer.at[step], sems.at[step]))
+        present.append(held)
+        sources.append(jnp.where(held, source, -1 - step))
+    for copy in copies:
+        copy.start()
+    clash = jnp.int32(0)
+    for one in range(GLOBALS):
+        for two in range(one):
+            clash = jnp.where(sources[one] == sources[two], 1, clash)
+    for step in range(GLOBALS):
+        copies[step].wait()
+        block = buffer[step]
+        outs[step][:BLOCK] = jnp.where(present[step], block, jnp.zeros_like(block))
+        flag = jnp.where(clash > 0, 1.0, 0.0)
+        outs[step][BLOCK:] = jnp.full((16, HEAD_DIM), flag, jnp.float32).astype(jnp.bfloat16)
+
+
+def pick_early(where, rows, above, kinds):
+    return pl.pallas_call(
+        early_pick_kernel,
+        out_shape=[jax.ShapeDtypeStruct((BLOCK + 16, HEAD_DIM), jnp.bfloat16)] * GLOBALS,
+        in_specs=[SCALARS, SCALARS, SCALARS, LEFT],
+        out_specs=[WHOLE] * GLOBALS,
+        scratch_shapes=[
+            pltpu.VMEM((GLOBALS, BLOCK, HEAD_DIM), jnp.bfloat16),
+            pltpu.SemaphoreType.DMA((GLOBALS,)),
+        ],
+        compiler_params=pltpu.CompilerParams(vmem_limit_bytes=12 << 20),
+        name="pick_early",
+    )(where, rows, above, kinds)
+
+
 def pick_kernel(where, rows, above, kinds, out, buffer, sems):
     group, last = row_of(where, PLANE // 2 - 1, 1)
     copies, present = [], []
@@ -173,7 +257,7 @@
             if kept:
                 place = jnp.where(place >= 0, place, place + halo_at + WIN)
         else:
-            place = global_at + slot - WSEL
+            place = global_at + (where[3] + SLOTS - slot) % GLOBALS
         return jnp.where(block_id >= 0, place, 0), block_id >= 0
 
     def score_phase(at, lane):
@@ -272,17 +356,24 @@
     return lax.ppermute(value, "core", [(0, 1), (1, 0)])
 
 
+def added(*values):
+    return sum(value.astype(jnp.float32) for value in values).astype(jnp.bfloat16)
+
+
 def shards(queries, key_vectors, value_vectors, key_blocks):
     depth = lax.axis_size("z")
     breadth = lax.axis_size("y")
     up = [(at, at + 1) for at in range(depth - 1)]
     down = [(at + 1, at) for at in range(depth - 1)]
-    where = jnp.stack(
-        [lax.axis_index("core"), lax.axis_index("z") * PLANE, lax.axis_index("y")]
-    )
-
-    received = lax.all_to_all(
-        pack(queries, key_vectors, value_vectors), PLANE_AXES, 0, 0, tiled=True
+    level, here = lax.axis_index("z"), lax.axis_index("y")
+    where = jnp.stack([lax.axis_index("core"), level * PLANE, here, level % GLOBALS])
+
+    ahead = lax.ppermute(
+        key_blocks[-1, WSEL:], ("z", "y"), [(at + 1, at) for at in range(depth * breadth - 1)]
+    )
+    base = level * PLANE + 2 * lax.axis_index(PLANE_AXES)
+    early = lax.all_to_all(
+        pack_early(ahead, base[None], key_vectors, value_vectors), PLANE_AXES, 0, 0, tiled=True
     )
 
     rows = jnp.stack(
@@ -293,18 +384,42 @@
         ]
     )
     above = lax.ppermute(key_blocks[-1, WSEL:], "z", down)
-    own, rows, above = lax.optimization_barrier((received, rows, above))
+
+    packed = pack(queries, key_vectors, value_vectors)
+    early, packed, rows, above = lax.optimization_barrier((early, packed, rows, above))
+    own = lax.all_to_all(packed, PLANE_AXES, 0, 0, tiled=True)
+
+    def within(step):
+        return [(at, at - at % GLOBALS + (at + step) % GLOBALS) for at in range(depth)]
+
+    def across(step):
+        return [(at, (at + GLOBALS * step) % depth) for at in range(depth)]
+
+    parts = pick_early(where, rows, above, early)
+    held = added(
+        parts[0], *[lax.ppermute(parts[step], "z", within(step)) for step in range(1, GLOBALS)]
+    )
+    held = added(
+        held, *[lax.ppermute(held, "z", across(step)) for step in range(1, depth // GLOBALS)]
+    )
+    clash = held[BLOCK, 0].astype(jnp.float32) > 0.5
+    held = held[:BLOCK]
+    global_own = jnp.stack(
+        [held] + [lax.ppermute(held, "z", within(step)) for step in range(1, GLOBALS)]
+    )
+
+    def again(blocks):
+        part = pick_globals(where, rows, above, blocks).astype(jnp.float32)
+        full = lax.psum(part, "z").astype(jnp.bfloat16)
+        return full[(level + GLOBALS - jnp.arange(GLOBALS)) % GLOBALS]
+
+    own, shared = lax.optimization_barrier((own, global_own))
+    global_own = lax.cond(clash, again, lambda blocks: shared, own)
     other = swapped(own)
-
-    part = pick_globals(where, rows, above, own).reshape(depth, -1, HEAD_DIM)
-    pieces = lax.all_to_all(part, "z", 0, 0, tiled=True)
-    summed = jnp.sum(pieces.astype(jnp.float32), axis=0, keepdims=True).astype(jnp.bfloat16)
-    global_own = lax.all_to_all(jnp.broadcast_to(summed, part.shape), "z", 0, 0, tiled=True)
-    last, global_own = lax.optimization_barrier((own[-WIN // 2 :, :2], global_own))
     pair = (GLOBALS // 2, 2, BLOCK, HEAD_DIM)
     global_own = global_own.reshape(pair)
     global_other = swapped(global_own)
-    halo_own = lax.ppermute(last, "z", up)
+    halo_own = lax.ppermute(own[-WIN // 2 :, :2], "z", up)
     rest = attend(
         WIN // 2, PLANE, where, rows, own, other, global_own, global_other
     )

time: 161 us -> 180 us (1.12)
  starting transfers between devices: 45.6 us -> 86.7 us
  waiting for transfers between devices: 40.1 us -> 17.4 us
  blocking collectives: 45.3 us -> 24.3 us
  between operations: 0.16 us -> 14.4 us
  Pallas kernels: 25.1 us -> 30 us
  local copies, waits for them, and re-layouts: 3.52 us -> 5.83 us
    ppermute x1 -> x11, starting transfers between devices: 3.68 us -> 48.6 us  [the longest x3 21.9 us: shards(): lax.ppermute(held, 'z', across(step))]
    all_to_all x1 -> x0, blocking collectives: 25 us -> none  [shards(): pieces = lax.all_to_all(part, 'z', 0, 0, tiled=True)]
    ppermute x3, waiting for transfers between devices: 22.9 us -> 0.01 us  [shards(): lax.ppermute(key_blocks, 'y', [(at, (at + step) % breadth) for at in rang...]
    all_to_all x2, waiting for transfers between devices: 14.7 us -> 2.22 us  [the longest x1 2.21 us: shards(): lax.all_to_all(pack_early(ahead, base[None], key_vectors, value_vectors),...]
    ppermute x1 -> x11, waiting for transfers between devices: 0.01 us -> 12.3 us  [the longest x3 4.01 us: shards(): lax.ppermute(held, 'z', across(step))]
    all_to_all x1, blocking collectives: 20.3 us -> 24.3 us  [shards(): back = lax.all_to_all(context, PLANE_AXES, 0, 0, tiled=True)]
    pallas_call x1 -> x2, Pallas kernels: 1.37 us -> 4.34 us  [the longest x1 2.95 us: pack_early(): pl.pallas_call(early_kernel, out_shape=jax.ShapeDtypeStruct((2 * HEADS, B...]
    pallas_call x2, Pallas kernels: 20.3 us -> 22.2 us  [attend(): pl.pallas_call(functools.partial(attend_kernel, start, high, kept), out_s...]
  transfers between devices with their start and end apart: 10 -> 20, of which waited for: 5 -> 9; matrix products, arithmetic and copies ran while one was open for 1% -> 1% of each run, Pallas kernels for 10% -> 11%
where the time goes in v8:
time: 180 us; the launch traced here: 179 us
  starting transfers between devices  86.7 us (48%)
  Pallas kernels  30 us (17%)
  blocking collectives  24.3 us (14%)
  waiting for transfers between devices  17.4 us (10%)
  between operations  14.4 us (8%)
  local copies, waits for them, and re-layouts  5.83 us (3%)
    all_to_all x1, blocking collectives, shards(): back = lax.all_to_all(context, PLANE_AXES, 0, 0, tiled=True)  24.3 us
    pallas_call x2, Pallas kernels, attend(): pl.pallas_call(functools.partial(attend_kernel, start, high, kept), out_s...  22.2 us
    ppermute x3, starting transfers between devices, shards(): lax.ppermute(held, 'z', across(step))  21.9 us
    ppermute x3, starting transfers between devices, shards(): lax.ppermute(parts[step], 'z', within(step))  12.8 us
    all_to_all x1, starting transfers between devices, shards(): lax.all_to_all(pack_early(ahead, base[None], key_vectors, value_vectors),...  11 us
    ppermute x3, starting transfers between devices, swapped(): return lax.ppermute(value, 'core', [(0, 1), (1, 0)])  10.6 us
    ppermute x3, starting transfers between devices, shards(): lax.ppermute(key_blocks, 'y', [(at, (at + step) % breadth) for at in rang...  10.1 us
    ppermute x3, starting transfers between devices, shards(): lax.ppermute(held, 'z', within(step))  9 us
  transfers between devices with their start and end apart: 20, of which 9 were waited for; matrix products, arithmetic and copies ran while one was open for 1% of the time, Pallas kernels for 11%

profile of v8, /device:TPU:1, one launch (start us, length us, event | category | flops | bytes accessed | tf_op | source)
XLA Modules:
  0.0 178.9 jit_solution(2198321726258855830)
XLA Ops:
  6.5 0.8 slice_bitcast_fusion
  7.4 1.3 collective-permute-start
  8.7 3.6 %collective-permute-done.ids = s32[4]{0:T(128)S(1)} collective-permute-done((s32[4]{0:T(128)S(1)}, s32[4]{0:T(128)S(1)}, u32[]{:S(2)}, u32[]{:S(2)}) %collective-permute-start) | collective-permute-done | bytes 48 | tf_op jit(solution)/shard_map/ppermute | solution.py:371
  12.3 0.6 copy-done.1
  12.9 3.0 %pack_early.1 = bf16[32,128,128]{2,1,0:T(8,128)(2,1)} custom-call(s32[4]{0:T(128)} %copy-done.1, s32[1]{0:T(128)} %bitcast.6.base, bf16[2,128,2048]{2,1,0:T(8,128)(2,1)} %bitcast.33, bf16[2,128,2048]{2,1,0:T(8,128)(2,1)} %bitcast.35), custom_call_target="tpu_custom_call" | custom-call | tf_op jit(solution)/shard_map/pack_early/pallas_call | solution.py:105
  15.9 11.0 %all-to-all-start = ((bf16[32,128,128]{2,1,0:T(8,128)(2,1)}), bf16[32,128,128]{2,1,0:T(8,128)(2,1)S(1)}, u32[]{:S(2)}, u32[]{:S(2)}) async-start(bf16[32,128,128]{2,1,0:T(8,128)(2,1)} %pack_early.1), calls=%async_computation | async-start | bytes 2097152 | tf_op jit(solution)/shard_map/all_to_all | solution.py:375
  26.9 3.3 %collective-permute-start.1 = (s32[16,14]{1,0:T(8,128)S(1)}, s32[16,14]{1,0:T(8,128)S(1)}, u32[]{:S(2)}, u32[]{:S(2)}) collective-permute-start(s32[16,14]{1,0:T(8,128)S(1)} %copy-done), channel_id=1, source_target_pairs={{0,8},{8,16},{16,24},{24,0},{1,9},{9,17},{17,25},{25,1},{2,10},{10... | collective-permute-start | bytes 2696 | tf_op jit(solution)/shard_map/ppermute | solution.py:382
  30.2 3.2 %collective-permute-start.3 = (s32[16,14]{1,0:T(8,128)S(1)}, s32[16,14]{1,0:T(8,128)S(1)}, u32[]{:S(2)}, u32[]{:S(2)}) collective-permute-start(s32[16,14]{1,0:T(8,128)S(1)} %copy-done), channel_id=1, source_target_pairs={{0,24},{8,0},{16,8},{24,16},{1,25},{9,1},{17,9},{25,17},{2,26},{10... | collective-permute-start | bytes 2696 | tf_op jit(solution)/shard_map/ppermute | solution.py:382
  33.4 3.6 %collective-permute-start.2 = (s32[16,14]{1,0:T(8,128)S(1)}, s32[16,14]{1,0:T(8,128)S(1)}, u32[]{:S(2)}, u32[]{:S(2)}) collective-permute-start(s32[16,14]{1,0:T(8,128)S(1)} %copy-done), channel_id=1, source_target_pairs={{0,16},{8,24},{16,0},{24,8},{1,17},{9,25},{17,1},{25,9},{2,18},{10... | collective-permute-start | bytes 2696 | tf_op jit(solution)/shard_map/ppermute | solution.py:382
  37.0 1.3 collective-permute-start.4
  38.3 3.5 %pack.1 = bf16[32,3,128,128]{3,2,1,0:T(8,128)(2,1)} custom-call(bf16[2,128,2048]{2,1,0:T(8,128)(2,1)} %bitcast.37, bf16[2,128,2048]{2,1,0:T(8,128)(2,1)} %bitcast.34, bf16[2,128,2048]{2,1,0:T(8,128)(2,1)} %bitcast.36), custom_call_target="tpu_custom_call" | custom-call | tf_op jit(solution)/shard_map/pack/pallas_call | solution.py:62
  41.9 0.0 collective-permute-done.1
  41.9 0.0 collective-permute-done.3
  41.9 0.0 collective-permute-done.4.above
  41.9 2.2 %all-to-all-done.kinds = bf16[32,128,128]{2,1,0:T(8,128)(2,1)S(1)} async-done(((bf16[32,128,128]{2,1,0:T(8,128)(2,1)}), bf16[32,128,128]{2,1,0:T(8,128)(2,1)S(1)}, u32[]{:S(2)}, u32[]{:S(2)}) %all-to-all-start) | async-done | bytes 1048608 | tf_op jit(solution)/shard_map/all_to_all | solution.py:375
  44.1 5.2 %all-to-all-start.1 = ((bf16[32,3,128,128]{3,2,1,0:T(8,128)(2,1)}), bf16[32,3,128,128]{3,2,1,0:T(8,128)(2,1)}, u32[]{:S(2)}, u32[]{:S(2)}) async-start(bf16[32,3,128,128]{3,2,1,0:T(8,128)(2,1)} %pack.1), calls=%async_computation.1 | async-start | bytes 6291456 | tf_op jit(solution)/shard_map/all_to_all | solution.py:390
  49.3 0.1 pad_add_fusion.1.where
  49.4 1.4 pick_early.1
  50.8 3.7 %collective-permute-start.5 = (bf16[144,128]{1,0:T(8,128)(2,1)S(1)}, bf16[144,128]{1,0:T(8,128)(2,1)S(1)}, u32[]{:S(2)}, u32[]{:S(2)}) collective-permute-start(bf16[144,128]{1,0:T(8,128)(2,1)S(1)} %get-tuple-element.47), channel_id=1, source_target_pairs={{0,32},{32,64},{64,96},{96,0},{128,160},{160,192},{192,224},{224,1... | collective-permute-start | bytes 110600 | tf_op jit(solution)/shard_map/ppermute | solution.py:400
  54.5 7.1 %collective-permute-start.6 = (bf16[144,128]{1,0:T(8,128)(2,1)S(1)}, bf16[144,128]{1,0:T(8,128)(2,1)S(1)}, u32[]{:S(2)}, u32[]{:S(2)}) collective-permute-start(bf16[144,128]{1,0:T(8,128)(2,1)S(1)} %get-tuple-element.48), channel_id=1, source_target_pairs={{0,64},{32,96},{64,0},{96,32},{128,192},{160,224},{192,128},{224,1... | collective-permute-start | bytes 110600 | tf_op jit(solution)/shard_map/ppermute | solution.py:400
  61.7 1.9 %collective-permute-start.7 = (bf16[144,128]{1,0:T(8,128)(2,1)S(1)}, bf16[144,128]{1,0:T(8,128)(2,1)S(1)}, u32[]{:S(2)}, u32[]{:S(2)}) collective-permute-start(bf16[144,128]{1,0:T(8,128)(2,1)S(1)} %get-tuple-element.49), channel_id=1, source_target_pairs={{0,96},{32,0},{64,32},{96,64},{128,224},{160,128},{192,160},{224,1... | collective-permute-start | bytes 110600 | tf_op jit(solution)/shard_map/ppermute | solution.py:400
  63.6 0.4 collective-permute-done.6
  64.0 2.8 %collective-permute-done.7 = bf16[144,128]{1,0:T(8,128)(2,1)S(1)} collective-permute-done((bf16[144,128]{1,0:T(8,128)(2,1)S(1)}, bf16[144,128]{1,0:T(8,128)(2,1)S(1)}, u32[]{:S(2)}, u32[]{:S(2)}) %collective-permute-start.7) | collective-permute-done | bytes 36896 | tf_op jit(solution)/shard_map/ppermute | solution.py:400
  66.8 11.0 %collective-permute-start.10 = (bf16[144,128]{1,0:T(8,128)(2,1)S(1)}, bf16[144,128]{1,0:T(8,128)(2,1)S(1)}, u32[]{:S(2)}, u32[]{:S(2)}) collective-permute-start(bf16[144,128]{1,0:T(8,128)(2,1)S(1)} %add_convert_fusion.1), channel_id=1, source_target_pairs={{0,384},{32,416},{64,448},{96,480},{128,0},{160,32},{192,64},{224,... | collective-permute-start | bytes 110600 | tf_op jit(solution)/shard_map/ppermute | solution.py:403
  77.8 4.8 %collective-permute-start.9 = (bf16[144,128]{1,0:T(8,128)(2,1)S(1)}, bf16[144,128]{1,0:T(8,128)(2,1)S(1)}, u32[]{:S(2)}, u32[]{:S(2)}) collective-permute-start(bf16[144,128]{1,0:T(8,128)(2,1)S(1)} %add_convert_fusion.1), channel_id=1, source_target_pairs={{0,256},{32,288},{64,320},{96,352},{128,384},{160,416},{192,448},{... | collective-permute-start | bytes 110600 | tf_op jit(solution)/shard_map/ppermute | solution.py:403
  82.6 6.1 %collective-permute-start.8 = (bf16[144,128]{1,0:T(8,128)(2,1)S(1)}, bf16[144,128]{1,0:T(8,128)(2,1)S(1)}, u32[]{:S(2)}, u32[]{:S(2)}) collective-permute-start(bf16[144,128]{1,0:T(8,128)(2,1)S(1)} %add_convert_fusion.1), channel_id=1, source_target_pairs={{0,128},{32,160},{64,192},{96,224},{128,256},{160,288},{192,320},{... | collective-permute-start | bytes 110600 | tf_op jit(solution)/shard_map/ppermute | solution.py:403
  88.8 0.0 collective-permute-done.10
  88.8 2.6 %collective-permute-done.9 = bf16[144,128]{1,0:T(8,128)(2,1)S(1)} collective-permute-done((bf16[144,128]{1,0:T(8,128)(2,1)S(1)}, bf16[144,128]{1,0:T(8,128)(2,1)S(1)}, u32[]{:S(2)}, u32[]{:S(2)}) %collective-permute-start.9) | collective-permute-done | bytes 36896 | tf_op jit(solution)/shard_map/ppermute | solution.py:403
  91.4 1.4 collective-permute-done.8
  92.8 1.9 %collective-permute-start.12 = (bf16[128,128]{1,0:T(8,128)(2,1)S(1)}, bf16[128,128]{1,0:T(8,128)(2,1)S(1)}, u32[]{:S(2)}, u32[]{:S(2)}) collective-permute-start(bf16[128,128]{1,0:T(8,128)(2,1)S(1)} %get-tuple-element.57), channel_id=1, source_target_pairs={{0,64},{32,96},{64,0},{96,32},{128,192},{160,224},{192,128},{224,1... | collective-permute-start | bytes 98312 | tf_op jit(solution)/shard_map/ppermute | solution.py:408
  94.7 4.0 %collective-permute-start.11 = (bf16[128,128]{1,0:T(8,128)(2,1)S(1)}, bf16[128,128]{1,0:T(8,128)(2,1)S(1)}, u32[]{:S(2)}, u32[]{:S(2)}) collective-permute-start(bf16[128,128]{1,0:T(8,128)(2,1)S(1)} %get-tuple-element.57), channel_id=1, source_target_pairs={{0,32},{32,64},{64,96},{96,0},{128,160},{160,192},{192,224},{224,1... | collective-permute-start | bytes 98312 | tf_op jit(solution)/shard_map/ppermute | solution.py:408
  98.7 3.1 %collective-permute-start.13 = (bf16[128,128]{1,0:T(8,128)(2,1)S(1)}, bf16[128,128]{1,0:T(8,128)(2,1)S(1)}, u32[]{:S(2)}, u32[]{:S(2)}) collective-permute-start(bf16[128,128]{1,0:T(8,128)(2,1)S(1)} %get-tuple-element.57), channel_id=1, source_target_pairs={{0,96},{32,0},{64,32},{96,64},{128,224},{160,128},{192,160},{224,1... | collective-permute-start | bytes 98312 | tf_op jit(solution)/shard_map/ppermute | solution.py:408
  101.8 0.0 collective-permute-done.11
  101.9 1.5 collective-permute-done.13
  103.4 6.2 %collective-permute-start.14 = (bf16[32,3,128,128]{3,2,1,0:T(8,128)(2,1)}, bf16[32,3,128,128]{3,2,1,0:T(8,128)(2,1)S(1)}, u32[]{:S(2)}, u32[]{:S(2)}) collective-permute-start(bf16[32,3,128,128]{3,2,1,0:T(8,128)(2,1)} %all-to-all-done.1.own), channel_id=1, source_target_pairs={{0,1},{1,0},{2,3},{3,2},{4,5},{5,4},{6,7},{7,6},{8,9},{9,8},{10,11... | collective-permute-start | bytes 9437192 | tf_op jit(solution)/shard_map/ppermute | solution.py:356
  109.6 1.9 %slice.16 = bf16[8,2,128,128]{3,2,1,0:T(8,128)(2,1)} slice(bf16[32,3,128,128]{3,2,1,0:T(8,128)(2,1)} %all-to-all-done.1.own), slice={[24:32], [0:2], [0:128], [0:128]} | slice | bytes 1048576 | tf_op jit(solution)/shard_map/slice | solution.py:422
  111.5 3.6 %collective-permute-start.16 = (bf16[8,2,128,128]{3,2,1,0:T(8,128)(2,1)}, bf16[8,2,128,128]{3,2,1,0:T(8,128)(2,1)}, u32[]{:S(2)}, u32[]{:S(2)}) collective-permute-start(bf16[8,2,128,128]{3,2,1,0:T(8,128)(2,1)} %slice.16), channel_id=1, source_target_pairs={{0,32},{32,64},{64,96},{96,128},{128,160},{160,192},{192,224},{224... | collective-permute-start | bytes 1572872 | tf_op jit(solution)/shard_map/ppermute | solution.py:422
  115.1 0.6 slice.20
  116.4 2.2 %collective-permute-start.15 = (bf16[2,2,128,128]{3,2,1,0:T(8,128)(2,1)S(1)}, bf16[2,2,128,128]{3,2,1,0:T(8,128)(2,1)S(1)}, u32[]{:S(2)}, u32[]{:S(2)}) collective-permute-start(bf16[2,2,128,128]{3,2,1,0:T(8,128)(2,1)S(1)} %bitcast.38), channel_id=1, source_target_pairs={{0,1},{1,0},{2,3},{3,2},{4,5},{5,4},{6,7},{7,6},{8,9},{9,8},{10,11... | collective-permute-start | bytes 393224 | tf_op jit(solution)/shard_map/ppermute | solution.py:356
  118.6 1.0 collective-permute-done.15.global_other
  119.6 0.0 collective-permute-done.14.other
  119.6 14.4 %attend_rest.1.refs_2_ = bf16[24,128,128]{2,1,0:T(8,128)(2,1)S(1)} custom-call(s32[4]{0:T(128)S(1)} %pad_add_fusion.1.where, s32[4,16,14]{2,1,0:T(8,128)S(1)} %pad_add_fusion.rows, bf16[32,3,128,128]{3,2,1,0:T(8,128)(2,1)} %all-to-all-done.1.own, bf16[32,3,128,128]{3,2,1,0:T(8,128)(2,1)S(1)} %collective-permute-done.14.other, ...), custom_call_target="tpu_custom_call" | custom-call | flops 2818572288 | bytes 8388608 | tf_op jit(solution)/shard_map/attend_rest/pallas_call | solution.py:333
  134.1 2.2 %collective-permute-start.17 = (bf16[8,2,128,128]{3,2,1,0:T(8,128)(2,1)}, bf16[8,2,128,128]{3,2,1,0:T(8,128)(2,1)S(1)}, u32[]{:S(2)}, u32[]{:S(2)}) collective-permute-start(bf16[8,2,128,128]{3,2,1,0:T(8,128)(2,1)} %collective-permute-done.16.refs_0_), channel_id=1, source_target_pairs={{0,1},{1,0},{2,3},{3,2},{4,5},{5,4},{6,7},{7,6},{8,9},{9,8},{10,11... | collective-permute-start | bytes 1572872 | tf_op jit(solution)/shard_map/ppermute | solution.py:356
  136.3 1.8 %collective-permute-done.17.refs_1_ = bf16[8,2,128,128]{3,2,1,0:T(8,128)(2,1)S(1)} collective-permute-done((bf16[8,2,128,128]{3,2,1,0:T(8,128)(2,1)}, bf16[8,2,128,128]{3,2,1,0:T(8,128)(2,1)S(1)}, u32[]{:S(2)}, u32[]{:S(2)}) %collective-permute-start.17) | collective-permute-done | bytes 524320 | tf_op jit(solution)/shard_map/ppermute | solution.py:356
  138.1 7.8 %attend_first.1 = bf16[32,128,128]{2,1,0:T(8,128)(2,1)S(1)} custom-call(s32[4]{0:T(128)S(1)} %pad_add_fusion.1.where, s32[4,16,14]{2,1,0:T(8,128)S(1)} %pad_add_fusion.rows, bf16[32,3,128,128]{3,2,1,0:T(8,128)(2,1)} %all-to-all-done.1.own, bf16[32,3,128,128]{3,2,1,0:T(8,128)(2,1)S(1)} %collective-permute-done.14.other, ...), custom_call_target="tpu_custom_call" | custom-call | flops 939524096 | bytes 8388608 | tf_op jit(solution)/shard_map/attend_first/pallas_call | solution.py:333
  145.8 24.3 %all_to_all.15 = bf16[32,128,128]{2,1,0:T(8,128)(2,1)S(1)} all-to-all(bf16[32,128,128]{2,1,0:T(8,128)(2,1)S(1)} %attend_first.1), channel_id=1, replica_groups=mesh['z'=16,'y'=4,'x'=4,'core'=2] {'y','x','core'}, dimensions={0} | all-to-all | bytes 2097152 | tf_op jit(solution)/shard_map/all_to_all | solution.py:431
  170.2 0.7 copy.5
  170.9 1.2 copy.8
  (14 shorter events, 0.1 us)
Async XLA Ops:
  6.5 20.3 %copy-start = (s32[16,14]{1,0:T(8,128)S(1)}, s32[16,14]{1,0:T(8,128)}, u32[]{:S(2)}) copy-start(s32[16,14]{1,0:T(8,128)} %param.9) | copy-start | bytes 2692
  7.4 4.9 %collective-permute-start = (s32[4]{0:T(128)S(1)}, s32[4]{0:T(128)S(1)}, u32[]{:S(2)}, u32[]{:S(2)}) collective-permute-start(s32[4]{0:T(128)S(1)} %slice_bitcast_fusion), channel_id=1, source_target_pairs={{8,0},{16,8},{24,16},{32,24},{40,32},{48,40},{56,48},{64,56},{72,6... | collective-permute-start | bytes 56 | tf_op jit(solution)/shard_map/ppermute | solution.py:371
  12.3 0.6 copy-start.1
  15.9 28.3 %all-to-all-start = ((bf16[32,128,128]{2,1,0:T(8,128)(2,1)}), bf16[32,128,128]{2,1,0:T(8,128)(2,1)S(1)}, u32[]{:S(2)}, u32[]{:S(2)}) async-start(bf16[32,128,128]{2,1,0:T(8,128)(2,1)} %pack_early.1), calls=%async_computation | async-start | bytes 2097152 | tf_op jit(solution)/shard_map/all_to_all | solution.py:375
  26.9 15.0 %collective-permute-start.1 = (s32[16,14]{1,0:T(8,128)S(1)}, s32[16,14]{1,0:T(8,128)S(1)}, u32[]{:S(2)}, u32[]{:S(2)}) collective-permute-start(s32[16,14]{1,0:T(8,128)S(1)} %copy-done), channel_id=1, source_target_pairs={{0,8},{8,16},{16,24},{24,0},{1,9},{9,17},{17,25},{25,1},{2,10},{10... | collective-permute-start | bytes 2696 | tf_op jit(solution)/shard_map/ppermute | solution.py:382
  30.2 11.7 %collective-permute-start.3 = (s32[16,14]{1,0:T(8,128)S(1)}, s32[16,14]{1,0:T(8,128)S(1)}, u32[]{:S(2)}, u32[]{:S(2)}) collective-permute-start(s32[16,14]{1,0:T(8,128)S(1)} %copy-done), channel_id=1, source_target_pairs={{0,24},{8,0},{16,8},{24,16},{1,25},{9,1},{17,9},{25,17},{2,26},{10... | collective-permute-start | bytes 2696 | tf_op jit(solution)/shard_map/ppermute | solution.py:382
  33.4 8.4 %collective-permute-start.2 = (s32[16,14]{1,0:T(8,128)S(1)}, s32[16,14]{1,0:T(8,128)S(1)}, u32[]{:S(2)}, u32[]{:S(2)}) collective-permute-start(s32[16,14]{1,0:T(8,128)S(1)} %copy-done), channel_id=1, source_target_pairs={{0,16},{8,24},{16,0},{24,8},{1,17},{9,25},{17,1},{25,9},{2,18},{10... | collective-permute-start | bytes 2696 | tf_op jit(solution)/shard_map/ppermute | solution.py:382
  37.0 4.9 %collective-permute-start.4 = (s32[4]{0:T(128)S(1)}, s32[4]{0:T(128)S(1)}, u32[]{:S(2)}, u32[]{:S(2)}) collective-permute-start(s32[4]{0:T(128)S(1)} %slice_bitcast_fusion), channel_id=1, source_target_pairs={{32,0},{64,32},{96,64},{128,96},{160,128},{192,160},{224,192},{256... | collective-permute-start | bytes 56 | tf_op jit(solution)/shard_map/ppermute | solution.py:386
  44.1 59.3 %all-to-all-start.1 = ((bf16[32,3,128,128]{3,2,1,0:T(8,128)(2,1)}), bf16[32,3,128,128]{3,2,1,0:T(8,128)(2,1)}, u32[]{:S(2)}, u32[]{:S(2)}) async-start(bf16[32,3,128,128]{3,2,1,0:T(8,128)(2,1)} %pack.1), calls=%async_computation.1 | async-start | bytes 6291456 | tf_op jit(solution)/shard_map/all_to_all | solution.py:390
  50.8 12.8 %collective-permute-start.5 = (bf16[144,128]{1,0:T(8,128)(2,1)S(1)}, bf16[144,128]{1,0:T(8,128)(2,1)S(1)}, u32[]{:S(2)}, u32[]{:S(2)}) collective-permute-start(bf16[144,128]{1,0:T(8,128)(2,1)S(1)} %get-tuple-element.47), channel_id=1, source_target_pairs={{0,32},{32,64},{64,96},{96,0},{128,160},{160,192},{192,224},{224,1... | collective-permute-start | bytes 110600 | tf_op jit(solution)/shard_map/ppermute | solution.py:400
  54.5 9.5 %collective-permute-start.6 = (bf16[144,128]{1,0:T(8,128)(2,1)S(1)}, bf16[144,128]{1,0:T(8,128)(2,1)S(1)}, u32[]{:S(2)}, u32[]{:S(2)}) collective-permute-start(bf16[144,128]{1,0:T(8,128)(2,1)S(1)} %get-tuple-element.48), channel_id=1, source_target_pairs={{0,64},{32,96},{64,0},{96,32},{128,192},{160,224},{192,128},{224,1... | collective-permute-start | bytes 110600 | tf_op jit(solution)/shard_map/ppermute | solution.py:400
  61.7 5.1 %collective-permute-start.7 = (bf16[144,128]{1,0:T(8,128)(2,1)S(1)}, bf16[144,128]{1,0:T(8,128)(2,1)S(1)}, u32[]{:S(2)}, u32[]{:S(2)}) collective-permute-start(bf16[144,128]{1,0:T(8,128)(2,1)S(1)} %get-tuple-element.49), channel_id=1, source_target_pairs={{0,96},{32,0},{64,32},{96,64},{128,224},{160,128},{192,160},{224,1... | collective-permute-start | bytes 110600 | tf_op jit(solution)/shard_map/ppermute | solution.py:400
  66.8 22.0 %collective-permute-start.10 = (bf16[144,128]{1,0:T(8,128)(2,1)S(1)}, bf16[144,128]{1,0:T(8,128)(2,1)S(1)}, u32[]{:S(2)}, u32[]{:S(2)}) collective-permute-start(bf16[144,128]{1,0:T(8,128)(2,1)S(1)} %add_convert_fusion.1), channel_id=1, source_target_pairs={{0,384},{32,416},{64,448},{96,480},{128,0},{160,32},{192,64},{224,... | collective-permute-start | bytes 110600 | tf_op jit(solution)/shard_map/ppermute | solution.py:403
  77.8 13.6 %collective-permute-start.9 = (bf16[144,128]{1,0:T(8,128)(2,1)S(1)}, bf16[144,128]{1,0:T(8,128)(2,1)S(1)}, u32[]{:S(2)}, u32[]{:S(2)}) collective-permute-start(bf16[144,128]{1,0:T(8,128)(2,1)S(1)} %add_convert_fusion.1), channel_id=1, source_target_pairs={{0,256},{32,288},{64,320},{96,352},{128,384},{160,416},{192,448},{... | collective-permute-start | bytes 110600 | tf_op jit(solution)/shard_map/ppermute | solution.py:403
  82.6 10.1 %collective-permute-start.8 = (bf16[144,128]{1,0:T(8,128)(2,1)S(1)}, bf16[144,128]{1,0:T(8,128)(2,1)S(1)}, u32[]{:S(2)}, u32[]{:S(2)}) collective-permute-start(bf16[144,128]{1,0:T(8,128)(2,1)S(1)} %add_convert_fusion.1), channel_id=1, source_target_pairs={{0,128},{32,160},{64,192},{96,224},{128,256},{160,288},{192,320},{... | collective-permute-start | bytes 110600 | tf_op jit(solution)/shard_map/ppermute | solution.py:403
  92.8 9.0 %collective-permute-start.12 = (bf16[128,128]{1,0:T(8,128)(2,1)S(1)}, bf16[128,128]{1,0:T(8,128)(2,1)S(1)}, u32[]{:S(2)}, u32[]{:S(2)}) collective-permute-start(bf16[128,128]{1,0:T(8,128)(2,1)S(1)} %get-tuple-element.57), channel_id=1, source_target_pairs={{0,64},{32,96},{64,0},{96,32},{128,192},{160,224},{192,128},{224,1... | collective-permute-start | bytes 98312 | tf_op jit(solution)/shard_map/ppermute | solution.py:408
  94.7 7.1 %collective-permute-start.11 = (bf16[128,128]{1,0:T(8,128)(2,1)S(1)}, bf16[128,128]{1,0:T(8,128)(2,1)S(1)}, u32[]{:S(2)}, u32[]{:S(2)}) collective-permute-start(bf16[128,128]{1,0:T(8,128)(2,1)S(1)} %get-tuple-element.57), channel_id=1, source_target_pairs={{0,32},{32,64},{64,96},{96,0},{128,160},{160,192},{192,224},{224,1... | collective-permute-start | bytes 98312 | tf_op jit(solution)/shard_map/ppermute | solution.py:408
  98.7 4.7 %collective-permute-start.13 = (bf16[128,128]{1,0:T(8,128)(2,1)S(1)}, bf16[128,128]{1,0:T(8,128)(2,1)S(1)}, u32[]{:S(2)}, u32[]{:S(2)}) collective-permute-start(bf16[128,128]{1,0:T(8,128)(2,1)S(1)} %get-tuple-element.57), channel_id=1, source_target_pairs={{0,96},{32,0},{64,32},{96,64},{128,224},{160,128},{192,160},{224,1... | collective-permute-start | bytes 98312 | tf_op jit(solution)/shard_map/ppermute | solution.py:408
  103.4 16.2 %collective-permute-start.14 = (bf16[32,3,128,128]{3,2,1,0:T(8,128)(2,1)}, bf16[32,3,128,128]{3,2,1,0:T(8,128)(2,1)S(1)}, u32[]{:S(2)}, u32[]{:S(2)}) collective-permute-start(bf16[32,3,128,128]{3,2,1,0:T(8,128)(2,1)} %all-to-all-done.1.own), channel_id=1, source_target_pairs={{0,1},{1,0},{2,3},{3,2},{4,5},{5,4},{6,7},{7,6},{8,9},{9,8},{10,11... | collective-permute-start | bytes 9437192 | tf_op jit(solution)/shard_map/ppermute | solution.py:356
  111.5 22.5 %collective-permute-start.16 = (bf16[8,2,128,128]{3,2,1,0:T(8,128)(2,1)}, bf16[8,2,128,128]{3,2,1,0:T(8,128)(2,1)}, u32[]{:S(2)}, u32[]{:S(2)}) collective-permute-start(bf16[8,2,128,128]{3,2,1,0:T(8,128)(2,1)} %slice.16), channel_id=1, source_target_pairs={{0,32},{32,64},{64,96},{96,128},{128,160},{160,192},{192,224},{224... | collective-permute-start | bytes 1572872 | tf_op jit(solution)/shard_map/ppermute | solution.py:422
  116.4 3.2 %collective-permute-start.15 = (bf16[2,2,128,128]{3,2,1,0:T(8,128)(2,1)S(1)}, bf16[2,2,128,128]{3,2,1,0:T(8,128)(2,1)S(1)}, u32[]{:S(2)}, u32[]{:S(2)}) collective-permute-start(bf16[2,2,128,128]{3,2,1,0:T(8,128)(2,1)S(1)} %bitcast.38), channel_id=1, source_target_pairs={{0,1},{1,0},{2,3},{3,2},{4,5},{5,4},{6,7},{7,6},{8,9},{9,8},{10,11... | collective-permute-start | bytes 393224 | tf_op jit(solution)/shard_map/ppermute | solution.py:356
  134.1 4.0 %collective-permute-start.17 = (bf16[8,2,128,128]{3,2,1,0:T(8,128)(2,1)}, bf16[8,2,128,128]{3,2,1,0:T(8,128)(2,1)S(1)}, u32[]{:S(2)}, u32[]{:S(2)}) collective-permute-start(bf16[8,2,128,128]{3,2,1,0:T(8,128)(2,1)} %collective-permute-done.16.refs_0_), channel_id=1, source_target_pairs={{0,1},{1,0},{2,3},{3,2},{4,5},{5,4},{6,7},{7,6},{8,9},{9,8},{10,11... | collective-permute-start | bytes 1572872 | tf_op jit(solution)/shard_map/ppermute | solution.py:356

commit v9 on v5

--- a/solution.py
+++ b/solution.py
@@ -301,12 +301,9 @@
         copies = jnp.broadcast_to(value[None], (GLOBALS,) + value.shape)
         return lax.all_to_all(copies, axis, 0, 0, tiled=True)
 
-    def summed(values):
-        return jnp.sum(values.astype(jnp.float32), axis=0).astype(jnp.bfloat16)
-
     part = pick_globals(where, rows, above, own)
-    held = summed(lax.all_to_all(part, "near", 0, 0, tiled=True))
-    held = summed(spread(held, "far"))
+    held = jnp.sum(lax.all_to_all(part, "near", 0, 0, tiled=True).astype(jnp.float32), axis=0)
+    held = lax.psum(held, "far").astype(jnp.bfloat16)
     global_own = spread(held, "near")
     last, global_own = lax.optimization_barrier((own[-WIN // 2 :, :2], global_own))
     pair = (GLOBALS // 2, 2, BLOCK, HEAD_DIM)

time: 159 us -> 162 us (1.019)
  starting transfers between devices: 42.9 us -> 45.5 us
    all_to_all x2 -> x1, blocking collectives: 33.7 us -> 8.17 us  [shards(): lax.all_to_all(part, 'near', 0, 0, tiled=True).astype(jnp.float32)]
    psum x0 -> x1, blocking collectives: none -> 25.1 us  [shards(): held = lax.psum(held, 'far').astype(jnp.bfloat16)]
    ppermute x3, starting transfers between devices: 13.4 us -> 15.9 us  [swapped(): return lax.ppermute(value, 'core', [(0, 1), (1, 0)])]
  transfers between devices with their start and end apart: 10 -> 10, of which waited for: 5 -> 5; matrix products, arithmetic and copies ran while one was open for 1% -> 1% of each run, Pallas kernels for 10% -> 9%
where the time goes in v9:
time: 162 us; the launch traced here: 161 us
  blocking collectives  53.6 us (33%)
  starting transfers between devices  45.5 us (28%)
  waiting for transfers between devices  32.9 us (20%)
  Pallas kernels  25.1 us (15%)
  local copies, waits for them, and re-layouts  3.51 us (2%)
    psum x1, blocking collectives, shards(): held = lax.psum(held, 'far').astype(jnp.bfloat16)  25.1 us
    ppermute x3, waiting for transfers between devices, shards(): lax.ppermute(key_blocks, 'y', [(at, (at + step) % breadth) for at in rang...  22.9 us
    pallas_call x2, Pallas kernels, attend(): pl.pallas_call(functools.partial(attend_kernel, start, high, kept), out_s...  20.3 us
    all_to_all x1, blocking collectives, shards(): back = lax.all_to_all(context, PLANE_AXES, 0, 0, tiled=True)  20.3 us
    ppermute x3, starting transfers between devices, swapped(): return lax.ppermute(value, 'core', [(0, 1), (1, 0)])  15.9 us
    ppermute x3, starting transfers between devices, shards(): lax.ppermute(key_blocks, 'y', [(at, (at + step) % breadth) for at in rang...  11.4 us
    all_to_all x1, starting transfers between devices, shards(): lax.all_to_all(pack(queries, key_vectors, value_vectors), PLANE_AXES, 0,...  10.6 us
    all_to_all x1, blocking collectives, shards(): lax.all_to_all(part, 'near', 0, 0, tiled=True).astype(jnp.float32)  8.17 us
  transfers between devices with their start and end apart: 10, of which 5 were waited for; matrix products, arithmetic and copies ran while one was open for 1% of the time, Pallas kernels for 9%

profile of v9, /device:TPU:1, one launch (start us, length us, event | category | flops | bytes accessed | tf_op | source)
XLA Modules:
  0.0 160.9 jit_solution(4360064486327914727)
XLA Ops:
  0.0 3.5 %pack.1 = bf16[32,3,128,128]{3,2,1,0:T(8,128)(2,1)} custom-call(bf16[2,128,2048]{2,1,0:T(8,128)(2,1)} %bitcast.26, bf16[2,128,2048]{2,1,0:T(8,128)(2,1)} %bitcast.27, bf16[2,128,2048]{2,1,0:T(8,128)(2,1)} %bitcast.28), custom_call_target="tpu_custom_call" | custom-call | tf_op jit(solution)/shard_map/pack/pallas_call | solution.py:63
  3.5 0.0 copy-start
  3.5 10.6 %all-to-all-start = ((bf16[32,3,128,128]{3,2,1,0:T(8,128)(2,1)}), bf16[32,3,128,128]{3,2,1,0:T(8,128)(2,1)S(1)}, u32[]{:S(2)}, u32[]{:S(2)}) async-start(bf16[32,3,128,128]{3,2,1,0:T(8,128)(2,1)} %pack.1), calls=%async_computation | async-start | bytes 6291456 | tf_op jit(solution)/shard_map/all_to_all | solution.py:285
  14.1 0.0 copy-done
  14.1 4.9 %collective-permute-start.1 = (s32[16,14]{1,0:T(8,128)S(1)}, s32[16,14]{1,0:T(8,128)S(1)}, u32[]{:S(2)}, u32[]{:S(2)}) collective-permute-start(s32[16,14]{1,0:T(8,128)S(1)} %copy-done), channel_id=1, source_target_pairs={{0,16},{8,24},{16,0},{24,8},{1,17},{9,25},{17,1},{25,9},{2,18},{10... | collective-permute-start | bytes 2696 | tf_op jit(solution)/shard_map/ppermute | solution.py:292
  19.0 2.2 %collective-permute-start = (s32[16,14]{1,0:T(8,128)S(1)}, s32[16,14]{1,0:T(8,128)S(1)}, u32[]{:S(2)}, u32[]{:S(2)}) collective-permute-start(s32[16,14]{1,0:T(8,128)S(1)} %copy-done), channel_id=1, source_target_pairs={{0,8},{8,16},{16,24},{24,0},{1,9},{9,17},{17,25},{25,1},{2,10},{10... | collective-permute-start | bytes 2696 | tf_op jit(solution)/shard_map/ppermute | solution.py:292
  21.3 4.2 %collective-permute-start.2 = (s32[16,14]{1,0:T(8,128)S(1)}, s32[16,14]{1,0:T(8,128)S(1)}, u32[]{:S(2)}, u32[]{:S(2)}) collective-permute-start(s32[16,14]{1,0:T(8,128)S(1)} %copy-done), channel_id=1, source_target_pairs={{0,24},{8,0},{16,8},{24,16},{1,25},{9,1},{17,9},{25,17},{2,26},{10... | collective-permute-start | bytes 2696 | tf_op jit(solution)/shard_map/ppermute | solution.py:292
  25.5 0.1 slice_bitcast_fusion
  25.6 1.3 collective-permute-start.3
  26.9 22.9 %collective-permute-done.1 = s32[16,14]{1,0:T(8,128)S(1)} collective-permute-done((s32[16,14]{1,0:T(8,128)S(1)}, s32[16,14]{1,0:T(8,128)S(1)}, u32[]{:S(2)}, u32[]{:S(2)}) %collective-permute-start.1) | collective-permute-done | bytes 928 | tf_op jit(solution)/shard_map/ppermute | solution.py:292
  49.8 0.0 collective-permute-done
  49.8 0.0 collective-permute-done.2
  49.8 0.0 collective-permute-done.3.above
  49.9 3.5 %all-to-all-done.kinds.own = bf16[32,3,128,128]{3,2,1,0:T(8,128)(2,1)S(1)} async-done(((bf16[32,3,128,128]{3,2,1,0:T(8,128)(2,1)}), bf16[32,3,128,128]{3,2,1,0:T(8,128)(2,1)S(1)}, u32[]{:S(2)}, u32[]{:S(2)}) %all-to-all-start) | async-done | bytes 3145760 | tf_op jit(solution)/shard_map/all_to_all | solution.py:285
  53.4 4.8 %collective-permute-start.4 = (bf16[32,3,128,128]{3,2,1,0:T(8,128)(2,1)S(1)}, bf16[32,3,128,128]{3,2,1,0:T(8,128)(2,1)}, u32[]{:S(2)}, u32[]{:S(2)}) collective-permute-start(bf16[32,3,128,128]{3,2,1,0:T(8,128)(2,1)S(1)} %all-to-all-done.kinds.own), channel_id=1, source_target_pairs={{0,1},{1,0},{2,3},{3,2},{4,5},{5,4},{6,7},{7,6},{8,9},{9,8},{10,11... | collective-permute-start | bytes 9437192 | tf_op jit(solution)/shard_map/ppermute | solution.py:273
  58.1 0.1 pad_add_fusion.1.where
  58.2 1.4 pick_globals.1
  59.6 8.2 %all_to_all.20 = bf16[4,128,128]{2,1,0:T(8,128)(2,1)S(1)} all-to-all(bf16[4,128,128]{2,1,0:T(8,128)(2,1)S(1)} %pick_globals.1), channel_id=1, replica_groups=mesh['far'=4,'near'=4,'y'=4,'x'=4,'core'=2] {'near'}, dimensions={0} | all-to-all | bytes 262144 | tf_op jit(solution)/shard_map/all_to_all | solution.py:305
  67.8 25.1 %psum.7 = bf16[128,128]{1,0:T(8,128)(2,1)S(1)} all-reduce(f32[128,128]{1,0:T(8,128)S(1)} %convert_reduce_fusion), channel_id=1, replica_groups=mesh['far'=4,'near'=4,'y'=4,'x'=4,'core'=2] {'far'}, use_global_device_ids=true, to_apply=%region_1.0 | all-reduce | flops 16384 | bytes 98304 | tf_op jit(solution)/shard_map/psum | solution.py:306
  92.9 0.7 broadcast_in_dim.2
  93.6 3.4 %all-to-all-start.2 = ((bf16[4,128,128]{2,1,0:T(8,128)(2,1)}), bf16[4,128,128]{2,1,0:T(8,128)(2,1)S(1)}, u32[]{:S(2)}, u32[]{:S(2)}) async-start(bf16[4,128,128]{2,1,0:T(8,128)(2,1)} %broadcast_in_dim.2), calls=%async_computation.2 | async-start | bytes 262144 | tf_op jit(solution)/shard_map/all_to_all | solution.py:302
  97.0 0.8 slice.7
  97.9 3.9 %all-to-all-done.2 = bf16[4,128,128]{2,1,0:T(8,128)(2,1)S(1)} async-done(((bf16[4,128,128]{2,1,0:T(8,128)(2,1)}), bf16[4,128,128]{2,1,0:T(8,128)(2,1)S(1)}, u32[]{:S(2)}, u32[]{:S(2)}) %all-to-all-start.2) | async-done | bytes 131104 | tf_op jit(solution)/shard_map/all_to_all | solution.py:302
  101.8 2.9 %collective-permute-start.6 = (bf16[8,2,128,128]{3,2,1,0:T(8,128)(2,1)}, bf16[8,2,128,128]{3,2,1,0:T(8,128)(2,1)S(1)}, u32[]{:S(2)}, u32[]{:S(2)}) collective-permute-start(bf16[8,2,128,128]{3,2,1,0:T(8,128)(2,1)} %slice.7), channel_id=1, source_target_pairs={{0,32},{32,64},{64,96},{96,128},{128,160},{160,192},{192,224},{224... | collective-permute-start | bytes 1572872 | tf_op jit(solution)/shard_map/ppermute | solution.py:312
  104.7 8.9 %collective-permute-start.5 = (bf16[2,2,128,128]{3,2,1,0:T(8,128)(2,1)S(1)}, bf16[2,2,128,128]{3,2,1,0:T(8,128)(2,1)S(1)}, u32[]{:S(2)}, u32[]{:S(2)}) collective-permute-start(bf16[2,2,128,128]{3,2,1,0:T(8,128)(2,1)S(1)} %bitcast.21), channel_id=1, source_target_pairs={{0,1},{1,0},{2,3},{3,2},{4,5},{5,4},{6,7},{7,6},{8,9},{9,8},{10,11... | collective-permute-start | bytes 393224 | tf_op jit(solution)/shard_map/ppermute | solution.py:273
  113.6 1.0 collective-permute-done.5.global_other
  114.5 0.0 collective-permute-done.4.other
  114.5 13.9 %attend_rest.1.refs_2_ = bf16[24,128,128]{2,1,0:T(8,128)(2,1)S(1)} custom-call(s32[3]{0:T(128)S(1)} %pad_add_fusion.1.where, s32[4,16,14]{2,1,0:T(8,128)S(1)} %pad_add_fusion.rows, bf16[32,3,128,128]{3,2,1,0:T(8,128)(2,1)S(1)} %all-to-all-done.kinds.own, bf16[32,3,128,128]{3,2,1,0:T(8,128)(2,1)} %collective-permute-done.4.other, ...), custom_call_target="tpu_custom_call" | custom-call | flops 2818572288 | bytes 8388608 | tf_op jit(solution)/shard_map/attend_rest/pallas_call | solution.py:250
  128.4 0.0 collective-permute-done.6.refs_0_
  128.4 2.3 %collective-permute-start.7 = (bf16[8,2,128,128]{3,2,1,0:T(8,128)(2,1)S(1)}, bf16[8,2,128,128]{3,2,1,0:T(8,128)(2,1)S(1)}, u32[]{:S(2)}, u32[]{:S(2)}) collective-permute-start(bf16[8,2,128,128]{3,2,1,0:T(8,128)(2,1)S(1)} %collective-permute-done.6.refs_0_), channel_id=1, source_target_pairs={{0,1},{1,0},{2,3},{3,2},{4,5},{5,4},{6,7},{7,6},{8,9},{9,8},{10,11... | collective-permute-start | bytes 1572872 | tf_op jit(solution)/shard_map/ppermute | solution.py:273
  130.7 1.5 collective-permute-done.7.refs_1_
  132.2 6.4 %attend_first.1 = bf16[32,128,128]{2,1,0:T(8,128)(2,1)S(1)} custom-call(s32[3]{0:T(128)S(1)} %pad_add_fusion.1.where, s32[4,16,14]{2,1,0:T(8,128)S(1)} %pad_add_fusion.rows, bf16[32,3,128,128]{3,2,1,0:T(8,128)(2,1)S(1)} %all-to-all-done.kinds.own, bf16[32,3,128,128]{3,2,1,0:T(8,128)(2,1)} %collective-permute-done.4.other, ...), custom_call_target="tpu_custom_call" | custom-call | flops 939524096 | bytes 8388608 | tf_op jit(solution)/shard_map/attend_first/pallas_call | solution.py:250
  138.7 20.3 %all_to_all.21 = bf16[32,128,128]{2,1,0:T(8,128)(2,1)S(1)} all-to-all(bf16[32,128,128]{2,1,0:T(8,128)(2,1)S(1)} %attend_first.1), channel_id=1, replica_groups=mesh['far'=4,'near'=4,'y'=4,'x'=4,'core'=2] {'y','x','core'}, dimensions={0} | all-to-all | bytes 2097152 | tf_op jit(solution)/shard_map/all_to_all | solution.py:321
  159.0 0.7 copy.5
  159.6 1.2 copy.8
  (2 shorter events, 0.0 us)
Async XLA Ops:
  3.5 10.6 %copy-start = (s32[16,14]{1,0:T(8,128)S(1)}, s32[16,14]{1,0:T(8,128)}, u32[]{:S(2)}) copy-start(s32[16,14]{1,0:T(8,128)} %param.7) | copy-start | bytes 2692
  3.5 49.9 %all-to-all-start = ((bf16[32,3,128,128]{3,2,1,0:T(8,128)(2,1)}), bf16[32,3,128,128]{3,2,1,0:T(8,128)(2,1)S(1)}, u32[]{:S(2)}, u32[]{:S(2)}) async-start(bf16[32,3,128,128]{3,2,1,0:T(8,128)(2,1)} %pack.1), calls=%async_computation | async-start | bytes 6291456 | tf_op jit(solution)/shard_map/all_to_all | solution.py:285
  14.1 35.7 %collective-permute-start.1 = (s32[16,14]{1,0:T(8,128)S(1)}, s32[16,14]{1,0:T(8,128)S(1)}, u32[]{:S(2)}, u32[]{:S(2)}) collective-permute-start(s32[16,14]{1,0:T(8,128)S(1)} %copy-done), channel_id=1, source_target_pairs={{0,16},{8,24},{16,0},{24,8},{1,17},{9,25},{17,1},{25,9},{2,18},{10... | collective-permute-start | bytes 2696 | tf_op jit(solution)/shard_map/ppermute | solution.py:292
  19.0 30.8 %collective-permute-start = (s32[16,14]{1,0:T(8,128)S(1)}, s32[16,14]{1,0:T(8,128)S(1)}, u32[]{:S(2)}, u32[]{:S(2)}) collective-permute-start(s32[16,14]{1,0:T(8,128)S(1)} %copy-done), channel_id=1, source_target_pairs={{0,8},{8,16},{16,24},{24,0},{1,9},{9,17},{17,25},{25,1},{2,10},{10... | collective-permute-start | bytes 2696 | tf_op jit(solution)/shard_map/ppermute | solution.py:292
  21.3 28.6 %collective-permute-start.2 = (s32[16,14]{1,0:T(8,128)S(1)}, s32[16,14]{1,0:T(8,128)S(1)}, u32[]{:S(2)}, u32[]{:S(2)}) collective-permute-start(s32[16,14]{1,0:T(8,128)S(1)} %copy-done), channel_id=1, source_target_pairs={{0,24},{8,0},{16,8},{24,16},{1,25},{9,1},{17,9},{25,17},{2,26},{10... | collective-permute-start | bytes 2696 | tf_op jit(solution)/shard_map/ppermute | solution.py:292
  25.6 24.2 %collective-permute-start.3 = (s32[4]{0:T(128)S(1)}, s32[4]{0:T(128)S(1)}, u32[]{:S(2)}, u32[]{:S(2)}) collective-permute-start(s32[4]{0:T(128)S(1)} %slice_bitcast_fusion), channel_id=1, source_target_pairs={{32,0},{64,32},{96,64},{128,96},{160,128},{192,160},{224,192},{256... | collective-permute-start | bytes 56 | tf_op jit(solution)/shard_map/ppermute | solution.py:296
  53.4 61.2 %collective-permute-start.4 = (bf16[32,3,128,128]{3,2,1,0:T(8,128)(2,1)S(1)}, bf16[32,3,128,128]{3,2,1,0:T(8,128)(2,1)}, u32[]{:S(2)}, u32[]{:S(2)}) collective-permute-start(bf16[32,3,128,128]{3,2,1,0:T(8,128)(2,1)S(1)} %all-to-all-done.kinds.own), channel_id=1, source_target_pairs={{0,1},{1,0},{2,3},{3,2},{4,5},{5,4},{6,7},{7,6},{8,9},{9,8},{10,11... | collective-permute-start | bytes 9437192 | tf_op jit(solution)/shard_map/ppermute | solution.py:273
  93.6 8.2 %all-to-all-start.2 = ((bf16[4,128,128]{2,1,0:T(8,128)(2,1)}), bf16[4,128,128]{2,1,0:T(8,128)(2,1)S(1)}, u32[]{:S(2)}, u32[]{:S(2)}) async-start(bf16[4,128,128]{2,1,0:T(8,128)(2,1)} %broadcast_in_dim.2), calls=%async_computation.2 | async-start | bytes 262144 | tf_op jit(solution)/shard_map/all_to_all | solution.py:302
  101.8 26.6 %collective-permute-start.6 = (bf16[8,2,128,128]{3,2,1,0:T(8,128)(2,1)}, bf16[8,2,128,128]{3,2,1,0:T(8,128)(2,1)S(1)}, u32[]{:S(2)}, u32[]{:S(2)}) collective-permute-start(bf16[8,2,128,128]{3,2,1,0:T(8,128)(2,1)} %slice.7), channel_id=1, source_target_pairs={{0,32},{32,64},{64,96},{96,128},{128,160},{160,192},{192,224},{224... | collective-permute-start | bytes 1572872 | tf_op jit(solution)/shard_map/ppermute | solution.py:312
  104.7 9.8 %collective-permute-start.5 = (bf16[2,2,128,128]{3,2,1,0:T(8,128)(2,1)S(1)}, bf16[2,2,128,128]{3,2,1,0:T(8,128)(2,1)S(1)}, u32[]{:S(2)}, u32[]{:S(2)}) collective-permute-start(bf16[2,2,128,128]{3,2,1,0:T(8,128)(2,1)S(1)} %bitcast.21), channel_id=1, source_target_pairs={{0,1},{1,0},{2,3},{3,2},{4,5},{5,4},{6,7},{7,6},{8,9},{9,8},{10,11... | collective-permute-start | bytes 393224 | tf_op jit(solution)/shard_map/ppermute | solution.py:273
  128.4 3.8 %collective-permute-start.7 = (bf16[8,2,128,128]{3,2,1,0:T(8,128)(2,1)S(1)}, bf16[8,2,128,128]{3,2,1,0:T(8,128)(2,1)S(1)}, u32[]{:S(2)}, u32[]{:S(2)}) collective-permute-start(bf16[8,2,128,128]{3,2,1,0:T(8,128)(2,1)S(1)} %collective-permute-done.6.refs_0_), channel_id=1, source_target_pairs={{0,1},{1,0},{2,3},{3,2},{4,5},{5,4},{6,7},{7,6},{8,9},{9,8},{10,11... | collective-permute-start | bytes 1572872 | tf_op jit(solution)/shard_map/ppermute | solution.py:273
